TPU v7x, 32 devices: a whole 2x2x4 slice. The times are simulated.
32 devices in a mesh: gx: 4 (over x, core), gy: 2 (over y), gz: 4 (over z).
Axes of the slice: x: 2, y: 2, z: 4, core: 2. Of those that a mesh axis runs over, the one named last changes fastest.
Arguments:
- hidden_rows: bfloat16 [4096, 5120], P(('gx', 'gy', 'gz')), may hold values from -12 to 12
- query_grad: bfloat16 [4096, 5120], P(('gx', 'gy', 'gz')), may hold values from -384 to 384
- value_grad: bfloat16 [4096, 5120], P(('gx', 'gy', 'gz')), may hold values from -384 to 384
- query_down: bfloat16 [16, 5120], replicated, may hold values from -0.078125 to 0.078125
- query_up: bfloat16 [16, 5120], replicated, may hold values from -0.078125 to 0.078125
- value_down: bfloat16 [16, 5120], replicated, may hold values from -0.078125 to 0.078125
- value_up: bfloat16 [16, 5120], replicated, may hold values from -0.078125 to 0.078125
- lengths: int32 [64], P(('gx', 'gy', 'gz')), may hold values from 8 to 64, as said below
Outputs:
- grad_query_down: float32 [16, 5120], replicated
- grad_query_up: float32 [16, 5120], replicated
- grad_value_down: float32 [16, 5120], replicated
- grad_value_up: float32 [16, 5120], replicated
Inputs may be any that keep to these rules, and one draw needn't show every extreme that they name: `lengths`: the last sequence has 64 valid tokens and the first one 64 // 8.
All inputs are finite; a program needn't handle non-finite values.
Results may differ from a plain program's by a relative error of at most 0.0031.
Values sent between devices are 32-bit elements; how exact they have to be, the bound alone decides.
No kernel may reach another device: no remote copies, remote signals or barrier semaphores. Data moves between devices by JAX's collectives and lax.ppermute only.
A program may use at most 64 MiB of HBM per device.

v0:
```python
import jax
import jax.numpy as jnp
from jax import lax
from jax.sharding import PartitionSpec as P


def adapter_sums(rows, grad_out, down, up, valid):
    inner = lax.dot_general(
        rows, down, (((1,), (1,)), ((), ())), preferred_element_type=jnp.float32
    )
    inner = jnp.where(valid[:, None], inner, 0.0).astype(jnp.bfloat16)
    back = lax.dot_general(
        grad_out, up, (((1,), (1,)), ((), ())), preferred_element_type=jnp.float32
    )
    back = jnp.where(valid[:, None], back, 0.0).astype(jnp.bfloat16)
    up_sum = lax.dot_general(
        inner, grad_out, (((0,), (0,)), ((), ())), preferred_element_type=jnp.float32
    )
    down_sum = lax.dot_general(
        back, rows, (((0,), (0,)), ((), ())), preferred_element_type=jnp.float32
    )
    return jnp.stack([down_sum, up_sum]).reshape(-1)


def reduce_bucket(flat):
    summed = lax.psum(flat, ("gx", "gy", "gz"))
    return summed


def body(hidden_rows, query_grad, value_grad, query_down, query_up, value_down, value_up, lengths):
    seq_len = hidden_rows.shape[0] // lengths.shape[0]
    slots = jnp.arange(seq_len, dtype=jnp.int32)
    valid = (slots[None, :] < lengths[:, None]).reshape(-1)
    local_count = jnp.sum(lengths.astype(jnp.float32))
    rank_dim, width = query_down.shape
    query_flat = adapter_sums(hidden_rows, query_grad, query_down, query_up, valid)
    total = lax.psum(local_count, ("gx", "gy", "gz"))
    query_summed = reduce_bucket(query_flat)
    value_flat = adapter_sums(hidden_rows, value_grad, value_down, value_up, valid)
    value_summed = reduce_bucket(value_flat)
    query_pair = query_summed.reshape(2, rank_dim, width) / total
    value_pair = value_summed.reshape(2, rank_dim, width) / total
    return (query_pair[0], query_pair[1], value_pair[0], value_pair[1])


def solution(mesh):
    placed = (
        P(("gx", "gy", "gz"), None),
        P(("gx", "gy", "gz"), None),
        P(("gx", "gy", "gz"), None),
        P(),
        P(),
        P(),
        P(),
        P(("gx", "gy", "gz")),
    )
    return jax.shard_map(
        body, mesh=mesh, in_specs=placed, out_specs=(P(), P(), P(), P()), check_vma=False
    )
```

profile of v0, /device:TPU:0, one launch (start us, length us, event | category | flops | bytes accessed | tf_op | source)
XLA Modules:
  0.0 165.6 jit_solution(17214740851250227584)
XLA Ops:
  7.2 0.0 copy-start
  7.2 0.0 all-reduce.3.cloned.1.call-start
  7.2 0.8 iota_compare_fusion
  8.0 0.1 lt.23
  8.1 0.4 copy-done
  8.5 0.0 copy-start.1
  8.5 0.0 copy-start.3
  8.5 2.6 %convolution_bitcast_fusion = f32[1,16,5120]{2,1,0:T(8,128)S(1)} fusion(bf16[128,5120]{1,0:T(8,128)(2,1)} %param.10, bf16[128,5120]{1,0:T(8,128)(2,1)S(1)} %copy-done, bf16[16,5120]{1,0:T(8,128)(2,1)} %param.13, pred[128]{0:T(512)(128)(4,1)S(1)} %lt.23), kind=kOutput, calls=%fused_computation | convolution fusion | flops 41947136 | bytes 3113088 | tf_op jit(solution)/shard_map/dot_general | solution.py:16
  11.1 0.0 copy-done.1
  11.1 0.0 copy-done.3
  11.1 1.1 convolution_bitcast_fusion.1
  12.2 0.0 copy-start.2
  12.2 0.0 copy-start.4
  12.2 0.1 pad_maximum_fusion.1
  12.3 1.0 copy.13
  13.2 0.6 copy-done.2
  13.8 0.0 copy-done.4
  13.8 1.1 convolution_bitcast_fusion.2
  14.9 2.0 %convolution_bitcast_fusion.3 = f32[1,16,5120]{2,1,0:T(8,128)S(1)} fusion(bf16[128,5120]{1,0:T(8,128)(2,1)S(1)} %copy-done, bf16[128,5120]{1,0:T(8,128)(2,1)S(1)} %copy-done.2, bf16[16,5120]{1,0:T(8,128)(2,1)} %param.12, pred[128]{0:T(512)(128)(4,1)S(1)} %lt.23), kind=kOutput, calls=%fused_computation.3 | convolution fusion | flops 41947136 | bytes 3113088 | tf_op jit(solution)/shard_map/dot_general | solution.py:19
  16.9 0.1 pad_maximum_fusion
  17.0 0.0 copy-start.5
  17.0 1.0 copy.12
  18.0 0.0 all-reduce.3.cloned.1.call-update
  18.0 0.0 copy-done.5
  18.0 0.6 convert_reduce_fusion
  18.6 42.3 %psum.22 = f32[]{:T(128)} all-reduce(f32[]{:T(128)} %convert_reduce_fusion), channel_id=1, replica_groups=mesh['gx'=4,'gy'=2,'gz'=4] {'gx','gy','gz'}, use_global_device_ids=true, to_apply=%region_2.3 | all-reduce | flops 1 | bytes 8 | tf_op jit(solution)/shard_map/psum | solution.py:37
  60.9 92.6 %all-reduce.3.cloned.1.call-done = (f32[163840]{0:T(1024)}, f32[163840]{0:T(1024)}) async-done(((f32[163840]{0:T(1024)}, f32[163840]{0:T(1024)}), (f32[163840]{0:T(1024)}, f32[163840]{0:T(1024)})) %all-reduce.3.cloned.1.call-update) | async-done | bytes 1310736 | tf_op jit(solution)/shard_map/psum | solution.py:26
  153.5 2.0 %broadcast_divide_fusion = (f32[163840]{0:T(1024)S(1)}, f32[163840]{0:T(1024)S(1)}) fusion(f32[163840]{0:T(1024)} %get-tuple-element.5, f32[]{:T(128)} %psum.22, f32[163840]{0:T(1024)} %get-tuple-element.4), kind=kLoop, calls=%fused_computation.14 | loop fusion | flops 327680 | bytes 2621444 | tf_op jit(solution)/shard_map/div | solution.py:42
  155.5 0.8 squeeze.12
  156.3 0.8 squeeze.13
  157.2 0.8 squeeze.14
  157.9 0.8 squeeze.15
  (2 shorter events, 0.1 us)
Async XLA Ops:
  7.2 1.3 copy-start
  7.2 146.3 %all-reduce.3.cloned.1.call-start = ((), (), s32[]{:S(2)}) async-start(), calls=%async_computation | async-start | bytes 2621440 | tf_op jit(solution)/shard_map/psum | solution.py:26
  8.5 2.6 %copy-start.1 = (bf16[128,5120]{1,0:T(8,128)(2,1)S(1)}, bf16[128,5120]{1,0:T(8,128)(2,1)}, u32[]{:S(2)}) copy-start(bf16[128,5120]{1,0:T(8,128)(2,1)} %param.10) | copy-start | bytes 3932164
  8.5 2.6 %copy-start.3 = (bf16[16,5120]{1,0:T(8,128)(2,1)S(1)}, bf16[16,5120]{1,0:T(8,128)(2,1)}, u32[]{:S(2)}) copy-start(bf16[16,5120]{1,0:T(8,128)(2,1)} %param.14) | copy-start | bytes 491524
  12.2 1.6 copy-start.2
  12.2 1.6 copy-start.4
  17.0 1.0 copy-start.5
Sparse Core Ops, SparseCore 0:
  18.1 135.3 all-reduce.2
where the time goes:
time: 166 us
  waiting for transfers between devices  92.6 us (56%)
  blocking collectives  42.3 us (25%)
  between operations  14.1 us (8%)
  matrix products  6.82 us (4%)
  local copies, waits for them, and re-layouts  6.18 us (4%)
  other arithmetic  3.54 us (2%)
    psum x1, waiting for transfers between devices, reduce_bucket(): summed = lax.psum(flat, ('gx', 'gy', 'gz'))  92.6 us
    psum x1, blocking collectives, body(): total = lax.psum(local_count, ('gx', 'gy', 'gz'))  42.3 us
    dot_general x2, matrix products, adapter_sums(): lax.dot_general(inner, grad_out, (((0,), (0,)), ((), ())), preferred_elem...  3.69 us
  transfers between devices with their start and end apart: 1, of which 1 were waited for; matrix products, arithmetic and copies ran while one was open for 0% of the time, Pallas kernels for 0%

commit v1 on v0

v1 whole, which is shorter than its diff:
```python
import jax
import jax.numpy as jnp
from jax import lax
from jax.sharding import PartitionSpec as P

AXES = ("gx", "gy", "gz")
LANES = 128
SUBLANES = 8


def adapter_sums(rows, grad_out, down, up, valid):
    inner = lax.dot_general(
        rows, down, (((1,), (1,)), ((), ())), preferred_element_type=jnp.float32
    )
    inner = jnp.where(valid[:, None], inner, 0.0).astype(jnp.bfloat16)
    back = lax.dot_general(
        grad_out, up, (((1,), (1,)), ((), ())), preferred_element_type=jnp.float32
    )
    back = jnp.where(valid[:, None], back, 0.0).astype(jnp.bfloat16)
    up_sum = lax.dot_general(
        inner, grad_out, (((0,), (0,)), ((), ())), preferred_element_type=jnp.float32
    )
    down_sum = lax.dot_general(
        back, rows, (((0,), (0,)), ((), ())), preferred_element_type=jnp.float32
    )
    return down_sum, up_sum


def axis_bits(axis, size, first=0):
    bits = size.bit_length() - 1
    assert size == 1 << bits
    return [(axis, 1 << k) for k in range(first, bits)]


class Swaps:
    def __init__(self, sizes):
        self.sizes = sizes
        near = axis_bits("gx", sizes["gx"], 1) + axis_bits("gy", sizes["gy"])
        far = axis_bits("gz", sizes["gz"])
        self.orders = (near + far, self.paired(near) + self.paired(far))
        self.at = {axis: lax.axis_index(axis) for axis in AXES}
        self.core = self.at["gx"] & 1

    @staticmethod
    def paired(bits):
        order = list(bits)
        for k in range(0, len(order) - 1, 2):
            order[k], order[k + 1] = order[k + 1], order[k]
        return order

    def count(self):
        return len(self.orders[0])

    def high(self, stage):
        flags = [(self.at[axis] & bit) != 0 for axis, bit in (order[stage] for order in self.orders)]
        return jnp.where(self.core == 0, flags[0], flags[1])

    def swap(self, stage, array):
        gx, gy, gz = (self.sizes[axis] for axis in AXES)
        pairs = []
        for i in range(gx):
            for j in range(gy):
                for k in range(gz):
                    place = {"gx": i, "gy": j, "gz": k}
                    axis, bit = self.orders[i & 1][stage]
                    place[axis] ^= bit
                    there = (place["gx"] * gy + place["gy"]) * gz + place["gz"]
                    pairs.append(((i * gy + j) * gz + k, there))
        return lax.ppermute(array, AXES, pairs)

    def swap_cores(self, array):
        return lax.ppermute(array, "gx", [(i, i ^ 1) for i in range(self.sizes["gx"])])


def body(sizes, hidden_rows, query_grad, value_grad, query_down, query_up, value_down, value_up, lengths):
    seq_len = hidden_rows.shape[0] // lengths.shape[0]
    slots = jnp.arange(seq_len, dtype=jnp.int32)
    valid = (slots[None, :] < lengths[:, None]).reshape(-1)
    local_count = jnp.sum(lengths.astype(jnp.float32))
    rank_dim, width = query_down.shape
    swaps = Swaps(sizes)
    tail = jnp.full((2 * rank_dim, LANES), local_count, jnp.float32)

    def sums(grad_out, down, up):
        pair = jnp.concatenate(adapter_sums(hidden_rows, grad_out, down, up, valid), axis=0)
        return jnp.concatenate([pair, tail], axis=1)

    query = sums(query_grad, query_down, query_up)
    value = sums(value_grad, value_down, value_up)
    core = swaps.core == 0
    held = jnp.where(core, query, value) + swaps.swap_cores(jnp.where(core, value, query))
    halved = 0
    for stage in range(swaps.count()):
        rows = held.shape[0] // 2
        if stage == halved and rows % SUBLANES == 0:
            high = swaps.high(stage)
            low_half, high_half = held[:rows], held[rows:]
            sent = jnp.where(high, low_half, high_half)
            held = jnp.where(high, high_half, low_half) + swaps.swap(stage, sent)
            halved += 1
        else:
            held = held + swaps.swap(stage, held)
    held = held[:, :width] / held[:, width:width + 1]
    for stage in reversed(range(halved)):
        high = swaps.high(stage)
        other = swaps.swap(stage, held)
        held = jnp.concatenate([jnp.where(high, other, held), jnp.where(high, held, other)], axis=0)
    other = swaps.swap_cores(held)
    query = jnp.where(core, held, other)
    value = jnp.where(core, other, held)
    return query[:rank_dim], query[rank_dim:], value[:rank_dim], value[rank_dim:]


def solution(mesh):
    sizes = dict(mesh.shape)
    split = P(AXES)
    placed = (split, split, split, P(), P(), P(), P(), split)

    def step(*args):
        return body(sizes, *args)

    return jax.shard_map(step, mesh=mesh, in_specs=placed, out_specs=(P(),) * 4, check_vma=False)
```

time: 166 us -> 64.1 us (0.39)
  waiting for transfers between devices: 92.6 us -> 29.3 us
  blocking collectives: 42.3 us -> 0 us
  starting transfers between devices: 0.04 us -> 17.3 us
  between operations: 14.1 us -> 0.73 us
  local copies, waits for them, and re-layouts: 6.18 us -> 1.31 us
  other arithmetic: 3.54 us -> 6.38 us
  matrix products: 6.82 us -> 8.8 us
    psum x1 -> x0, waiting for transfers between devices: 92.6 us -> none  [reduce_bucket(): summed = lax.psum(flat, ('gx', 'gy', 'gz'))]
    psum x1 -> x0, blocking collectives: 42.3 us -> none  [body(): total = lax.psum(local_count, ('gx', 'gy', 'gz'))]
    ppermute x0 -> x8, waiting for transfers between devices: none -> 29.3 us  [the longest x6 25.3 us: swap(): return lax.ppermute(array, AXES, pairs)]
    ppermute x0 -> x8, starting transfers between devices: none -> 17.3 us  [the longest x6 16.7 us: swap(): return lax.ppermute(array, AXES, pairs)]
    squeeze x4 -> x0, local copies, waits for them, and re-layouts: 3.12 us -> none  [body(): return (query_pair[0], query_pair[1], value_pair[0], value_pair[1])]
    unnamed x14, local copies, waits for them, and re-layouts: 2.89 us -> 0.03 us
    select_n x0 -> x6, other arithmetic: none -> 2.14 us  [the longest x1 1.85 us: body(): jnp.where(core, value, query)]
    add x0 -> x5, other arithmetic: none -> 2 us  [the longest x1 1.84 us: body(): jnp.where(core, query, value)]
  transfers between devices with their start and end apart: 1 -> 8, of which waited for: 1 -> 8; matrix products, arithmetic and copies ran while one was open for 0% -> 0% of each run, Pallas kernels for 0% -> 0%
where the time goes in v1:
time: 64.1 us; the launch traced here: 63.8 us
  waiting for transfers between devices  29.3 us (46%)
  starting transfers between devices  17.3 us (27%)
  matrix products  8.8 us (14%)
  other arithmetic  6.38 us (10%)
  local copies, waits for them, and re-layouts  1.31 us (2%)
  between operations  0.73 us (1%)
    ppermute x6, waiting for transfers between devices, swap(): return lax.ppermute(array, AXES, pairs)  25.3 us
    ppermute x6, starting transfers between devices, swap(): return lax.ppermute(array, AXES, pairs)  16.7 us
    dot_general x2, matrix products, adapter_sums(): lax.dot_general(inner, grad_out, (((0,), (0,)), ((), ())), preferred_elem...  4.45 us
    dot_general x2, matrix products, adapter_sums(): lax.dot_general(back, rows, (((0,), (0,)), ((), ())), preferred_element_t...  4.35 us
    ppermute x2, waiting for transfers between devices, swap_cores(): lax.ppermute(array, 'gx', [(i, i ^ 1) for i in range(self.sizes['gx'])])  3.96 us
    select_n x1, other arithmetic, body(): jnp.where(core, value, query)  1.85 us
    add x1, other arithmetic, body(): jnp.where(core, query, value)  1.84 us
    reduce_sum x1, other arithmetic, body(): local_count = jnp.sum(lengths.astype(jnp.float32))  1.36 us
  transfers between devices with their start and end apart: 8, of which 8 were waited for; matrix products, arithmetic and copies ran while one was open for 0% of the time, Pallas kernels for 0%

profile of v1, /device:TPU:0, one launch (start us, length us, event | category | flops | bytes accessed | tf_op | source)
XLA Modules:
  0.0 63.8 jit_solution(10891675054249145252)
XLA Ops:
  0.6 0.0 copy-start
  0.6 1.4 %convert_reduce_fusion = f32[]{:T(128)} fusion(s32[2]{0:T(128)} %param.15), kind=kLoop, calls=%fused_computation.40 | loop fusion | flops 3 | bytes 12 | tf_op jit(solution)/shard_map/reduce_sum | solution.py:79
  2.0 0.7 %iota_compare_fusion.1 = pred[2,64]{1,0:T(4,128)(4,1)S(1)} fusion(s32[2]{0:T(128)} %param.15), kind=kLoop, calls=%fused_computation.39 | loop fusion | flops 128 | bytes 136 | tf_op jit(solution)/shard_map/lt | solution.py:78
  2.7 0.1 lt.23
  2.8 0.0 copy-done
  2.8 0.0 copy-start.1
  2.8 0.0 copy-start.5
  2.8 2.5 %fusion.5 = f32[16,5120]{1,0:T(8,128)S(1)} fusion(bf16[128,5120]{1,0:T(8,128)(2,1)S(1)} %copy-done, bf16[128,5120]{1,0:T(8,128)(2,1)} %param.10, bf16[16,5120]{1,0:T(8,128)(2,1)} %param.14, pred[128]{0:T(512)(128)(4,1)S(1)} %lt.23), kind=kOutput, calls=%fused_computation.9 | convolution fusion | flops 41947136 | bytes 3113088 | tf_op jit(solution)/shard_map/dot_general | solution.py:23
  5.4 0.0 copy-done.1
  5.4 0.0 copy-done.5
  5.4 1.1 %fusion.4 = f32[16,5120]{1,0:T(8,128)S(1)} fusion(bf16[128,5120]{1,0:T(8,128)(2,1)S(1)} %copy-done.1, bf16[128,5120]{1,0:T(8,128)(2,1)S(1)} %copy-done, bf16[16,5120]{1,0:T(8,128)(2,1)S(1)} %copy-done.5, pred[128]{0:T(512)(128)(4,1)S(1)} %lt.23), kind=kOutput, calls=%fused_computation.8 | convolution fusion | flops 41947136 | bytes 3113088 | tf_op jit(solution)/shard_map/dot_general | solution.py:20
  6.5 0.0 copy-start.2
  6.5 0.0 copy-start.6
  6.5 3.3 %fusion.6 = f32[16,5120]{1,0:T(8,128)} fusion(bf16[128,5120]{1,0:T(8,128)(2,1)} %param.9, bf16[128,5120]{1,0:T(8,128)(2,1)S(1)} %copy-done, bf16[16,5120]{1,0:T(8,128)(2,1)} %param.11, pred[128]{0:T(512)(128)(4,1)S(1)} %lt.23), kind=kOutput, calls=%fused_computation.10 | convolution fusion | flops 41947136 | bytes 3113088 | tf_op jit(solution)/shard_map/dot_general | solution.py:20
  9.8 0.0 copy-done.2
  9.8 0.0 copy-done.6
  9.8 1.8 %fusion.7 = f32[16,5120]{1,0:T(8,128)} fusion(bf16[128,5120]{1,0:T(8,128)(2,1)S(1)} %copy-done, bf16[128,5120]{1,0:T(8,128)(2,1)S(1)} %copy-done.2, bf16[16,5120]{1,0:T(8,128)(2,1)S(1)} %copy-done.6, pred[128]{0:T(512)(128)(4,1)S(1)} %lt.23), kind=kOutput, calls=%fused_computation.11 | convolution fusion | flops 41947136 | bytes 3113088 | tf_op jit(solution)/shard_map/dot_general | solution.py:23
  11.7 0.0 copy-start.3
  11.7 0.0 copy-start.4
  11.7 1.9 %fusion.8 = f32[32,5248]{1,0:T(8,128)S(1)} fusion(f32[16,5120]{1,0:T(8,128)} %fusion.6, f32[16,5120]{1,0:T(8,128)} %fusion.7, f32[16,5120]{1,0:T(8,128)S(1)} %fusion.4, f32[16,5120]{1,0:T(8,128)S(1)} %fusion.5, f32[]{:T(128)} %convert_reduce_fusion, pred[]{:T(512)S(6)} %eq.2), kind=kLoop, calls=%fused_computation.17 | loop fusion | flops 1343488 | bytes 1982469 | tf_op jit(solution)/shard_map/jit(_where)/select_n | solution.py:91
  13.5 0.6 collective-permute-start
  14.1 1.9 %collective-permute-done = f32[32,5248]{1,0:T(8,128)} collective-permute-done((f32[32,5248]{1,0:T(8,128)S(1)}, f32[32,5248]{1,0:T(8,128)}, u32[]{:S(2)}, u32[]{:S(2)}) %collective-permute-start) | collective-permute-done | bytes 671776 | tf_op jit(solution)/shard_map/ppermute | solution.py:72
  16.0 0.0 copy-done.3
  16.0 0.0 copy-done.4
  16.0 1.8 %select_add_fusion = f32[32,5248]{1,0:T(8,128)S(1)} fusion(f32[32,5248]{1,0:T(8,128)} %collective-permute-done, f32[16,5120]{1,0:T(8,128)S(1)} %copy-done.3, f32[16,5120]{1,0:T(8,128)S(1)} %copy-done.4, f32[16,5120]{1,0:T(8,128)S(1)} %fusion.4, f32[16,5120]{1,0:T(8,128)S(1)} %fusion.5, f32[]{:T(128)} %convert_reduce_fusion, pred[]{:T(512)S(6)} %eq.2), kind=kLoop, calls=%fused_computation.15 | loop fusion | flops 1511424 | bytes 2654213 | tf_op jit(solution)/shard_map/add | solution.py:91
  17.8 2.9 %collective-permute-start.1 = (f32[16,5248]{1,0:T(8,128)S(1)}, f32[16,5248]{1,0:T(8,128)S(1)}, u32[]{:S(2)}, u32[]{:S(2)}) collective-permute-start(f32[16,5248]{1,0:T(8,128)S(1)} %slice_select_fusion), channel_id=1, source_target_pairs={{0,16},{1,17},{2,18},{3,19},{4,20},{5,21},{6,22},{7,23},{8,12},{9,... | collective-permute-start | bytes 1007624 | tf_op jit(solution)/shard_map/ppermute | solution.py:69
  20.8 5.1 %collective-permute-done.1 = f32[16,5248]{1,0:T(8,128)S(1)} collective-permute-done((f32[16,5248]{1,0:T(8,128)S(1)}, f32[16,5248]{1,0:T(8,128)S(1)}, u32[]{:S(2)}, u32[]{:S(2)}) %collective-permute-start.1) | collective-permute-done | bytes 335904 | tf_op jit(solution)/shard_map/ppermute | solution.py:69
  25.9 0.1 select_add_fusion.1
  26.0 2.1 %collective-permute-start.2 = (f32[8,5248]{1,0:T(8,128)S(1)}, f32[8,5248]{1,0:T(8,128)S(1)}, u32[]{:S(2)}, u32[]{:S(2)}) collective-permute-start(f32[8,5248]{1,0:T(8,128)S(1)} %slice_select_fusion.1), channel_id=1, source_target_pairs={{0,4},{1,5},{2,6},{3,7},{4,0},{5,1},{6,2},{7,3},{8,24},{9,25},{10,... | collective-permute-start | bytes 503816 | tf_op jit(solution)/shard_map/ppermute | solution.py:69
  28.1 3.3 %collective-permute-done.2 = f32[8,5248]{1,0:T(8,128)S(1)} collective-permute-done((f32[8,5248]{1,0:T(8,128)S(1)}, f32[8,5248]{1,0:T(8,128)S(1)}, u32[]{:S(2)}, u32[]{:S(2)}) %collective-permute-start.2) | collective-permute-done | bytes 167968 | tf_op jit(solution)/shard_map/ppermute | solution.py:69
  31.5 2.1 %collective-permute-start.3 = (f32[8,5248]{1,0:T(8,128)S(1)}, f32[8,5248]{1,0:T(8,128)S(1)}, u32[]{:S(2)}, u32[]{:S(2)}) collective-permute-start(f32[8,5248]{1,0:T(8,128)S(1)} %select_add_fusion.2), channel_id=1, source_target_pairs={{0,1},{1,0},{2,3},{3,2},{4,5},{5,4},{6,7},{7,6},{8,10},{9,11},{10,... | collective-permute-start | bytes 503816 | tf_op jit(solution)/shard_map/ppermute | solution.py:69
  33.6 3.4 %collective-permute-done.3 = f32[8,5248]{1,0:T(8,128)S(1)} collective-permute-done((f32[8,5248]{1,0:T(8,128)S(1)}, f32[8,5248]{1,0:T(8,128)S(1)}, u32[]{:S(2)}, u32[]{:S(2)}) %collective-permute-start.3) | collective-permute-done | bytes 167968 | tf_op jit(solution)/shard_map/ppermute | solution.py:69
  37.0 3.9 %collective-permute-start.4 = (f32[8,5248]{1,0:T(8,128)S(1)}, f32[8,5248]{1,0:T(8,128)S(1)}, u32[]{:S(2)}, u32[]{:S(2)}) collective-permute-start(f32[8,5248]{1,0:T(8,128)S(1)} %add.22), channel_id=1, source_target_pairs={{0,2},{1,3},{2,0},{3,1},{4,6},{5,7},{6,4},{7,5},{8,9},{9,8},{10,11... | collective-permute-start | bytes 503816 | tf_op jit(solution)/shard_map/ppermute | solution.py:69
  40.9 3.3 %collective-permute-done.4 = f32[8,5248]{1,0:T(8,128)S(1)} collective-permute-done((f32[8,5248]{1,0:T(8,128)S(1)}, f32[8,5248]{1,0:T(8,128)S(1)}, u32[]{:S(2)}, u32[]{:S(2)}) %collective-permute-start.4) | collective-permute-done | bytes 167968 | tf_op jit(solution)/shard_map/ppermute | solution.py:69
  44.2 0.1 slice_reduce_fusion
  44.4 0.1 slice_divide_fusion
  44.5 3.6 %collective-permute-start.5 = (f32[8,5120]{1,0:T(8,128)S(1)}, f32[8,5120]{1,0:T(8,128)S(1)}, u32[]{:S(2)}, u32[]{:S(2)}) collective-permute-start(f32[8,5120]{1,0:T(8,128)S(1)} %slice_divide_fusion), channel_id=1, source_target_pairs={{0,4},{1,5},{2,6},{3,7},{4,0},{5,1},{6,2},{7,3},{8,24},{9,25},{10,... | collective-permute-start | bytes 491528 | tf_op jit(solution)/shard_map/ppermute | solution.py:69
  48.1 5.0 %collective-permute-done.5 = f32[8,5120]{1,0:T(8,128)S(1)} collective-permute-done((f32[8,5120]{1,0:T(8,128)S(1)}, f32[8,5120]{1,0:T(8,128)S(1)}, u32[]{:S(2)}, u32[]{:S(2)}) %collective-permute-start.5) | collective-permute-done | bytes 163872 | tf_op jit(solution)/shard_map/ppermute | solution.py:69
  53.1 0.1 broadcast_select_fusion.5
  53.3 2.1 %collective-permute-start.6 = (f32[16,5120]{1,0:T(8,128)S(1)}, f32[16,5120]{1,0:T(8,128)S(1)}, u32[]{:S(2)}, u32[]{:S(2)}) collective-permute-start(f32[16,5120]{1,0:T(8,128)S(1)} %pad_maximum_fusion.1), channel_id=1, source_target_pairs={{0,16},{1,17},{2,18},{3,19},{4,20},{5,21},{6,22},{7,23},{8,12},{9,... | collective-permute-start | bytes 983048 | tf_op jit(solution)/shard_map/ppermute | solution.py:69
  55.3 5.1 %collective-permute-done.6 = f32[16,5120]{1,0:T(8,128)S(1)} collective-permute-done((f32[16,5120]{1,0:T(8,128)S(1)}, f32[16,5120]{1,0:T(8,128)S(1)}, u32[]{:S(2)}, u32[]{:S(2)}) %collective-permute-start.6) | collective-permute-done | bytes 327712 | tf_op jit(solution)/shard_map/ppermute | solution.py:69
  60.5 0.1 collective-permute-start.7
  60.6 2.1 %collective-permute-done.7 = f32[32,5120]{1,0:T(8,128)S(1)} collective-permute-done((f32[32,5120]{1,0:T(8,128)S(1)}, f32[32,5120]{1,0:T(8,128)S(1)}, u32[]{:S(2)}, u32[]{:S(2)}) %collective-permute-start.7) | collective-permute-done | bytes 655392 | tf_op jit(solution)/shard_map/ppermute | solution.py:72
  62.7 0.1 broadcast_select_fusion
  62.8 1.1 %fusion.21 = (f32[16,5120]{1,0:T(8,128)}, f32[16,5120]{1,0:T(8,128)}, f32[16,5120]{1,0:T(8,128)}, f32[16,5120]{1,0:T(8,128)}) fusion(f32[32,5120]{1,0:T(8,128)S(1)} %get-tuple-element.4, f32[32,5120]{1,0:T(8,128)S(1)} %get-tuple-element.5), kind=kLoop, calls=%fused_computation.45 | loop fusion | bytes 2621440 | tf_op jit(solution)/shard_map/slice | solution.py:111
  (8 shorter events, 0.3 us)
Async XLA Ops:
  0.6 2.2 %copy-start = (bf16[128,5120]{1,0:T(8,128)(2,1)S(1)}, bf16[128,5120]{1,0:T(8,128)(2,1)}, u32[]{:S(2)}) copy-start(bf16[128,5120]{1,0:T(8,128)(2,1)} %param.8) | copy-start | bytes 3932164
  2.8 2.5 %copy-start.1 = (bf16[128,5120]{1,0:T(8,128)(2,1)S(1)}, bf16[128,5120]{1,0:T(8,128)(2,1)}, u32[]{:S(2)}) copy-start(bf16[128,5120]{1,0:T(8,128)(2,1)} %param.10) | copy-start | bytes 3932164
  2.8 2.5 %copy-start.5 = (bf16[16,5120]{1,0:T(8,128)(2,1)S(1)}, bf16[16,5120]{1,0:T(8,128)(2,1)}, u32[]{:S(2)}) copy-start(bf16[16,5120]{1,0:T(8,128)(2,1)} %param.13) | copy-start | bytes 491524
  6.5 3.4 %copy-start.2 = (bf16[128,5120]{1,0:T(8,128)(2,1)S(1)}, bf16[128,5120]{1,0:T(8,128)(2,1)}, u32[]{:S(2)}) copy-start(bf16[128,5120]{1,0:T(8,128)(2,1)} %param.9) | copy-start | bytes 3932164
  6.5 3.4 %copy-start.6 = (bf16[16,5120]{1,0:T(8,128)(2,1)S(1)}, bf16[16,5120]{1,0:T(8,128)(2,1)}, u32[]{:S(2)}) copy-start(bf16[16,5120]{1,0:T(8,128)(2,1)} %param.12) | copy-start | bytes 491524
  11.7 4.3 %copy-start.3 = (f32[16,5120]{1,0:T(8,128)S(1)}, f32[16,5120]{1,0:T(8,128)}, u32[]{:S(2)}) copy-start(f32[16,5120]{1,0:T(8,128)} %fusion.6) | copy-start | bytes 983044
  11.7 4.3 %copy-start.4 = (f32[16,5120]{1,0:T(8,128)S(1)}, f32[16,5120]{1,0:T(8,128)}, u32[]{:S(2)}) copy-start(f32[16,5120]{1,0:T(8,128)} %fusion.7) | copy-start | bytes 983044
  13.5 2.4 %collective-permute-start = (f32[32,5248]{1,0:T(8,128)S(1)}, f32[32,5248]{1,0:T(8,128)}, u32[]{:S(2)}, u32[]{:S(2)}) collective-permute-start(f32[32,5248]{1,0:T(8,128)S(1)} %fusion.8), channel_id=1, source_target_pairs={{0,8},{8,0},{16,24},{24,16},{1,9},{9,1},{17,25},{25,17},{2,10},{10... | collective-permute-start | bytes 2015240 | tf_op jit(solution)/shard_map/ppermute | solution.py:72
  17.8 8.1 %collective-permute-start.1 = (f32[16,5248]{1,0:T(8,128)S(1)}, f32[16,5248]{1,0:T(8,128)S(1)}, u32[]{:S(2)}, u32[]{:S(2)}) collective-permute-start(f32[16,5248]{1,0:T(8,128)S(1)} %slice_select_fusion), channel_id=1, source_target_pairs={{0,16},{1,17},{2,18},{3,19},{4,20},{5,21},{6,22},{7,23},{8,12},{9,... | collective-permute-start | bytes 1007624 | tf_op jit(solution)/shard_map/ppermute | solution.py:69
  26.0 5.5 %collective-permute-start.2 = (f32[8,5248]{1,0:T(8,128)S(1)}, f32[8,5248]{1,0:T(8,128)S(1)}, u32[]{:S(2)}, u32[]{:S(2)}) collective-permute-start(f32[8,5248]{1,0:T(8,128)S(1)} %slice_select_fusion.1), channel_id=1, source_target_pairs={{0,4},{1,5},{2,6},{3,7},{4,0},{5,1},{6,2},{7,3},{8,24},{9,25},{10,... | collective-permute-start | bytes 503816 | tf_op jit(solution)/shard_map/ppermute | solution.py:69
  31.5 5.5 %collective-permute-start.3 = (f32[8,5248]{1,0:T(8,128)S(1)}, f32[8,5248]{1,0:T(8,128)S(1)}, u32[]{:S(2)}, u32[]{:S(2)}) collective-permute-start(f32[8,5248]{1,0:T(8,128)S(1)} %select_add_fusion.2), channel_id=1, source_target_pairs={{0,1},{1,0},{2,3},{3,2},{4,5},{5,4},{6,7},{7,6},{8,10},{9,11},{10,... | collective-permute-start | bytes 503816 | tf_op jit(solution)/shard_map/ppermute | solution.py:69
  37.0 7.2 %collective-permute-start.4 = (f32[8,5248]{1,0:T(8,128)S(1)}, f32[8,5248]{1,0:T(8,128)S(1)}, u32[]{:S(2)}, u32[]{:S(2)}) collective-permute-start(f32[8,5248]{1,0:T(8,128)S(1)} %add.22), channel_id=1, source_target_pairs={{0,2},{1,3},{2,0},{3,1},{4,6},{5,7},{6,4},{7,5},{8,9},{9,8},{10,11... | collective-permute-start | bytes 503816 | tf_op jit(solution)/shard_map/ppermute | solution.py:69
  44.5 8.7 %collective-permute-start.5 = (f32[8,5120]{1,0:T(8,128)S(1)}, f32[8,5120]{1,0:T(8,128)S(1)}, u32[]{:S(2)}, u32[]{:S(2)}) collective-permute-start(f32[8,5120]{1,0:T(8,128)S(1)} %slice_divide_fusion), channel_id=1, source_target_pairs={{0,4},{1,5},{2,6},{3,7},{4,0},{5,1},{6,2},{7,3},{8,24},{9,25},{10,... | collective-permute-start | bytes 491528 | tf_op jit(solution)/shard_map/ppermute | solution.py:69
  53.3 7.1 %collective-permute-start.6 = (f32[16,5120]{1,0:T(8,128)S(1)}, f32[16,5120]{1,0:T(8,128)S(1)}, u32[]{:S(2)}, u32[]{:S(2)}) collective-permute-start(f32[16,5120]{1,0:T(8,128)S(1)} %pad_maximum_fusion.1), channel_id=1, source_target_pairs={{0,16},{1,17},{2,18},{3,19},{4,20},{5,21},{6,22},{7,23},{8,12},{9,... | collective-permute-start | bytes 983048 | tf_op jit(solution)/shard_map/ppermute | solution.py:69
  60.5 2.2 %collective-permute-start.7 = (f32[32,5120]{1,0:T(8,128)S(1)}, f32[32,5120]{1,0:T(8,128)S(1)}, u32[]{:S(2)}, u32[]{:S(2)}) collective-permute-start(f32[32,5120]{1,0:T(8,128)S(1)} %pad_maximum_fusion), channel_id=1, source_target_pairs={{0,8},{8,0},{16,24},{24,16},{1,9},{9,1},{17,25},{25,17},{2,10},{10... | collective-permute-start | bytes 1966088 | tf_op jit(solution)/shard_map/ppermute | solution.py:72

commit v2 on v1

v2 whole, which is shorter than its diff:
```python
import functools

import jax
import jax.numpy as jnp
from jax import lax
from jax.experimental import pallas as pl
from jax.experimental.pallas import tpu as pltpu
from jax.sharding import PartitionSpec as P

AXES = ("gx", "gy", "gz")
LANES = 128
SUBLANES = 8
PARTS = 4
NT = (((1,), (1,)), ((), ()))
NN = (((1,), (0,)), ((), ()))
dot = functools.partial(lax.dot_general, preferred_element_type=jnp.float32)


def adapter_kernel(
    parts, flip, lengths_in, rows, query_grad, value_grad, query_down, value_down, query_up, value_up,
    down_sum, up_sum, held_rows, held_grad, held_down, held_up, lengths, sems,
):
    tokens, width = held_rows.shape
    step = width // parts
    cuts = [pl.ds(k * step, step) for k in range(parts)]
    query = ((lax.axis_index("gx") + flip) & 1) == 0

    def copies(down, up, grad):
        small = [
            pltpu.make_async_copy(down, held_down, sems.at[0, parts]),
            pltpu.make_async_copy(up, held_up, sems.at[1, parts]),
            pltpu.make_async_copy(lengths_in, lengths, sems.at[0, parts + 1]),
        ]
        large = [
            (
                pltpu.make_async_copy(rows.at[:, cut], held_rows.at[:, cut], sems.at[0, k]),
                pltpu.make_async_copy(grad.at[:, cut], held_grad.at[:, cut], sems.at[1, k]),
            )
            for k, cut in enumerate(cuts)
        ]
        return small, large

    def start(*which):
        small, large = copies(*which)
        for copy in small:
            copy.start()
        for pair in large:
            for copy in pair:
                copy.start()

    @pl.when(query)
    def _():
        start(query_down, query_up, query_grad)

    @pl.when(jnp.logical_not(query))
    def _():
        start(value_down, value_up, value_grad)

    small, large = copies(query_down, query_up, query_grad)
    for copy in small:
        copy.wait()
    inner = back = 0.0
    for cut, pair in zip(cuts, large):
        for copy in pair:
            copy.wait()
        inner = inner + dot(held_down[:, cut], held_rows[:, cut], NT)
        back = back + dot(held_up[:, cut], held_grad[:, cut], NT)
    seqs = lengths.shape[0]
    seq_len = tokens // seqs
    token = lax.broadcasted_iota(jnp.int32, inner.shape, 1)
    valid = token < 0
    count = 0
    for s in range(seqs):
        first = s * seq_len
        valid = valid | ((token >= first) & (token < first + lengths[s]))
        count = count + lengths[s]
    inner = jnp.where(valid, inner, 0.0).astype(jnp.bfloat16)
    back = jnp.where(valid, back, 0.0).astype(jnp.bfloat16)
    for cut in cuts:
        down_sum[:, cut] = dot(back, held_rows[:, cut], NN)
        up_sum[:, cut] = dot(inner, held_grad[:, cut], NN)
    down_sum[:, width:] = jnp.full((down_sum.shape[0], LANES), count.astype(jnp.float32), jnp.float32)


def adapter_sums(flip, lengths, rows, *rest):
    tokens, width = rows.shape
    rank = rest[-1].shape[0]
    wide = pltpu.VMEM((tokens, width), rows.dtype)
    thin = pltpu.VMEM((rank, width), rows.dtype)
    args = [pltpu.with_memory_space_constraint(x, pltpu.HBM) for x in (lengths, rows, *rest)]
    return pl.pallas_call(
        functools.partial(adapter_kernel, PARTS, flip),
        out_shape=(pltpu.VMEM((rank, width + LANES), jnp.float32), pltpu.VMEM((rank, width), jnp.float32)),
        in_specs=[pl.BlockSpec(memory_space=pltpu.HBM)] * len(args),
        out_specs=(pl.BlockSpec(memory_space=pltpu.VMEM),) * 2,
        scratch_shapes=[
            wide, wide, thin, thin, pltpu.SMEM(lengths.shape, lengths.dtype),
            pltpu.SemaphoreType.DMA((2, PARTS + 2)),
        ],
        compiler_params=pltpu.CompilerParams(vmem_limit_bytes=16 << 20),
        cost_estimate=pl.CostEstimate(
            flops=8 * rank * tokens * width, bytes_accessed=4 * tokens * width, transcendentals=0
        ),
        name="adapter",
    )(*args)


def axis_bits(axis, size, first=0):
    bits = size.bit_length() - 1
    assert size == 1 << bits
    return [(axis, 1 << k) for k in range(first, bits)]


class Swaps:
    def __init__(self, sizes):
        self.sizes = sizes
        near = axis_bits("gx", sizes["gx"], 1) + axis_bits("gy", sizes["gy"])
        far = axis_bits("gz", sizes["gz"])
        self.orders = (near + far, self.paired(near) + self.paired(far))
        self.at = {axis: lax.axis_index(axis) for axis in AXES}
        self.core = self.at["gx"] & 1

    @staticmethod
    def paired(bits):
        order = list(bits)
        for k in range(0, len(order) - 1, 2):
            order[k], order[k + 1] = order[k + 1], order[k]
        return order

    def count(self):
        return len(self.orders[0])

    def high(self, stage):
        flags = [(self.at[axis] & bit) != 0 for axis, bit in (order[stage] for order in self.orders)]
        return jnp.where(self.core == 0, flags[0], flags[1])

    def swap(self, stage, array):
        gx, gy, gz = (self.sizes[axis] for axis in AXES)
        pairs = []
        for i in range(gx):
            for j in range(gy):
                for k in range(gz):
                    place = {"gx": i, "gy": j, "gz": k}
                    axis, bit = self.orders[i & 1][stage]
                    place[axis] ^= bit
                    there = (place["gx"] * gy + place["gy"]) * gz + place["gz"]
                    pairs.append(((i * gy + j) * gz + k, there))
        return lax.ppermute(array, AXES, pairs)

    def swap_cores(self, array):
        return lax.ppermute(array, "gx", [(i, i ^ 1) for i in range(self.sizes["gx"])])


def halves(array, width, axis):
    if axis == 0:
        rows = array.shape[0] // 2
        return array[:rows], array[rows:]
    tail = array[:, width:]
    half = width // 2
    low, high = array[:, :half], array[:, half:width]
    if not tail.shape[1]:
        return low, high
    return jnp.concatenate([low, tail], axis=1), jnp.concatenate([high, tail], axis=1)


def body(sizes, hidden_rows, query_grad, value_grad, query_down, query_up, value_down, value_up, lengths):
    args = (lengths, hidden_rows, query_grad, value_grad, query_down, value_down, query_up, value_up)
    swaps = Swaps(sizes)
    widths = [hidden_rows.shape[1]] * 2
    sent = adapter_sums(1, *args)
    got = [swaps.swap_cores(x) for x in sent]
    kept = adapter_sums(0, *args)
    held = [x + y for x, y in zip(kept, got)]
    cut = []
    for stage in range(swaps.count()):
        axis = None
        if stage == len(cut):
            if held[0].shape[0] % (2 * SUBLANES) == 0:
                axis = 0
            elif widths[0] % (2 * LANES) == 0 and len(cut) < 2:
                axis = 1
        if axis is None:
            held = [x + swaps.swap(stage, x) for x in held]
            continue
        high = swaps.high(stage)
        for c, x in enumerate(held):
            low_half, high_half = halves(x, widths[c], axis)
            held[c] = jnp.where(high, high_half, low_half) + swaps.swap(stage, jnp.where(high, low_half, high_half))
            if axis == 1:
                widths[c] //= 2
        cut.append(axis)
    total = held[0][0, widths[0]]
    held = [x[:, :width] for x, width in zip(held, widths)]
    for stage, axis in reversed(list(enumerate(cut))):
        high = swaps.high(stage)
        for c, x in enumerate(held):
            other = swaps.swap(stage, x)
            held[c] = jnp.concatenate([jnp.where(high, other, x), jnp.where(high, x, other)], axis=axis)
    core = swaps.core == 0
    query, value = [], []
    for x in held:
        other = swaps.swap_cores(x)
        query.append(jnp.where(core, x, other) / total)
        value.append(jnp.where(core, other, x) / total)
    return (*query, *value)


def solution(mesh):
    sizes = dict(mesh.shape)
    split = P(AXES)
    placed = (split, split, split, P(), P(), P(), P(), split)

    def step(*args):
        return body(sizes, *args)

    return jax.shard_map(step, mesh=mesh, in_specs=placed, out_specs=(P(),) * 4, check_vma=False)
```

time: 64.1 us -> 46.2 us (0.72)
  waiting for transfers between devices: 29.3 us -> 10.4 us
  matrix products: 8.8 us -> 0 us
  starting transfers between devices: 17.3 us -> 25.1 us
  Pallas kernels: 0 us -> 5.59 us
  other arithmetic: 6.38 us -> 3.48 us
  local copies, waits for them, and re-layouts: 1.31 us -> 0.59 us
    ppermute x6 -> x12, waiting for transfers between devices: 25.3 us -> 10.3 us  [swap(): return lax.ppermute(array, AXES, pairs)]
    dot_general x4 -> x0, matrix products: 8.8 us -> none  [the longest x2 4.45 us: adapter_sums(): lax.dot_general(inner, grad_out, (((0,), (0,)), ((), ())), preferred_elem...]
    ppermute x6 -> x12, starting transfers between devices: 16.7 us -> 24.3 us  [swap(): return lax.ppermute(array, AXES, pairs)]
    pallas_call x0 -> x2, Pallas kernels: none -> 5.59 us  [adapter_sums(): pl.pallas_call(functools.partial(adapter_kernel, PARTS, flip), out_shape=...]
    ppermute x2 -> x4, waiting for transfers between devices: 3.96 us -> 0.1 us  [swap_cores(): lax.ppermute(array, 'gx', [(i, i ^ 1) for i in range(self.sizes['gx'])])]
    div x1 -> x2, other arithmetic: 0.09 us -> 3.02 us  [body(): value.append(jnp.where(core, other, x) / total)]
    select_n x6 -> x8, other arithmetic: 2.14 us -> 0.15 us  [the longest x4 0.08 us: body(): jnp.where(high, other, x)]
    add x5 -> x10, other arithmetic: 2 us -> 0.24 us  [the longest x4 0.1 us: body(): jnp.where(high, high_half, low_half)]
  transfers between devices with their start and end apart: 8 -> 16, of which waited for: 8 -> 8; matrix products, arithmetic and copies ran while one was open for 0% -> 6% of each run, Pallas kernels for 0% -> 6%
where the time goes in v2:
time: 46.2 us; the launch traced here: 46 us
  starting transfers between devices  25.1 us (54%)
  waiting for transfers between devices  10.4 us (23%)
  Pallas kernels  5.59 us (12%)
  other arithmetic  3.48 us (8%)
  between operations  0.8 us (2%)
  local copies, waits for them, and re-layouts  0.59 us (1%)
    ppermute x12, starting transfers between devices, swap(): return lax.ppermute(array, AXES, pairs)  24.3 us
    ppermute x12, waiting for transfers between devices, swap(): return lax.ppermute(array, AXES, pairs)  10.3 us
    pallas_call x2, Pallas kernels, adapter_sums(): pl.pallas_call(functools.partial(adapter_kernel, PARTS, flip), out_shape=...  5.59 us
    div x2, other arithmetic, body(): value.append(jnp.where(core, other, x) / total)  3.02 us
  transfers between devices with their start and end apart: 16, of which 8 were waited for; matrix products, arithmetic and copies ran while one was open for 6% of the time, Pallas kernels for 6%

profile of v2, /device:TPU:0, one launch (start us, length us, event | category | flops | bytes accessed | tf_op | source)
XLA Modules:
  0.0 46.0 jit_solution(1835894637639616572)
XLA Ops:
  0.6 2.8 %adapter.3 = (f32[16,5248]{1,0:T(8,128)S(1)}, f32[16,5120]{1,0:T(8,128)S(1)}) custom-call(s32[2]{0:T(128)} %lengths_in.3, bf16[128,5120]{1,0:T(8,128)(2,1)} %rows.3, bf16[128,5120]{1,0:T(8,128)(2,1)} %query_grad.3, bf16[128,5120]{1,0:T(8,128)(2,1)} %value_grad.3, bf16[16,5120]{1,0:T(8,128)(2,1)} %query_down.3, bf16[16,5120]{1,0:T(8,128)(2,1)} %value_down.3, ...), custom_call_target="tpu_custom_call" | custom-call | flops 83886080 | bytes 2621440 | tf_op jit(solution)/shard_map/adapter/pallas_call | solution.py:91
  3.4 0.6 %collective-permute-start.8 = (f32[16,5120]{1,0:T(8,128)S(1)}, f32[16,5120]{1,0:T(8,128)S(1)}, u32[]{:S(2)}, u32[]{:S(2)}) collective-permute-start(f32[16,5120]{1,0:T(8,128)S(1)} %get-tuple-element.11), channel_id=1, source_target_pairs={{0,8},{8,0},{16,24},{24,16},{1,9},{9,1},{17,25},{25,17},{2,10},{10... | collective-permute-start | bytes 983048 | tf_op jit(solution)/shard_map/ppermute | solution.py:151
  4.0 0.1 collective-permute-start
  4.1 2.8 %adapter.2 = (f32[16,5248]{1,0:T(8,128)S(1)}, f32[16,5120]{1,0:T(8,128)S(1)}) custom-call(s32[2]{0:T(128)} %lengths_in.3, bf16[128,5120]{1,0:T(8,128)(2,1)} %rows.3, bf16[128,5120]{1,0:T(8,128)(2,1)} %query_grad.3, bf16[128,5120]{1,0:T(8,128)(2,1)} %value_grad.3, bf16[16,5120]{1,0:T(8,128)(2,1)} %query_down.3, bf16[16,5120]{1,0:T(8,128)(2,1)} %value_down.3, ...), custom_call_target="tpu_custom_call" | custom-call | flops 83886080 | bytes 2621440 | tf_op jit(solution)/shard_map/adapter/pallas_call | solution.py:91
  6.9 0.0 collective-permute-done.8
  7.0 3.0 %collective-permute-start.9 = (f32[8,5120]{1,0:T(8,128)S(1)}, f32[8,5120]{1,0:T(8,128)S(1)}, u32[]{:S(2)}, u32[]{:S(2)}) collective-permute-start(f32[8,5120]{1,0:T(8,128)S(1)} %slice_select_fusion.1), channel_id=1, source_target_pairs={{0,16},{1,17},{2,18},{3,19},{4,20},{5,21},{6,22},{7,23},{8,12},{9,... | collective-permute-start | bytes 491528 | tf_op jit(solution)/shard_map/ppermute | solution.py:148
  9.9 0.0 collective-permute-done
  10.0 0.1 collective-permute-start.1
  10.1 3.1 %collective-permute-done.9 = f32[8,5120]{1,0:T(8,128)S(1)} collective-permute-done((f32[8,5120]{1,0:T(8,128)S(1)}, f32[8,5120]{1,0:T(8,128)S(1)}, u32[]{:S(2)}, u32[]{:S(2)}) %collective-permute-start.9) | collective-permute-done | bytes 163872 | tf_op jit(solution)/shard_map/ppermute | solution.py:148
  13.3 2.1 %collective-permute-start.10 = (f32[8,2560]{1,0:T(8,128)S(1)}, f32[8,2560]{1,0:T(8,128)S(1)}, u32[]{:S(2)}, u32[]{:S(2)}) collective-permute-start(f32[8,2560]{1,0:T(8,128)S(1)} %slice_select_fusion.3), channel_id=1, source_target_pairs={{0,4},{1,5},{2,6},{3,7},{4,0},{5,1},{6,2},{7,3},{8,24},{9,25},{10,... | collective-permute-start | bytes 245768 | tf_op jit(solution)/shard_map/ppermute | solution.py:148
  15.4 0.0 collective-permute-done.1
  15.5 1.7 %collective-permute-start.2 = (f32[8,2688]{1,0:T(8,128)S(1)}, f32[8,2688]{1,0:T(8,128)S(1)}, u32[]{:S(2)}, u32[]{:S(2)}) collective-permute-start(f32[8,2688]{1,0:T(8,128)S(1)} %slice_select_fusion.2), channel_id=1, source_target_pairs={{0,4},{1,5},{2,6},{3,7},{4,0},{5,1},{6,2},{7,3},{8,24},{9,25},{10,... | collective-permute-start | bytes 258056 | tf_op jit(solution)/shard_map/ppermute | solution.py:148
  17.2 0.6 %collective-permute-done.10 = f32[8,2560]{1,0:T(8,128)S(1)} collective-permute-done((f32[8,2560]{1,0:T(8,128)S(1)}, f32[8,2560]{1,0:T(8,128)S(1)}, u32[]{:S(2)}, u32[]{:S(2)}) %collective-permute-start.10) | collective-permute-done | bytes 81952 | tf_op jit(solution)/shard_map/ppermute | solution.py:148
  17.8 2.1 %collective-permute-start.11 = (f32[8,2560]{1,0:T(8,128)S(1)}, f32[8,2560]{1,0:T(8,128)S(1)}, u32[]{:S(2)}, u32[]{:S(2)}) collective-permute-start(f32[8,2560]{1,0:T(8,128)S(1)} %select_add_fusion.3), channel_id=1, source_target_pairs={{0,1},{1,0},{2,3},{3,2},{4,5},{5,4},{6,7},{7,6},{8,10},{9,11},{10,... | collective-permute-start | bytes 245768 | tf_op jit(solution)/shard_map/ppermute | solution.py:148
  20.0 0.1 collective-permute-done.2
  20.1 1.8 %collective-permute-start.3 = (f32[8,2688]{1,0:T(8,128)S(1)}, f32[8,2688]{1,0:T(8,128)S(1)}, u32[]{:S(2)}, u32[]{:S(2)}) collective-permute-start(f32[8,2688]{1,0:T(8,128)S(1)} %select_add_fusion.2), channel_id=1, source_target_pairs={{0,1},{1,0},{2,3},{3,2},{4,5},{5,4},{6,7},{7,6},{8,10},{9,11},{10,... | collective-permute-start | bytes 258056 | tf_op jit(solution)/shard_map/ppermute | solution.py:148
  21.9 0.8 %collective-permute-done.11 = f32[8,2560]{1,0:T(8,128)S(1)} collective-permute-done((f32[8,2560]{1,0:T(8,128)S(1)}, f32[8,2560]{1,0:T(8,128)S(1)}, u32[]{:S(2)}, u32[]{:S(2)}) %collective-permute-start.11) | collective-permute-done | bytes 81952 | tf_op jit(solution)/shard_map/ppermute | solution.py:148
  22.7 3.1 %collective-permute-start.12 = (f32[8,2560]{1,0:T(8,128)S(1)}, f32[8,2560]{1,0:T(8,128)S(1)}, u32[]{:S(2)}, u32[]{:S(2)}) collective-permute-start(f32[8,2560]{1,0:T(8,128)S(1)} %add.38), channel_id=1, source_target_pairs={{0,2},{1,3},{2,0},{3,1},{4,6},{5,7},{6,4},{7,5},{8,9},{9,8},{10,11... | collective-permute-start | bytes 245768 | tf_op jit(solution)/shard_map/ppermute | solution.py:148
  25.8 0.0 collective-permute-done.3
  25.8 2.4 %collective-permute-start.4 = (f32[8,2688]{1,0:T(8,128)S(1)}, f32[8,2688]{1,0:T(8,128)S(1)}, u32[]{:S(2)}, u32[]{:S(2)}) collective-permute-start(f32[8,2688]{1,0:T(8,128)S(1)} %add.33), channel_id=1, source_target_pairs={{0,2},{1,3},{2,0},{3,1},{4,6},{5,7},{6,4},{7,5},{8,9},{9,8},{10,11... | collective-permute-start | bytes 258056 | tf_op jit(solution)/shard_map/ppermute | solution.py:148
  28.3 0.0 collective-permute-done.12
  28.3 3.6 %collective-permute-start.13 = (f32[8,2560]{1,0:T(8,128)S(1)}, f32[8,2560]{1,0:T(8,128)S(1)}, u32[]{:S(2)}, u32[]{:S(2)}) collective-permute-start(f32[8,2560]{1,0:T(8,128)S(1)} %add.39), channel_id=1, source_target_pairs={{0,4},{1,5},{2,6},{3,7},{4,0},{5,1},{6,2},{7,3},{8,24},{9,25},{10,... | collective-permute-start | bytes 245768 | tf_op jit(solution)/shard_map/ppermute | solution.py:148
  31.9 0.0 collective-permute-done.4
  31.9 0.6 %slice.47 = f32[1,1]{1,0:T(1,128)} slice(f32[8,2688]{1,0:T(8,128)S(1)} %add.34), slice={[0:1], [2560:2561]} | slice | bytes 8 | tf_op jit(solution)/shard_map/slice | solution.py:192
  32.5 0.9 %collective-permute-start.5 = (f32[8,2560]{1,0:T(8,128)S(1)}, f32[8,2560]{1,0:T(8,128)S(1)}, u32[]{:S(2)}, u32[]{:S(2)}) collective-permute-start(f32[8,2560]{1,0:T(8,128)S(1)} %slice.46), channel_id=1, source_target_pairs={{0,4},{1,5},{2,6},{3,7},{4,0},{5,1},{6,2},{7,3},{8,24},{9,25},{10,... | collective-permute-start | bytes 245768 | tf_op jit(solution)/shard_map/ppermute | solution.py:148
  33.4 1.7 %collective-permute-done.13 = f32[8,2560]{1,0:T(8,128)S(1)} collective-permute-done((f32[8,2560]{1,0:T(8,128)S(1)}, f32[8,2560]{1,0:T(8,128)S(1)}, u32[]{:S(2)}, u32[]{:S(2)}) %collective-permute-start.13) | collective-permute-done | bytes 81952 | tf_op jit(solution)/shard_map/ppermute | solution.py:148
  35.2 2.1 %collective-permute-start.14 = (f32[8,5120]{1,0:T(8,128)S(1)}, f32[8,5120]{1,0:T(8,128)S(1)}, u32[]{:S(2)}, u32[]{:S(2)}) collective-permute-start(f32[8,5120]{1,0:T(8,128)S(1)} %pad_maximum_fusion.3), channel_id=1, source_target_pairs={{0,16},{1,17},{2,18},{3,19},{4,20},{5,21},{6,22},{7,23},{8,12},{9,... | collective-permute-start | bytes 491528 | tf_op jit(solution)/shard_map/ppermute | solution.py:148
  37.3 0.0 collective-permute-done.5
  37.4 1.3 %collective-permute-start.6 = (f32[8,5120]{1,0:T(8,128)S(1)}, f32[8,5120]{1,0:T(8,128)S(1)}, u32[]{:S(2)}, u32[]{:S(2)}) collective-permute-start(f32[8,5120]{1,0:T(8,128)S(1)} %pad_maximum_fusion.2), channel_id=1, source_target_pairs={{0,16},{1,17},{2,18},{3,19},{4,20},{5,21},{6,22},{7,23},{8,12},{9,... | collective-permute-start | bytes 491528 | tf_op jit(solution)/shard_map/ppermute | solution.py:148
  38.7 2.0 %collective-permute-done.14 = f32[8,5120]{1,0:T(8,128)S(1)} collective-permute-done((f32[8,5120]{1,0:T(8,128)S(1)}, f32[8,5120]{1,0:T(8,128)S(1)}, u32[]{:S(2)}, u32[]{:S(2)}) %collective-permute-start.14) | collective-permute-done | bytes 163872 | tf_op jit(solution)/shard_map/ppermute | solution.py:148
  40.7 0.1 collective-permute-start.15
  40.7 2.0 %collective-permute-done.6 = f32[8,5120]{1,0:T(8,128)S(1)} collective-permute-done((f32[8,5120]{1,0:T(8,128)S(1)}, f32[8,5120]{1,0:T(8,128)S(1)}, u32[]{:S(2)}, u32[]{:S(2)}) %collective-permute-start.6) | collective-permute-done | bytes 163872 | tf_op jit(solution)/shard_map/ppermute | solution.py:148
  42.8 0.1 collective-permute-start.7
  42.9 0.0 collective-permute-done.15
  42.9 1.5 %select_divide_fusion = (f32[16,5120]{1,0:T(8,128)}, f32[16,5120]{1,0:T(8,128)}) fusion(f32[16,5120]{1,0:T(8,128)S(1)} %collective-permute-done.15, f32[]{:T(128)} %bitcast, pred[]{:T(512)S(6)} %eq.2, f32[8,5120]{1,0:T(8,128)S(1)} %get-tuple-element.17, f32[8,5120]{1,0:T(8,128)S(1)} %get-tuple-element.16), kind=kLoop, calls=%fused_computation.2 | loop fusion | flops 409600 | bytes 1310725 | tf_op jit(solution)/shard_map/div | solution.py:204
  44.4 0.1 collective-permute-done.7
  44.5 1.5 %select_divide_fusion.1 = (f32[16,5120]{1,0:T(8,128)}, f32[16,5120]{1,0:T(8,128)}) fusion(f32[16,5120]{1,0:T(8,128)S(1)} %collective-permute-done.7, f32[]{:T(128)} %bitcast, pred[]{:T(512)S(6)} %eq.2, f32[8,5120]{1,0:T(8,128)S(1)} %get-tuple-element.19, f32[8,5120]{1,0:T(8,128)S(1)} %get-tuple-element.18), kind=kLoop, calls=%fused_computation.3 | loop fusion | flops 409600 | bytes 1310725 | tf_op jit(solution)/shard_map/div | solution.py:204
  (25 shorter events, 0.5 us)
Async XLA Ops:
  3.4 3.4 %collective-permute-start.8 = (f32[16,5120]{1,0:T(8,128)S(1)}, f32[16,5120]{1,0:T(8,128)S(1)}, u32[]{:S(2)}, u32[]{:S(2)}) collective-permute-start(f32[16,5120]{1,0:T(8,128)S(1)} %get-tuple-element.11), channel_id=1, source_target_pairs={{0,8},{8,0},{16,24},{24,16},{1,9},{9,1},{17,25},{25,17},{2,10},{10... | collective-permute-start | bytes 983048 | tf_op jit(solution)/shard_map/ppermute | solution.py:151
  4.0 5.9 %collective-permute-start = (f32[16,5248]{1,0:T(8,128)S(1)}, f32[16,5248]{1,0:T(8,128)S(1)}, u32[]{:S(2)}, u32[]{:S(2)}) collective-permute-start(f32[16,5248]{1,0:T(8,128)S(1)} %get-tuple-element.9), channel_id=1, source_target_pairs={{0,8},{8,0},{16,24},{24,16},{1,9},{9,1},{17,25},{25,17},{2,10},{10... | collective-permute-start | bytes 1007624 | tf_op jit(solution)/shard_map/ppermute | solution.py:151
  7.0 6.3 %collective-permute-start.9 = (f32[8,5120]{1,0:T(8,128)S(1)}, f32[8,5120]{1,0:T(8,128)S(1)}, u32[]{:S(2)}, u32[]{:S(2)}) collective-permute-start(f32[8,5120]{1,0:T(8,128)S(1)} %slice_select_fusion.1), channel_id=1, source_target_pairs={{0,16},{1,17},{2,18},{3,19},{4,20},{5,21},{6,22},{7,23},{8,12},{9,... | collective-permute-start | bytes 491528 | tf_op jit(solution)/shard_map/ppermute | solution.py:148
  10.0 5.4 %collective-permute-start.1 = (f32[8,5248]{1,0:T(8,128)S(1)}, f32[8,5248]{1,0:T(8,128)S(1)}, u32[]{:S(2)}, u32[]{:S(2)}) collective-permute-start(f32[8,5248]{1,0:T(8,128)S(1)} %slice_select_fusion), channel_id=1, source_target_pairs={{0,16},{1,17},{2,18},{3,19},{4,20},{5,21},{6,22},{7,23},{8,12},{9,... | collective-permute-start | bytes 503816 | tf_op jit(solution)/shard_map/ppermute | solution.py:148
  13.3 4.5 %collective-permute-start.10 = (f32[8,2560]{1,0:T(8,128)S(1)}, f32[8,2560]{1,0:T(8,128)S(1)}, u32[]{:S(2)}, u32[]{:S(2)}) collective-permute-start(f32[8,2560]{1,0:T(8,128)S(1)} %slice_select_fusion.3), channel_id=1, source_target_pairs={{0,4},{1,5},{2,6},{3,7},{4,0},{5,1},{6,2},{7,3},{8,24},{9,25},{10,... | collective-permute-start | bytes 245768 | tf_op jit(solution)/shard_map/ppermute | solution.py:148
  15.5 4.6 %collective-permute-start.2 = (f32[8,2688]{1,0:T(8,128)S(1)}, f32[8,2688]{1,0:T(8,128)S(1)}, u32[]{:S(2)}, u32[]{:S(2)}) collective-permute-start(f32[8,2688]{1,0:T(8,128)S(1)} %slice_select_fusion.2), channel_id=1, source_target_pairs={{0,4},{1,5},{2,6},{3,7},{4,0},{5,1},{6,2},{7,3},{8,24},{9,25},{10,... | collective-permute-start | bytes 258056 | tf_op jit(solution)/shard_map/ppermute | solution.py:148
  17.8 4.8 %collective-permute-start.11 = (f32[8,2560]{1,0:T(8,128)S(1)}, f32[8,2560]{1,0:T(8,128)S(1)}, u32[]{:S(2)}, u32[]{:S(2)}) collective-permute-start(f32[8,2560]{1,0:T(8,128)S(1)} %select_add_fusion.3), channel_id=1, source_target_pairs={{0,1},{1,0},{2,3},{3,2},{4,5},{5,4},{6,7},{7,6},{8,10},{9,11},{10,... | collective-permute-start | bytes 245768 | tf_op jit(solution)/shard_map/ppermute | solution.py:148
  20.1 5.7 %collective-permute-start.3 = (f32[8,2688]{1,0:T(8,128)S(1)}, f32[8,2688]{1,0:T(8,128)S(1)}, u32[]{:S(2)}, u32[]{:S(2)}) collective-permute-start(f32[8,2688]{1,0:T(8,128)S(1)} %select_add_fusion.2), channel_id=1, source_target_pairs={{0,1},{1,0},{2,3},{3,2},{4,5},{5,4},{6,7},{7,6},{8,10},{9,11},{10,... | collective-permute-start | bytes 258056 | tf_op jit(solution)/shard_map/ppermute | solution.py:148
  22.7 5.6 %collective-permute-start.12 = (f32[8,2560]{1,0:T(8,128)S(1)}, f32[8,2560]{1,0:T(8,128)S(1)}, u32[]{:S(2)}, u32[]{:S(2)}) collective-permute-start(f32[8,2560]{1,0:T(8,128)S(1)} %add.38), channel_id=1, source_target_pairs={{0,2},{1,3},{2,0},{3,1},{4,6},{5,7},{6,4},{7,5},{8,9},{9,8},{10,11... | collective-permute-start | bytes 245768 | tf_op jit(solution)/shard_map/ppermute | solution.py:148
  25.8 6.1 %collective-permute-start.4 = (f32[8,2688]{1,0:T(8,128)S(1)}, f32[8,2688]{1,0:T(8,128)S(1)}, u32[]{:S(2)}, u32[]{:S(2)}) collective-permute-start(f32[8,2688]{1,0:T(8,128)S(1)} %add.33), channel_id=1, source_target_pairs={{0,2},{1,3},{2,0},{3,1},{4,6},{5,7},{6,4},{7,5},{8,9},{9,8},{10,11... | collective-permute-start | bytes 258056 | tf_op jit(solution)/shard_map/ppermute | solution.py:148
  28.3 6.8 %collective-permute-start.13 = (f32[8,2560]{1,0:T(8,128)S(1)}, f32[8,2560]{1,0:T(8,128)S(1)}, u32[]{:S(2)}, u32[]{:S(2)}) collective-permute-start(f32[8,2560]{1,0:T(8,128)S(1)} %add.39), channel_id=1, source_target_pairs={{0,4},{1,5},{2,6},{3,7},{4,0},{5,1},{6,2},{7,3},{8,24},{9,25},{10,... | collective-permute-start | bytes 245768 | tf_op jit(solution)/shard_map/ppermute | solution.py:148
  32.5 4.8 %collective-permute-start.5 = (f32[8,2560]{1,0:T(8,128)S(1)}, f32[8,2560]{1,0:T(8,128)S(1)}, u32[]{:S(2)}, u32[]{:S(2)}) collective-permute-start(f32[8,2560]{1,0:T(8,128)S(1)} %slice.46), channel_id=1, source_target_pairs={{0,4},{1,5},{2,6},{3,7},{4,0},{5,1},{6,2},{7,3},{8,24},{9,25},{10,... | collective-permute-start | bytes 245768 | tf_op jit(solution)/shard_map/ppermute | solution.py:148
  35.2 5.4 %collective-permute-start.14 = (f32[8,5120]{1,0:T(8,128)S(1)}, f32[8,5120]{1,0:T(8,128)S(1)}, u32[]{:S(2)}, u32[]{:S(2)}) collective-permute-start(f32[8,5120]{1,0:T(8,128)S(1)} %pad_maximum_fusion.3), channel_id=1, source_target_pairs={{0,16},{1,17},{2,18},{3,19},{4,20},{5,21},{6,22},{7,23},{8,12},{9,... | collective-permute-start | bytes 491528 | tf_op jit(solution)/shard_map/ppermute | solution.py:148
  37.4 5.4 %collective-permute-start.6 = (f32[8,5120]{1,0:T(8,128)S(1)}, f32[8,5120]{1,0:T(8,128)S(1)}, u32[]{:S(2)}, u32[]{:S(2)}) collective-permute-start(f32[8,5120]{1,0:T(8,128)S(1)} %pad_maximum_fusion.2), channel_id=1, source_target_pairs={{0,16},{1,17},{2,18},{3,19},{4,20},{5,21},{6,22},{7,23},{8,12},{9,... | collective-permute-start | bytes 491528 | tf_op jit(solution)/shard_map/ppermute | solution.py:148
  40.7 2.2 %collective-permute-start.15 = (f32[16,5120]{1,0:T(8,128)S(1)}, f32[16,5120]{1,0:T(8,128)S(1)}, u32[]{:S(2)}, u32[]{:S(2)}) collective-permute-start(f32[16,5120]{1,0:T(8,128)S(1)} %pad_maximum_fusion.1), channel_id=1, source_target_pairs={{0,8},{8,0},{16,24},{24,16},{1,9},{9,1},{17,25},{25,17},{2,10},{10... | collective-permute-start | bytes 983048 | tf_op jit(solution)/shard_map/ppermute | solution.py:151
  42.8 1.7 %collective-permute-start.7 = (f32[16,5120]{1,0:T(8,128)S(1)}, f32[16,5120]{1,0:T(8,128)S(1)}, u32[]{:S(2)}, u32[]{:S(2)}) collective-permute-start(f32[16,5120]{1,0:T(8,128)S(1)} %pad_maximum_fusion), channel_id=1, source_target_pairs={{0,8},{8,0},{16,24},{24,16},{1,9},{9,1},{17,25},{25,17},{2,10},{10... | collective-permute-start | bytes 983048 | tf_op jit(solution)/shard_map/ppermute | solution.py:151

commit v3 on v2

--- a/solution.py
+++ b/solution.py
@@ -105,6 +105,37 @@
     )(*args)
 
 
+def finish_kernel(mine, other, total, query, value, out, sems):
+    core = lax.axis_index("gx") & 1
+    rows = mine.shape[0] // 2
+    by = total[0, 0]
+    copies = []
+    for k in range(2):
+        cut = pl.ds(k * rows, rows)
+        out[core, cut] = mine[cut] / by
+        out[1 - core, cut] = other[cut] / by
+        for c, target in enumerate((query, value)):
+            copies.append(pltpu.make_async_copy(out.at[c, cut], target.at[cut], sems.at[c, k]))
+            copies[-1].start()
+    for copy in copies:
+        copy.wait()
+
+
+def finish(mine, other, total):
+    near = pl.BlockSpec(memory_space=pltpu.VMEM)
+    far = pl.BlockSpec(memory_space=pltpu.HBM)
+    return pl.pallas_call(
+        finish_kernel,
+        out_shape=(jax.ShapeDtypeStruct(mine.shape, mine.dtype),) * 2,
+        in_specs=[near] * 3,
+        out_specs=(far,) * 2,
+        scratch_shapes=[pltpu.VMEM((2, *mine.shape), mine.dtype), pltpu.SemaphoreType.DMA((2, 2))],
+        compiler_params=pltpu.CompilerParams(vmem_limit_bytes=8 << 20),
+        cost_estimate=pl.CostEstimate(flops=2 * mine.size, bytes_accessed=16 * mine.size, transcendentals=0),
+        name="finish",
+    )(*(pltpu.with_memory_space_constraint(x, pltpu.VMEM) for x in (mine, other, total)))
+
+
 def axis_bits(axis, size, first=0):
     bits = size.bit_length() - 1
     assert size == 1 << bits
@@ -130,18 +161,18 @@
     def count(self):
         return len(self.orders[0])
 
-    def high(self, stage):
+    def high(self, stage, chain):
         flags = [(self.at[axis] & bit) != 0 for axis, bit in (order[stage] for order in self.orders)]
-        return jnp.where(self.core == 0, flags[0], flags[1])
-
-    def swap(self, stage, array):
+        return jnp.where(self.core == chain, flags[0], flags[1])
+
+    def swap(self, stage, chain, array):
         gx, gy, gz = (self.sizes[axis] for axis in AXES)
         pairs = []
         for i in range(gx):
             for j in range(gy):
                 for k in range(gz):
                     place = {"gx": i, "gy": j, "gz": k}
-                    axis, bit = self.orders[i & 1][stage]
+                    axis, bit = self.orders[(i & 1) ^ chain][stage]
                     place[axis] ^= bit
                     there = (place["gx"] * gy + place["gy"]) * gz + place["gz"]
                     pairs.append(((i * gy + j) * gz + k, there))
@@ -180,28 +211,24 @@
             elif widths[0] % (2 * LANES) == 0 and len(cut) < 2:
                 axis = 1
         if axis is None:
-            held = [x + swaps.swap(stage, x) for x in held]
+            held = [x + swaps.swap(stage, c, x) for c, x in enumerate(held)]
             continue
-        high = swaps.high(stage)
         for c, x in enumerate(held):
+            high = swaps.high(stage, c)
             low_half, high_half = halves(x, widths[c], axis)
-            held[c] = jnp.where(high, high_half, low_half) + swaps.swap(stage, jnp.where(high, low_half, high_half))
+            sent = jnp.where(high, low_half, high_half)
+            held[c] = jnp.where(high, high_half, low_half) + swaps.swap(stage, c, sent)
             if axis == 1:
                 widths[c] //= 2
         cut.append(axis)
-    total = held[0][0, widths[0]]
+    total = held[0][:, widths[0]:]
     held = [x[:, :width] for x, width in zip(held, widths)]
     for stage, axis in reversed(list(enumerate(cut))):
-        high = swaps.high(stage)
         for c, x in enumerate(held):
-            other = swaps.swap(stage, x)
+            high = swaps.high(stage, c)
+            other = swaps.swap(stage, c, x)
             held[c] = jnp.concatenate([jnp.where(high, other, x), jnp.where(high, x, other)], axis=axis)
-    core = swaps.core == 0
-    query, value = [], []
-    for x in held:
-        other = swaps.swap_cores(x)
-        query.append(jnp.where(core, x, other) / total)
-        value.append(jnp.where(core, other, x) / total)
+    query, value = zip(*(finish(x, swaps.swap_cores(x), total) for x in held))
     return (*query, *value)
 
 

time: 46.2 us -> 48.4 us (1.048)
  waiting for transfers between devices: 10.4 us -> 17.3 us
  other arithmetic: 3.48 us -> 0.45 us
  starting transfers between devices: 25.1 us -> 22.2 us
  Pallas kernels: 5.59 us -> 7.45 us
  local copies, waits for them, and re-layouts: 0.59 us -> 0.02 us
    ppermute x12, waiting for transfers between devices: 10.3 us -> 16.6 us  [swap(): return lax.ppermute(array, AXES, pairs)]
    div x2 -> x0, other arithmetic: 3.02 us -> none  [body(): value.append(jnp.where(core, other, x) / total)]
    ppermute x12, starting transfers between devices: 24.3 us -> 21.4 us  [swap(): return lax.ppermute(array, AXES, pairs)]
    pallas_call x0 -> x2, Pallas kernels: none -> 1.85 us  [finish(): pl.pallas_call(finish_kernel, out_shape=(jax.ShapeDtypeStruct(mine.shape,...]
    slice x1, local copies, waits for them, and re-layouts: 0.58 us -> 0.01 us  [body(): total = held[0][:, widths[0]:]]
    ppermute x4, waiting for transfers between devices: 0.1 us -> 0.67 us  [swap_cores(): lax.ppermute(array, 'gx', [(i, i ^ 1) for i in range(self.sizes['gx'])])]
  transfers between devices with their start and end apart: 16 -> 16, of which waited for: 8 -> 10; matrix products, arithmetic and copies ran while one was open for 6% -> 1% of each run, Pallas kernels for 6% -> 8%
where the time goes in v3:
time: 48.4 us; the launch traced here: 48.2 us
  starting transfers between devices  22.2 us (46%)
  waiting for transfers between devices  17.3 us (36%)
  Pallas kernels  7.45 us (15%)
  between operations  0.82 us (2%)
    ppermute x12, starting transfers between devices, swap(): return lax.ppermute(array, AXES, pairs)  21.4 us
    ppermute x12, waiting for transfers between devices, swap(): return lax.ppermute(array, AXES, pairs)  16.6 us
    pallas_call x2, Pallas kernels, adapter_sums(): pl.pallas_call(functools.partial(adapter_kernel, PARTS, flip), out_shape=...  5.59 us
    pallas_call x2, Pallas kernels, finish(): pl.pallas_call(finish_kernel, out_shape=(jax.ShapeDtypeStruct(mine.shape,...  1.85 us
  transfers between devices with their start and end apart: 16, of which 10 were waited for; matrix products, arithmetic and copies ran while one was open for 1% of the time, Pallas kernels for 8%

profile of v3, /device:TPU:0, one launch (start us, length us, event | category | flops | bytes accessed | tf_op | source)
XLA Modules:
  0.0 48.2 jit_solution(11053355225882198780)
XLA Ops:
  0.6 2.8 %adapter.3 = (f32[16,5248]{1,0:T(8,128)S(1)}, f32[16,5120]{1,0:T(8,128)S(1)}) custom-call(s32[2]{0:T(128)} %lengths_in.3, bf16[128,5120]{1,0:T(8,128)(2,1)} %rows.3, bf16[128,5120]{1,0:T(8,128)(2,1)} %query_grad.3, bf16[128,5120]{1,0:T(8,128)(2,1)} %value_grad.3, bf16[16,5120]{1,0:T(8,128)(2,1)} %query_down.3, bf16[16,5120]{1,0:T(8,128)(2,1)} %value_down.3, ...), custom_call_target="tpu_custom_call" | custom-call | flops 83886080 | bytes 2621440 | tf_op jit(solution)/shard_map/adapter/pallas_call | solution.py:91
  3.4 0.6 %collective-permute-start.8 = (f32[16,5120]{1,0:T(8,128)S(1)}, f32[16,5120]{1,0:T(8,128)S(1)}, u32[]{:S(2)}, u32[]{:S(2)}) collective-permute-start(f32[16,5120]{1,0:T(8,128)S(1)} %get-tuple-element.16), channel_id=1, source_target_pairs={{0,8},{8,0},{16,24},{24,16},{1,9},{9,1},{17,25},{25,17},{2,10},{10... | collective-permute-start | bytes 983048 | tf_op jit(solution)/shard_map/ppermute | solution.py:182
  4.0 0.1 collective-permute-start
  4.1 2.8 %adapter.2 = (f32[16,5248]{1,0:T(8,128)S(1)}, f32[16,5120]{1,0:T(8,128)S(1)}) custom-call(s32[2]{0:T(128)} %lengths_in.3, bf16[128,5120]{1,0:T(8,128)(2,1)} %rows.3, bf16[128,5120]{1,0:T(8,128)(2,1)} %query_grad.3, bf16[128,5120]{1,0:T(8,128)(2,1)} %value_grad.3, bf16[16,5120]{1,0:T(8,128)(2,1)} %query_down.3, bf16[16,5120]{1,0:T(8,128)(2,1)} %value_down.3, ...), custom_call_target="tpu_custom_call" | custom-call | flops 83886080 | bytes 2621440 | tf_op jit(solution)/shard_map/adapter/pallas_call | solution.py:91
  6.9 0.0 collective-permute-done.8
  7.0 3.0 %collective-permute-start.9 = (f32[8,5120]{1,0:T(8,128)S(1)}, f32[8,5120]{1,0:T(8,128)S(1)}, u32[]{:S(2)}, u32[]{:S(2)}) collective-permute-start(f32[8,5120]{1,0:T(8,128)S(1)} %slice_select_fusion.1), channel_id=1, source_target_pairs={{0,4},{1,5},{2,6},{3,7},{4,0},{5,1},{6,2},{7,3},{8,24},{9,25},{10,... | collective-permute-start | bytes 491528 | tf_op jit(solution)/shard_map/ppermute | solution.py:179
  10.0 0.0 collective-permute-done
  10.0 1.6 %collective-permute-start.1 = (f32[8,5248]{1,0:T(8,128)S(1)}, f32[8,5248]{1,0:T(8,128)S(1)}, u32[]{:S(2)}, u32[]{:S(2)}) collective-permute-start(f32[8,5248]{1,0:T(8,128)S(1)} %slice_select_fusion), channel_id=1, source_target_pairs={{0,16},{1,17},{2,18},{3,19},{4,20},{5,21},{6,22},{7,23},{8,12},{9,... | collective-permute-start | bytes 503816 | tf_op jit(solution)/shard_map/ppermute | solution.py:179
  11.6 2.5 %collective-permute-done.9 = f32[8,5120]{1,0:T(8,128)S(1)} collective-permute-done((f32[8,5120]{1,0:T(8,128)S(1)}, f32[8,5120]{1,0:T(8,128)S(1)}, u32[]{:S(2)}, u32[]{:S(2)}) %collective-permute-start.9) | collective-permute-done | bytes 163872 | tf_op jit(solution)/shard_map/ppermute | solution.py:179
  14.1 2.3 %collective-permute-start.10 = (f32[8,2560]{1,0:T(8,128)S(1)}, f32[8,2560]{1,0:T(8,128)S(1)}, u32[]{:S(2)}, u32[]{:S(2)}) collective-permute-start(f32[8,2560]{1,0:T(8,128)S(1)} %slice_select_fusion.3), channel_id=1, source_target_pairs={{0,16},{1,17},{2,18},{3,19},{4,20},{5,21},{6,22},{7,23},{8,12},{9,... | collective-permute-start | bytes 245768 | tf_op jit(solution)/shard_map/ppermute | solution.py:179
  16.5 0.0 collective-permute-done.1
  16.5 1.8 %collective-permute-start.2 = (f32[8,2688]{1,0:T(8,128)S(1)}, f32[8,2688]{1,0:T(8,128)S(1)}, u32[]{:S(2)}, u32[]{:S(2)}) collective-permute-start(f32[8,2688]{1,0:T(8,128)S(1)} %slice_select_fusion.2), channel_id=1, source_target_pairs={{0,4},{1,5},{2,6},{3,7},{4,0},{5,1},{6,2},{7,3},{8,24},{9,25},{10,... | collective-permute-start | bytes 258056 | tf_op jit(solution)/shard_map/ppermute | solution.py:179
  18.3 1.4 %collective-permute-done.10 = f32[8,2560]{1,0:T(8,128)S(1)} collective-permute-done((f32[8,2560]{1,0:T(8,128)S(1)}, f32[8,2560]{1,0:T(8,128)S(1)}, u32[]{:S(2)}, u32[]{:S(2)}) %collective-permute-start.10) | collective-permute-done | bytes 81952 | tf_op jit(solution)/shard_map/ppermute | solution.py:179
  19.7 3.1 %collective-permute-start.11 = (f32[8,2560]{1,0:T(8,128)S(1)}, f32[8,2560]{1,0:T(8,128)S(1)}, u32[]{:S(2)}, u32[]{:S(2)}) collective-permute-start(f32[8,2560]{1,0:T(8,128)S(1)} %select_add_fusion.3), channel_id=1, source_target_pairs={{0,2},{1,3},{2,0},{3,1},{4,6},{5,7},{6,4},{7,5},{8,9},{9,8},{10,11... | collective-permute-start | bytes 245768 | tf_op jit(solution)/shard_map/ppermute | solution.py:179
  22.8 0.0 collective-permute-done.2
  22.8 1.6 %collective-permute-start.3 = (f32[8,2688]{1,0:T(8,128)S(1)}, f32[8,2688]{1,0:T(8,128)S(1)}, u32[]{:S(2)}, u32[]{:S(2)}) collective-permute-start(f32[8,2688]{1,0:T(8,128)S(1)} %select_add_fusion.2), channel_id=1, source_target_pairs={{0,1},{1,0},{2,3},{3,2},{4,5},{5,4},{6,7},{7,6},{8,10},{9,11},{10,... | collective-permute-start | bytes 258056 | tf_op jit(solution)/shard_map/ppermute | solution.py:179
  24.5 3.7 %collective-permute-done.11 = f32[8,2560]{1,0:T(8,128)S(1)} collective-permute-done((f32[8,2560]{1,0:T(8,128)S(1)}, f32[8,2560]{1,0:T(8,128)S(1)}, u32[]{:S(2)}, u32[]{:S(2)}) %collective-permute-start.11) | collective-permute-done | bytes 81952 | tf_op jit(solution)/shard_map/ppermute | solution.py:179
  28.2 0.5 %collective-permute-start.12 = (f32[8,2560]{1,0:T(8,128)S(1)}, f32[8,2560]{1,0:T(8,128)S(1)}, u32[]{:S(2)}, u32[]{:S(2)}) collective-permute-start(f32[8,2560]{1,0:T(8,128)S(1)} %add.38), channel_id=1, source_target_pairs={{0,1},{1,0},{2,3},{3,2},{4,5},{5,4},{6,7},{7,6},{8,10},{9,11},{10,... | collective-permute-start | bytes 245768 | tf_op jit(solution)/shard_map/ppermute | solution.py:179
  28.7 0.0 collective-permute-done.3
  28.8 3.4 %collective-permute-start.4 = (f32[8,2688]{1,0:T(8,128)S(1)}, f32[8,2688]{1,0:T(8,128)S(1)}, u32[]{:S(2)}, u32[]{:S(2)}) collective-permute-start(f32[8,2688]{1,0:T(8,128)S(1)} %add.33), channel_id=1, source_target_pairs={{0,2},{1,3},{2,0},{3,1},{4,6},{5,7},{6,4},{7,5},{8,9},{9,8},{10,11... | collective-permute-start | bytes 258056 | tf_op jit(solution)/shard_map/ppermute | solution.py:179
  32.2 0.5 %collective-permute-done.12 = f32[8,2560]{1,0:T(8,128)S(1)} collective-permute-done((f32[8,2560]{1,0:T(8,128)S(1)}, f32[8,2560]{1,0:T(8,128)S(1)}, u32[]{:S(2)}, u32[]{:S(2)}) %collective-permute-start.12) | collective-permute-done | bytes 81952 | tf_op jit(solution)/shard_map/ppermute | solution.py:179
  32.7 0.7 %collective-permute-start.13 = (f32[8,2560]{1,0:T(8,128)S(1)}, f32[8,2560]{1,0:T(8,128)S(1)}, u32[]{:S(2)}, u32[]{:S(2)}) collective-permute-start(f32[8,2560]{1,0:T(8,128)S(1)} %add.39), channel_id=1, source_target_pairs={{0,16},{1,17},{2,18},{3,19},{4,20},{5,21},{6,22},{7,23},{8,12},{9,... | collective-permute-start | bytes 245768 | tf_op jit(solution)/shard_map/ppermute | solution.py:179
  33.4 2.2 %collective-permute-done.4 = f32[8,2688]{1,0:T(8,128)S(1)} collective-permute-done((f32[8,2688]{1,0:T(8,128)S(1)}, f32[8,2688]{1,0:T(8,128)S(1)}, u32[]{:S(2)}, u32[]{:S(2)}) %collective-permute-start.4) | collective-permute-done | bytes 86048 | tf_op jit(solution)/shard_map/ppermute | solution.py:179
  35.6 1.3 %collective-permute-start.5 = (f32[8,2560]{1,0:T(8,128)S(1)}, f32[8,2560]{1,0:T(8,128)S(1)}, u32[]{:S(2)}, u32[]{:S(2)}) collective-permute-start(f32[8,2560]{1,0:T(8,128)S(1)} %slice.46), channel_id=1, source_target_pairs={{0,4},{1,5},{2,6},{3,7},{4,0},{5,1},{6,2},{7,3},{8,24},{9,25},{10,... | collective-permute-start | bytes 245768 | tf_op jit(solution)/shard_map/ppermute | solution.py:179
  36.9 0.7 %collective-permute-done.13 = f32[8,2560]{1,0:T(8,128)S(1)} collective-permute-done((f32[8,2560]{1,0:T(8,128)S(1)}, f32[8,2560]{1,0:T(8,128)S(1)}, u32[]{:S(2)}, u32[]{:S(2)}) %collective-permute-start.13) | collective-permute-done | bytes 81952 | tf_op jit(solution)/shard_map/ppermute | solution.py:179
  37.6 1.3 %collective-permute-start.14 = (f32[8,5120]{1,0:T(8,128)S(1)}, f32[8,5120]{1,0:T(8,128)S(1)}, u32[]{:S(2)}, u32[]{:S(2)}) collective-permute-start(f32[8,5120]{1,0:T(8,128)S(1)} %pad_maximum_fusion.3), channel_id=1, source_target_pairs={{0,4},{1,5},{2,6},{3,7},{4,0},{5,1},{6,2},{7,3},{8,24},{9,25},{10,... | collective-permute-start | bytes 491528 | tf_op jit(solution)/shard_map/ppermute | solution.py:179
  38.9 1.2 %collective-permute-done.5 = f32[8,2560]{1,0:T(8,128)S(1)} collective-permute-done((f32[8,2560]{1,0:T(8,128)S(1)}, f32[8,2560]{1,0:T(8,128)S(1)}, u32[]{:S(2)}, u32[]{:S(2)}) %collective-permute-start.5) | collective-permute-done | bytes 81952 | tf_op jit(solution)/shard_map/ppermute | solution.py:179
  40.2 0.8 %collective-permute-start.6 = (f32[8,5120]{1,0:T(8,128)S(1)}, f32[8,5120]{1,0:T(8,128)S(1)}, u32[]{:S(2)}, u32[]{:S(2)}) collective-permute-start(f32[8,5120]{1,0:T(8,128)S(1)} %pad_maximum_fusion.2), channel_id=1, source_target_pairs={{0,16},{1,17},{2,18},{3,19},{4,20},{5,21},{6,22},{7,23},{8,12},{9,... | collective-permute-start | bytes 491528 | tf_op jit(solution)/shard_map/ppermute | solution.py:179
  41.0 2.0 %collective-permute-done.14 = f32[8,5120]{1,0:T(8,128)S(1)} collective-permute-done((f32[8,5120]{1,0:T(8,128)S(1)}, f32[8,5120]{1,0:T(8,128)S(1)}, u32[]{:S(2)}, u32[]{:S(2)}) %collective-permute-start.14) | collective-permute-done | bytes 163872 | tf_op jit(solution)/shard_map/ppermute | solution.py:179
  43.1 0.1 collective-permute-start.15
  43.2 2.4 %collective-permute-done.6 = f32[8,5120]{1,0:T(8,128)S(1)} collective-permute-done((f32[8,5120]{1,0:T(8,128)S(1)}, f32[8,5120]{1,0:T(8,128)S(1)}, u32[]{:S(2)}, u32[]{:S(2)}) %collective-permute-start.6) | collective-permute-done | bytes 163872 | tf_op jit(solution)/shard_map/ppermute | solution.py:179
  45.6 0.1 collective-permute-start.7
  45.7 0.0 collective-permute-done.15.other
  45.7 0.9 %finish.3 = (f32[16,5120]{1,0:T(8,128)}, f32[16,5120]{1,0:T(8,128)}) custom-call(f32[16,5120]{1,0:T(8,128)S(1)} %pad_maximum_fusion.1.mine, f32[16,5120]{1,0:T(8,128)S(1)} %collective-permute-done.15.other, f32[8,128]{1,0:T(8,128)S(1)} %slice.47.total), custom_call_target="tpu_custom_call" | custom-call | flops 163840 | bytes 1310720 | tf_op jit(solution)/shard_map/finish/pallas_call | solution.py:127
  46.6 0.7 %collective-permute-done.7.other = f32[16,5120]{1,0:T(8,128)S(1)} collective-permute-done((f32[16,5120]{1,0:T(8,128)S(1)}, f32[16,5120]{1,0:T(8,128)S(1)}, u32[]{:S(2)}, u32[]{:S(2)}) %collective-permute-start.7) | collective-permute-done | bytes 327712 | tf_op jit(solution)/shard_map/ppermute | solution.py:182
  47.3 0.9 %finish.2 = (f32[16,5120]{1,0:T(8,128)}, f32[16,5120]{1,0:T(8,128)}) custom-call(f32[16,5120]{1,0:T(8,128)S(1)} %pad_maximum_fusion.mine, f32[16,5120]{1,0:T(8,128)S(1)} %collective-permute-done.7.other, f32[8,128]{1,0:T(8,128)S(1)} %slice.47.total), custom_call_target="tpu_custom_call" | custom-call | flops 163840 | bytes 1310720 | tf_op jit(solution)/shard_map/finish/pallas_call | solution.py:127
  (26 shorter events, 0.5 us)
Async XLA Ops:
  3.4 3.4 %collective-permute-start.8 = (f32[16,5120]{1,0:T(8,128)S(1)}, f32[16,5120]{1,0:T(8,128)S(1)}, u32[]{:S(2)}, u32[]{:S(2)}) collective-permute-start(f32[16,5120]{1,0:T(8,128)S(1)} %get-tuple-element.16), channel_id=1, source_target_pairs={{0,8},{8,0},{16,24},{24,16},{1,9},{9,1},{17,25},{25,17},{2,10},{10... | collective-permute-start | bytes 983048 | tf_op jit(solution)/shard_map/ppermute | solution.py:182
  4.0 6.0 %collective-permute-start = (f32[16,5248]{1,0:T(8,128)S(1)}, f32[16,5248]{1,0:T(8,128)S(1)}, u32[]{:S(2)}, u32[]{:S(2)}) collective-permute-start(f32[16,5248]{1,0:T(8,128)S(1)} %get-tuple-element.13), channel_id=1, source_target_pairs={{0,8},{8,0},{16,24},{24,16},{1,9},{9,1},{17,25},{25,17},{2,10},{10... | collective-permute-start | bytes 1007624 | tf_op jit(solution)/shard_map/ppermute | solution.py:182
  7.0 7.1 %collective-permute-start.9 = (f32[8,5120]{1,0:T(8,128)S(1)}, f32[8,5120]{1,0:T(8,128)S(1)}, u32[]{:S(2)}, u32[]{:S(2)}) collective-permute-start(f32[8,5120]{1,0:T(8,128)S(1)} %slice_select_fusion.1), channel_id=1, source_target_pairs={{0,4},{1,5},{2,6},{3,7},{4,0},{5,1},{6,2},{7,3},{8,24},{9,25},{10,... | collective-permute-start | bytes 491528 | tf_op jit(solution)/shard_map/ppermute | solution.py:179
  10.0 6.4 %collective-permute-start.1 = (f32[8,5248]{1,0:T(8,128)S(1)}, f32[8,5248]{1,0:T(8,128)S(1)}, u32[]{:S(2)}, u32[]{:S(2)}) collective-permute-start(f32[8,5248]{1,0:T(8,128)S(1)} %slice_select_fusion), channel_id=1, source_target_pairs={{0,16},{1,17},{2,18},{3,19},{4,20},{5,21},{6,22},{7,23},{8,12},{9,... | collective-permute-start | bytes 503816 | tf_op jit(solution)/shard_map/ppermute | solution.py:179
  14.1 5.6 %collective-permute-start.10 = (f32[8,2560]{1,0:T(8,128)S(1)}, f32[8,2560]{1,0:T(8,128)S(1)}, u32[]{:S(2)}, u32[]{:S(2)}) collective-permute-start(f32[8,2560]{1,0:T(8,128)S(1)} %slice_select_fusion.3), channel_id=1, source_target_pairs={{0,16},{1,17},{2,18},{3,19},{4,20},{5,21},{6,22},{7,23},{8,12},{9,... | collective-permute-start | bytes 245768 | tf_op jit(solution)/shard_map/ppermute | solution.py:179
  16.5 6.3 %collective-permute-start.2 = (f32[8,2688]{1,0:T(8,128)S(1)}, f32[8,2688]{1,0:T(8,128)S(1)}, u32[]{:S(2)}, u32[]{:S(2)}) collective-permute-start(f32[8,2688]{1,0:T(8,128)S(1)} %slice_select_fusion.2), channel_id=1, source_target_pairs={{0,4},{1,5},{2,6},{3,7},{4,0},{5,1},{6,2},{7,3},{8,24},{9,25},{10,... | collective-permute-start | bytes 258056 | tf_op jit(solution)/shard_map/ppermute | solution.py:179
  19.7 8.5 %collective-permute-start.11 = (f32[8,2560]{1,0:T(8,128)S(1)}, f32[8,2560]{1,0:T(8,128)S(1)}, u32[]{:S(2)}, u32[]{:S(2)}) collective-permute-start(f32[8,2560]{1,0:T(8,128)S(1)} %select_add_fusion.3), channel_id=1, source_target_pairs={{0,2},{1,3},{2,0},{3,1},{4,6},{5,7},{6,4},{7,5},{8,9},{9,8},{10,11... | collective-permute-start | bytes 245768 | tf_op jit(solution)/shard_map/ppermute | solution.py:179
  22.8 5.9 %collective-permute-start.3 = (f32[8,2688]{1,0:T(8,128)S(1)}, f32[8,2688]{1,0:T(8,128)S(1)}, u32[]{:S(2)}, u32[]{:S(2)}) collective-permute-start(f32[8,2688]{1,0:T(8,128)S(1)} %select_add_fusion.2), channel_id=1, source_target_pairs={{0,1},{1,0},{2,3},{3,2},{4,5},{5,4},{6,7},{7,6},{8,10},{9,11},{10,... | collective-permute-start | bytes 258056 | tf_op jit(solution)/shard_map/ppermute | solution.py:179
  28.2 4.5 %collective-permute-start.12 = (f32[8,2560]{1,0:T(8,128)S(1)}, f32[8,2560]{1,0:T(8,128)S(1)}, u32[]{:S(2)}, u32[]{:S(2)}) collective-permute-start(f32[8,2560]{1,0:T(8,128)S(1)} %add.38), channel_id=1, source_target_pairs={{0,1},{1,0},{2,3},{3,2},{4,5},{5,4},{6,7},{7,6},{8,10},{9,11},{10,... | collective-permute-start | bytes 245768 | tf_op jit(solution)/shard_map/ppermute | solution.py:179
  28.8 6.8 %collective-permute-start.4 = (f32[8,2688]{1,0:T(8,128)S(1)}, f32[8,2688]{1,0:T(8,128)S(1)}, u32[]{:S(2)}, u32[]{:S(2)}) collective-permute-start(f32[8,2688]{1,0:T(8,128)S(1)} %add.33), channel_id=1, source_target_pairs={{0,2},{1,3},{2,0},{3,1},{4,6},{5,7},{6,4},{7,5},{8,9},{9,8},{10,11... | collective-permute-start | bytes 258056 | tf_op jit(solution)/shard_map/ppermute | solution.py:179
  32.7 4.9 %collective-permute-start.13 = (f32[8,2560]{1,0:T(8,128)S(1)}, f32[8,2560]{1,0:T(8,128)S(1)}, u32[]{:S(2)}, u32[]{:S(2)}) collective-permute-start(f32[8,2560]{1,0:T(8,128)S(1)} %add.39), channel_id=1, source_target_pairs={{0,16},{1,17},{2,18},{3,19},{4,20},{5,21},{6,22},{7,23},{8,12},{9,... | collective-permute-start | bytes 245768 | tf_op jit(solution)/shard_map/ppermute | solution.py:179
  35.6 4.5 %collective-permute-start.5 = (f32[8,2560]{1,0:T(8,128)S(1)}, f32[8,2560]{1,0:T(8,128)S(1)}, u32[]{:S(2)}, u32[]{:S(2)}) collective-permute-start(f32[8,2560]{1,0:T(8,128)S(1)} %slice.46), channel_id=1, source_target_pairs={{0,4},{1,5},{2,6},{3,7},{4,0},{5,1},{6,2},{7,3},{8,24},{9,25},{10,... | collective-permute-start | bytes 245768 | tf_op jit(solution)/shard_map/ppermute | solution.py:179
  37.6 5.4 %collective-permute-start.14 = (f32[8,5120]{1,0:T(8,128)S(1)}, f32[8,5120]{1,0:T(8,128)S(1)}, u32[]{:S(2)}, u32[]{:S(2)}) collective-permute-start(f32[8,5120]{1,0:T(8,128)S(1)} %pad_maximum_fusion.3), channel_id=1, source_target_pairs={{0,4},{1,5},{2,6},{3,7},{4,0},{5,1},{6,2},{7,3},{8,24},{9,25},{10,... | collective-permute-start | bytes 491528 | tf_op jit(solution)/shard_map/ppermute | solution.py:179
  40.2 5.4 %collective-permute-start.6 = (f32[8,5120]{1,0:T(8,128)S(1)}, f32[8,5120]{1,0:T(8,128)S(1)}, u32[]{:S(2)}, u32[]{:S(2)}) collective-permute-start(f32[8,5120]{1,0:T(8,128)S(1)} %pad_maximum_fusion.2), channel_id=1, source_target_pairs={{0,16},{1,17},{2,18},{3,19},{4,20},{5,21},{6,22},{7,23},{8,12},{9,... | collective-permute-start | bytes 491528 | tf_op jit(solution)/shard_map/ppermute | solution.py:179
  43.1 2.6 %collective-permute-start.15 = (f32[16,5120]{1,0:T(8,128)S(1)}, f32[16,5120]{1,0:T(8,128)S(1)}, u32[]{:S(2)}, u32[]{:S(2)}) collective-permute-start(f32[16,5120]{1,0:T(8,128)S(1)} %pad_maximum_fusion.1.mine), channel_id=1, source_target_pairs={{0,8},{8,0},{16,24},{24,16},{1,9},{9,1},{17,25},{25,17},{2,10},{10... | collective-permute-start | bytes 983048 | tf_op jit(solution)/shard_map/ppermute | solution.py:182
  45.6 1.7 %collective-permute-start.7 = (f32[16,5120]{1,0:T(8,128)S(1)}, f32[16,5120]{1,0:T(8,128)S(1)}, u32[]{:S(2)}, u32[]{:S(2)}) collective-permute-start(f32[16,5120]{1,0:T(8,128)S(1)} %pad_maximum_fusion.mine), channel_id=1, source_target_pairs={{0,8},{8,0},{16,24},{24,16},{1,9},{9,1},{17,25},{25,17},{2,10},{10... | collective-permute-start | bytes 983048 | tf_op jit(solution)/shard_map/ppermute | solution.py:182

commit v4 on v3

--- a/solution.py
+++ b/solution.py
@@ -16,6 +16,14 @@
 dot = functools.partial(lax.dot_general, preferred_element_type=jnp.float32)
 
 
+def role_of(gx, gy, gz):
+    return (gx ^ (gx >> 1) ^ gy ^ gz) & 1
+
+
+def role_here():
+    return role_of(*(lax.axis_index(axis) for axis in AXES))
+
+
 def adapter_kernel(
     parts, flip, lengths_in, rows, query_grad, value_grad, query_down, value_down, query_up, value_up,
     down_sum, up_sum, held_rows, held_grad, held_down, held_up, lengths, sems,
@@ -23,7 +31,7 @@
     tokens, width = held_rows.shape
     step = width // parts
     cuts = [pl.ds(k * step, step) for k in range(parts)]
-    query = ((lax.axis_index("gx") + flip) & 1) == 0
+    query = (role_here() ^ flip) == 0
 
     def copies(down, up, grad):
         small = [
@@ -106,14 +114,14 @@
 
 
 def finish_kernel(mine, other, total, query, value, out, sems):
-    core = lax.axis_index("gx") & 1
+    role = role_here()
     rows = mine.shape[0] // 2
     by = total[0, 0]
     copies = []
     for k in range(2):
         cut = pl.ds(k * rows, rows)
-        out[core, cut] = mine[cut] / by
-        out[1 - core, cut] = other[cut] / by
+        out[role, cut] = mine[cut] / by
+        out[1 - role, cut] = other[cut] / by
         for c, target in enumerate((query, value)):
             copies.append(pltpu.make_async_copy(out.at[c, cut], target.at[cut], sems.at[c, k]))
             copies[-1].start()
@@ -148,8 +156,6 @@
         near = axis_bits("gx", sizes["gx"], 1) + axis_bits("gy", sizes["gy"])
         far = axis_bits("gz", sizes["gz"])
         self.orders = (near + far, self.paired(near) + self.paired(far))
-        self.at = {axis: lax.axis_index(axis) for axis in AXES}
-        self.core = self.at["gx"] & 1
 
     @staticmethod
     def paired(bits):
@@ -161,19 +167,21 @@
     def count(self):
         return len(self.orders[0])
 
-    def high(self, stage, chain):
-        flags = [(self.at[axis] & bit) != 0 for axis, bit in (order[stage] for order in self.orders)]
-        return jnp.where(self.core == chain, flags[0], flags[1])
-
-    def swap(self, stage, chain, array):
+    def high(self, stage):
+        flags = [(lax.axis_index(axis) & bit) != 0 for axis, bit in (order[stage] for order in self.orders)]
+        return jnp.where(role_here() == 0, flags[0], flags[1])
+
+    def swap(self, stage, array):
         gx, gy, gz = (self.sizes[axis] for axis in AXES)
         pairs = []
         for i in range(gx):
             for j in range(gy):
                 for k in range(gz):
+                    role = role_of(i, j, k)
                     place = {"gx": i, "gy": j, "gz": k}
-                    axis, bit = self.orders[(i & 1) ^ chain][stage]
+                    axis, bit = self.orders[role][stage]
                     place[axis] ^= bit
+                    place["gx"] ^= role_of(**place) ^ role
                     there = (place["gx"] * gy + place["gy"]) * gz + place["gz"]
                     pairs.append(((i * gy + j) * gz + k, there))
         return lax.ppermute(array, AXES, pairs)
@@ -211,22 +219,22 @@
             elif widths[0] % (2 * LANES) == 0 and len(cut) < 2:
                 axis = 1
         if axis is None:
-            held = [x + swaps.swap(stage, c, x) for c, x in enumerate(held)]
+            held = [x + swaps.swap(stage, x) for x in held]
             continue
+        high = swaps.high(stage)
         for c, x in enumerate(held):
-            high = swaps.high(stage, c)
             low_half, high_half = halves(x, widths[c], axis)
             sent = jnp.where(high, low_half, high_half)
-            held[c] = jnp.where(high, high_half, low_half) + swaps.swap(stage, c, sent)
+            held[c] = jnp.where(high, high_half, low_half) + swaps.swap(stage, sent)
             if axis == 1:
                 widths[c] //= 2
         cut.append(axis)
     total = held[0][:, widths[0]:]
     held = [x[:, :width] for x, width in zip(held, widths)]
     for stage, axis in reversed(list(enumerate(cut))):
+        high = swaps.high(stage)
         for c, x in enumerate(held):
-            high = swaps.high(stage, c)
-            other = swaps.swap(stage, c, x)
+            other = swaps.swap(stage, x)
             held[c] = jnp.concatenate([jnp.where(high, other, x), jnp.where(high, x, other)], axis=axis)
     query, value = zip(*(finish(x, swaps.swap_cores(x), total) for x in held))
     return (*query, *value)

time: 48.4 us -> 42.3 us (0.87)
  waiting for transfers between devices: 17.3 us -> 14 us
  starting transfers between devices: 22.2 us -> 19.4 us
    ppermute x12, waiting for transfers between devices: 16.6 us -> 13.4 us  [swap(): return lax.ppermute(array, AXES, pairs)]
    ppermute x12, starting transfers between devices: 21.4 us -> 18.3 us  [swap(): return lax.ppermute(array, AXES, pairs)]
  transfers between devices with their start and end apart: 16 -> 16, of which waited for: 10 -> 11; matrix products, arithmetic and copies ran while one was open for 1% -> 1% of each run, Pallas kernels for 8% -> 9%
where the time goes in v4:
time: 42.3 us; the launch traced here: 42.1 us
  starting transfers between devices  19.4 us (46%)
  waiting for transfers between devices  14 us (33%)
  Pallas kernels  7.45 us (18%)
  between operations  0.8 us (2%)
  other arithmetic  0.45 us (1%)
    ppermute x12, starting transfers between devices, swap(): return lax.ppermute(array, AXES, pairs)  18.3 us
    ppermute x12, waiting for transfers between devices, swap(): return lax.ppermute(array, AXES, pairs)  13.4 us
    pallas_call x2, Pallas kernels, adapter_sums(): pl.pallas_call(functools.partial(adapter_kernel, PARTS, flip), out_shape=...  5.6 us
    pallas_call x2, Pallas kernels, finish(): pl.pallas_call(finish_kernel, out_shape=(jax.ShapeDtypeStruct(mine.shape,...  1.85 us
    ppermute x4, starting transfers between devices, swap_cores(): lax.ppermute(array, 'gx', [(i, i ^ 1) for i in range(self.sizes['gx'])])  1.07 us
  transfers between devices with their start and end apart: 16, of which 11 were waited for; matrix products, arithmetic and copies ran while one was open for 1% of the time, Pallas kernels for 9%

profile of v4, /device:TPU:0, one launch (start us, length us, event | category | flops | bytes accessed | tf_op | source)
XLA Modules:
  0.0 42.1 jit_solution(1626524399843577672)
XLA Ops:
  0.6 2.8 %adapter.3 = (f32[16,5248]{1,0:T(8,128)S(1)}, f32[16,5120]{1,0:T(8,128)S(1)}) custom-call(s32[2]{0:T(128)} %lengths_in.3, bf16[128,5120]{1,0:T(8,128)(2,1)} %rows.3, bf16[128,5120]{1,0:T(8,128)(2,1)} %query_grad.3, bf16[128,5120]{1,0:T(8,128)(2,1)} %value_grad.3, bf16[16,5120]{1,0:T(8,128)(2,1)} %query_down.3, bf16[16,5120]{1,0:T(8,128)(2,1)} %value_down.3, ...), custom_call_target="tpu_custom_call" | custom-call | flops 83886080 | bytes 2621440 | tf_op jit(solution)/shard_map/adapter/pallas_call | solution.py:99
  3.5 0.5 %collective-permute-start.8 = (f32[16,5120]{1,0:T(8,128)S(1)}, f32[16,5120]{1,0:T(8,128)S(1)}, u32[]{:S(2)}, u32[]{:S(2)}) collective-permute-start(f32[16,5120]{1,0:T(8,128)S(1)} %get-tuple-element.16), channel_id=1, source_target_pairs={{0,8},{8,0},{16,24},{24,16},{1,9},{9,1},{17,25},{25,17},{2,10},{10... | collective-permute-start | bytes 983048 | tf_op jit(solution)/shard_map/ppermute | solution.py:190
  4.0 0.1 collective-permute-start
  4.1 2.8 %adapter.2 = (f32[16,5248]{1,0:T(8,128)S(1)}, f32[16,5120]{1,0:T(8,128)S(1)}) custom-call(s32[2]{0:T(128)} %lengths_in.3, bf16[128,5120]{1,0:T(8,128)(2,1)} %rows.3, bf16[128,5120]{1,0:T(8,128)(2,1)} %query_grad.3, bf16[128,5120]{1,0:T(8,128)(2,1)} %value_grad.3, bf16[16,5120]{1,0:T(8,128)(2,1)} %query_down.3, bf16[16,5120]{1,0:T(8,128)(2,1)} %value_down.3, ...), custom_call_target="tpu_custom_call" | custom-call | flops 83886080 | bytes 2621440 | tf_op jit(solution)/shard_map/adapter/pallas_call | solution.py:99
  6.9 0.0 collective-permute-done.8
  7.0 2.7 %collective-permute-start.9 = (f32[8,5120]{1,0:T(8,128)S(1)}, f32[8,5120]{1,0:T(8,128)S(1)}, u32[]{:S(2)}, u32[]{:S(2)}) collective-permute-start(f32[8,5120]{1,0:T(8,128)S(1)} %slice_select_fusion.1), channel_id=1, source_target_pairs={{0,24},{1,13},{2,26},{3,15},{4,8},{5,29},{6,10},{7,31},{8,4},{9,17... | collective-permute-start | bytes 491528 | tf_op jit(solution)/shard_map/ppermute | solution.py:187
  9.6 0.0 collective-permute-done
  9.7 0.1 collective-permute-start.1
  9.8 2.8 %collective-permute-done.9 = f32[8,5120]{1,0:T(8,128)S(1)} collective-permute-done((f32[8,5120]{1,0:T(8,128)S(1)}, f32[8,5120]{1,0:T(8,128)S(1)}, u32[]{:S(2)}, u32[]{:S(2)}) %collective-permute-start.9) | collective-permute-done | bytes 163872 | tf_op jit(solution)/shard_map/ppermute | solution.py:187
  12.7 2.1 %collective-permute-start.10 = (f32[8,2560]{1,0:T(8,128)S(1)}, f32[8,2560]{1,0:T(8,128)S(1)}, u32[]{:S(2)}, u32[]{:S(2)}) collective-permute-start(f32[8,2560]{1,0:T(8,128)S(1)} %slice_select_fusion.3), channel_id=1, source_target_pairs={{0,12},{1,25},{2,14},{3,27},{4,28},{5,9},{6,30},{7,11},{8,16},{9,5... | collective-permute-start | bytes 245768 | tf_op jit(solution)/shard_map/ppermute | solution.py:187
  14.8 0.0 collective-permute-done.1
  14.9 1.5 %collective-permute-start.2 = (f32[8,2688]{1,0:T(8,128)S(1)}, f32[8,2688]{1,0:T(8,128)S(1)}, u32[]{:S(2)}, u32[]{:S(2)}) collective-permute-start(f32[8,2688]{1,0:T(8,128)S(1)} %slice_select_fusion.2), channel_id=1, source_target_pairs={{0,12},{1,25},{2,14},{3,27},{4,28},{5,9},{6,30},{7,11},{8,16},{9,5... | collective-permute-start | bytes 258056 | tf_op jit(solution)/shard_map/ppermute | solution.py:187
  16.4 0.5 %collective-permute-done.10 = f32[8,2560]{1,0:T(8,128)S(1)} collective-permute-done((f32[8,2560]{1,0:T(8,128)S(1)}, f32[8,2560]{1,0:T(8,128)S(1)}, u32[]{:S(2)}, u32[]{:S(2)}) %collective-permute-start.10) | collective-permute-done | bytes 81952 | tf_op jit(solution)/shard_map/ppermute | solution.py:187
  16.9 1.9 %collective-permute-start.11 = (f32[8,2560]{1,0:T(8,128)S(1)}, f32[8,2560]{1,0:T(8,128)S(1)}, u32[]{:S(2)}, u32[]{:S(2)}) collective-permute-start(f32[8,2560]{1,0:T(8,128)S(1)} %select_add_fusion.3), channel_id=1, source_target_pairs={{0,9},{1,3},{2,11},{3,1},{4,6},{5,12},{6,4},{7,14},{8,10},{9,0},{1... | collective-permute-start | bytes 245768 | tf_op jit(solution)/shard_map/ppermute | solution.py:187
  18.8 0.1 collective-permute-done.2
  18.9 1.5 %collective-permute-start.3 = (f32[8,2688]{1,0:T(8,128)S(1)}, f32[8,2688]{1,0:T(8,128)S(1)}, u32[]{:S(2)}, u32[]{:S(2)}) collective-permute-start(f32[8,2688]{1,0:T(8,128)S(1)} %select_add_fusion.2), channel_id=1, source_target_pairs={{0,9},{1,3},{2,11},{3,1},{4,6},{5,12},{6,4},{7,14},{8,10},{9,0},{1... | collective-permute-start | bytes 258056 | tf_op jit(solution)/shard_map/ppermute | solution.py:187
  20.4 0.8 %collective-permute-done.11 = f32[8,2560]{1,0:T(8,128)S(1)} collective-permute-done((f32[8,2560]{1,0:T(8,128)S(1)}, f32[8,2560]{1,0:T(8,128)S(1)}, u32[]{:S(2)}, u32[]{:S(2)}) %collective-permute-start.11) | collective-permute-done | bytes 81952 | tf_op jit(solution)/shard_map/ppermute | solution.py:187
  21.2 3.0 %collective-permute-start.12 = (f32[8,2560]{1,0:T(8,128)S(1)}, f32[8,2560]{1,0:T(8,128)S(1)}, u32[]{:S(2)}, u32[]{:S(2)}) collective-permute-start(f32[8,2560]{1,0:T(8,128)S(1)} %add.38), channel_id=1, source_target_pairs={{0,2},{1,8},{2,0},{3,10},{4,13},{5,7},{6,15},{7,5},{8,1},{9,11},{1... | collective-permute-start | bytes 245768 | tf_op jit(solution)/shard_map/ppermute | solution.py:187
  24.2 0.0 collective-permute-done.3
  24.2 1.7 %collective-permute-start.4 = (f32[8,2688]{1,0:T(8,128)S(1)}, f32[8,2688]{1,0:T(8,128)S(1)}, u32[]{:S(2)}, u32[]{:S(2)}) collective-permute-start(f32[8,2688]{1,0:T(8,128)S(1)} %add.33), channel_id=1, source_target_pairs={{0,2},{1,8},{2,0},{3,10},{4,13},{5,7},{6,15},{7,5},{8,1},{9,11},{1... | collective-permute-start | bytes 258056 | tf_op jit(solution)/shard_map/ppermute | solution.py:187
  25.9 2.1 %collective-permute-done.12 = f32[8,2560]{1,0:T(8,128)S(1)} collective-permute-done((f32[8,2560]{1,0:T(8,128)S(1)}, f32[8,2560]{1,0:T(8,128)S(1)}, u32[]{:S(2)}, u32[]{:S(2)}) %collective-permute-start.12) | collective-permute-done | bytes 81952 | tf_op jit(solution)/shard_map/ppermute | solution.py:187
  28.1 0.9 %collective-permute-start.13 = (f32[8,2560]{1,0:T(8,128)S(1)}, f32[8,2560]{1,0:T(8,128)S(1)}, u32[]{:S(2)}, u32[]{:S(2)}) collective-permute-start(f32[8,2560]{1,0:T(8,128)S(1)} %add.39), channel_id=1, source_target_pairs={{0,12},{1,25},{2,14},{3,27},{4,28},{5,9},{6,30},{7,11},{8,16},{9,5... | collective-permute-start | bytes 245768 | tf_op jit(solution)/shard_map/ppermute | solution.py:187
  29.0 1.6 %collective-permute-done.4 = f32[8,2688]{1,0:T(8,128)S(1)} collective-permute-done((f32[8,2688]{1,0:T(8,128)S(1)}, f32[8,2688]{1,0:T(8,128)S(1)}, u32[]{:S(2)}, u32[]{:S(2)}) %collective-permute-start.4) | collective-permute-done | bytes 86048 | tf_op jit(solution)/shard_map/ppermute | solution.py:187
  30.6 0.1 collective-permute-start.5
  30.7 1.3 %collective-permute-done.13 = f32[8,2560]{1,0:T(8,128)S(1)} collective-permute-done((f32[8,2560]{1,0:T(8,128)S(1)}, f32[8,2560]{1,0:T(8,128)S(1)}, u32[]{:S(2)}, u32[]{:S(2)}) %collective-permute-start.13) | collective-permute-done | bytes 81952 | tf_op jit(solution)/shard_map/ppermute | solution.py:187
  32.1 1.5 %collective-permute-start.14 = (f32[8,5120]{1,0:T(8,128)S(1)}, f32[8,5120]{1,0:T(8,128)S(1)}, u32[]{:S(2)}, u32[]{:S(2)}) collective-permute-start(f32[8,5120]{1,0:T(8,128)S(1)} %pad_maximum_fusion.3), channel_id=1, source_target_pairs={{0,24},{1,13},{2,26},{3,15},{4,8},{5,29},{6,10},{7,31},{8,4},{9,17... | collective-permute-start | bytes 491528 | tf_op jit(solution)/shard_map/ppermute | solution.py:187
  33.5 1.0 %collective-permute-done.5 = f32[8,2560]{1,0:T(8,128)S(1)} collective-permute-done((f32[8,2560]{1,0:T(8,128)S(1)}, f32[8,2560]{1,0:T(8,128)S(1)}, u32[]{:S(2)}, u32[]{:S(2)}) %collective-permute-start.5) | collective-permute-done | bytes 81952 | tf_op jit(solution)/shard_map/ppermute | solution.py:187
  34.6 1.4 %collective-permute-start.6 = (f32[8,5120]{1,0:T(8,128)S(1)}, f32[8,5120]{1,0:T(8,128)S(1)}, u32[]{:S(2)}, u32[]{:S(2)}) collective-permute-start(f32[8,5120]{1,0:T(8,128)S(1)} %pad_maximum_fusion.2), channel_id=1, source_target_pairs={{0,24},{1,13},{2,26},{3,15},{4,8},{5,29},{6,10},{7,31},{8,4},{9,17... | collective-permute-start | bytes 491528 | tf_op jit(solution)/shard_map/ppermute | solution.py:187
  36.0 0.9 %collective-permute-done.14 = f32[8,5120]{1,0:T(8,128)S(1)} collective-permute-done((f32[8,5120]{1,0:T(8,128)S(1)}, f32[8,5120]{1,0:T(8,128)S(1)}, u32[]{:S(2)}, u32[]{:S(2)}) %collective-permute-start.14) | collective-permute-done | bytes 163872 | tf_op jit(solution)/shard_map/ppermute | solution.py:187
  36.9 0.3 collective-permute-start.15
  37.2 2.2 %collective-permute-done.6 = f32[8,5120]{1,0:T(8,128)S(1)} collective-permute-done((f32[8,5120]{1,0:T(8,128)S(1)}, f32[8,5120]{1,0:T(8,128)S(1)}, u32[]{:S(2)}, u32[]{:S(2)}) %collective-permute-start.6) | collective-permute-done | bytes 163872 | tf_op jit(solution)/shard_map/ppermute | solution.py:187
  39.5 0.2 collective-permute-start.7
  39.7 0.0 collective-permute-done.15.other
  39.7 0.9 %finish.3 = (f32[16,5120]{1,0:T(8,128)}, f32[16,5120]{1,0:T(8,128)}) custom-call(f32[16,5120]{1,0:T(8,128)S(1)} %pad_maximum_fusion.1.mine, f32[16,5120]{1,0:T(8,128)S(1)} %collective-permute-done.15.other, f32[8,128]{1,0:T(8,128)S(1)} %slice.47.total), custom_call_target="tpu_custom_call" | custom-call | flops 163840 | bytes 1310720 | tf_op jit(solution)/shard_map/finish/pallas_call | solution.py:135
  40.6 0.6 %collective-permute-done.7.other = f32[16,5120]{1,0:T(8,128)S(1)} collective-permute-done((f32[16,5120]{1,0:T(8,128)S(1)}, f32[16,5120]{1,0:T(8,128)S(1)}, u32[]{:S(2)}, u32[]{:S(2)}) %collective-permute-start.7) | collective-permute-done | bytes 327712 | tf_op jit(solution)/shard_map/ppermute | solution.py:190
  41.2 0.9 %finish.2 = (f32[16,5120]{1,0:T(8,128)}, f32[16,5120]{1,0:T(8,128)}) custom-call(f32[16,5120]{1,0:T(8,128)S(1)} %pad_maximum_fusion.mine, f32[16,5120]{1,0:T(8,128)S(1)} %collective-permute-done.7.other, f32[8,128]{1,0:T(8,128)S(1)} %slice.47.total), custom_call_target="tpu_custom_call" | custom-call | flops 163840 | bytes 1310720 | tf_op jit(solution)/shard_map/finish/pallas_call | solution.py:135
  (26 shorter events, 0.5 us)
Async XLA Ops:
  3.5 3.4 %collective-permute-start.8 = (f32[16,5120]{1,0:T(8,128)S(1)}, f32[16,5120]{1,0:T(8,128)S(1)}, u32[]{:S(2)}, u32[]{:S(2)}) collective-permute-start(f32[16,5120]{1,0:T(8,128)S(1)} %get-tuple-element.16), channel_id=1, source_target_pairs={{0,8},{8,0},{16,24},{24,16},{1,9},{9,1},{17,25},{25,17},{2,10},{10... | collective-permute-start | bytes 983048 | tf_op jit(solution)/shard_map/ppermute | solution.py:190
  4.0 5.6 %collective-permute-start = (f32[16,5248]{1,0:T(8,128)S(1)}, f32[16,5248]{1,0:T(8,128)S(1)}, u32[]{:S(2)}, u32[]{:S(2)}) collective-permute-start(f32[16,5248]{1,0:T(8,128)S(1)} %get-tuple-element.13), channel_id=1, source_target_pairs={{0,8},{8,0},{16,24},{24,16},{1,9},{9,1},{17,25},{25,17},{2,10},{10... | collective-permute-start | bytes 1007624 | tf_op jit(solution)/shard_map/ppermute | solution.py:190
  7.0 5.7 %collective-permute-start.9 = (f32[8,5120]{1,0:T(8,128)S(1)}, f32[8,5120]{1,0:T(8,128)S(1)}, u32[]{:S(2)}, u32[]{:S(2)}) collective-permute-start(f32[8,5120]{1,0:T(8,128)S(1)} %slice_select_fusion.1), channel_id=1, source_target_pairs={{0,24},{1,13},{2,26},{3,15},{4,8},{5,29},{6,10},{7,31},{8,4},{9,17... | collective-permute-start | bytes 491528 | tf_op jit(solution)/shard_map/ppermute | solution.py:187
  9.7 5.1 %collective-permute-start.1 = (f32[8,5248]{1,0:T(8,128)S(1)}, f32[8,5248]{1,0:T(8,128)S(1)}, u32[]{:S(2)}, u32[]{:S(2)}) collective-permute-start(f32[8,5248]{1,0:T(8,128)S(1)} %slice_select_fusion), channel_id=1, source_target_pairs={{0,24},{1,13},{2,26},{3,15},{4,8},{5,29},{6,10},{7,31},{8,4},{9,17... | collective-permute-start | bytes 503816 | tf_op jit(solution)/shard_map/ppermute | solution.py:187
  12.7 4.3 %collective-permute-start.10 = (f32[8,2560]{1,0:T(8,128)S(1)}, f32[8,2560]{1,0:T(8,128)S(1)}, u32[]{:S(2)}, u32[]{:S(2)}) collective-permute-start(f32[8,2560]{1,0:T(8,128)S(1)} %slice_select_fusion.3), channel_id=1, source_target_pairs={{0,12},{1,25},{2,14},{3,27},{4,28},{5,9},{6,30},{7,11},{8,16},{9,5... | collective-permute-start | bytes 245768 | tf_op jit(solution)/shard_map/ppermute | solution.py:187
  14.9 4.0 %collective-permute-start.2 = (f32[8,2688]{1,0:T(8,128)S(1)}, f32[8,2688]{1,0:T(8,128)S(1)}, u32[]{:S(2)}, u32[]{:S(2)}) collective-permute-start(f32[8,2688]{1,0:T(8,128)S(1)} %slice_select_fusion.2), channel_id=1, source_target_pairs={{0,12},{1,25},{2,14},{3,27},{4,28},{5,9},{6,30},{7,11},{8,16},{9,5... | collective-permute-start | bytes 258056 | tf_op jit(solution)/shard_map/ppermute | solution.py:187
  16.9 4.2 %collective-permute-start.11 = (f32[8,2560]{1,0:T(8,128)S(1)}, f32[8,2560]{1,0:T(8,128)S(1)}, u32[]{:S(2)}, u32[]{:S(2)}) collective-permute-start(f32[8,2560]{1,0:T(8,128)S(1)} %select_add_fusion.3), channel_id=1, source_target_pairs={{0,9},{1,3},{2,11},{3,1},{4,6},{5,12},{6,4},{7,14},{8,10},{9,0},{1... | collective-permute-start | bytes 245768 | tf_op jit(solution)/shard_map/ppermute | solution.py:187
  18.9 5.3 %collective-permute-start.3 = (f32[8,2688]{1,0:T(8,128)S(1)}, f32[8,2688]{1,0:T(8,128)S(1)}, u32[]{:S(2)}, u32[]{:S(2)}) collective-permute-start(f32[8,2688]{1,0:T(8,128)S(1)} %select_add_fusion.2), channel_id=1, source_target_pairs={{0,9},{1,3},{2,11},{3,1},{4,6},{5,12},{6,4},{7,14},{8,10},{9,0},{1... | collective-permute-start | bytes 258056 | tf_op jit(solution)/shard_map/ppermute | solution.py:187
  21.2 6.9 %collective-permute-start.12 = (f32[8,2560]{1,0:T(8,128)S(1)}, f32[8,2560]{1,0:T(8,128)S(1)}, u32[]{:S(2)}, u32[]{:S(2)}) collective-permute-start(f32[8,2560]{1,0:T(8,128)S(1)} %add.38), channel_id=1, source_target_pairs={{0,2},{1,8},{2,0},{3,10},{4,13},{5,7},{6,15},{7,5},{8,1},{9,11},{1... | collective-permute-start | bytes 245768 | tf_op jit(solution)/shard_map/ppermute | solution.py:187
  24.2 6.4 %collective-permute-start.4 = (f32[8,2688]{1,0:T(8,128)S(1)}, f32[8,2688]{1,0:T(8,128)S(1)}, u32[]{:S(2)}, u32[]{:S(2)}) collective-permute-start(f32[8,2688]{1,0:T(8,128)S(1)} %add.33), channel_id=1, source_target_pairs={{0,2},{1,8},{2,0},{3,10},{4,13},{5,7},{6,15},{7,5},{8,1},{9,11},{1... | collective-permute-start | bytes 258056 | tf_op jit(solution)/shard_map/ppermute | solution.py:187
  28.1 3.9 %collective-permute-start.13 = (f32[8,2560]{1,0:T(8,128)S(1)}, f32[8,2560]{1,0:T(8,128)S(1)}, u32[]{:S(2)}, u32[]{:S(2)}) collective-permute-start(f32[8,2560]{1,0:T(8,128)S(1)} %add.39), channel_id=1, source_target_pairs={{0,12},{1,25},{2,14},{3,27},{4,28},{5,9},{6,30},{7,11},{8,16},{9,5... | collective-permute-start | bytes 245768 | tf_op jit(solution)/shard_map/ppermute | solution.py:187
  30.6 3.9 %collective-permute-start.5 = (f32[8,2560]{1,0:T(8,128)S(1)}, f32[8,2560]{1,0:T(8,128)S(1)}, u32[]{:S(2)}, u32[]{:S(2)}) collective-permute-start(f32[8,2560]{1,0:T(8,128)S(1)} %slice.46), channel_id=1, source_target_pairs={{0,12},{1,25},{2,14},{3,27},{4,28},{5,9},{6,30},{7,11},{8,16},{9,5... | collective-permute-start | bytes 245768 | tf_op jit(solution)/shard_map/ppermute | solution.py:187
  32.1 4.8 %collective-permute-start.14 = (f32[8,5120]{1,0:T(8,128)S(1)}, f32[8,5120]{1,0:T(8,128)S(1)}, u32[]{:S(2)}, u32[]{:S(2)}) collective-permute-start(f32[8,5120]{1,0:T(8,128)S(1)} %pad_maximum_fusion.3), channel_id=1, source_target_pairs={{0,24},{1,13},{2,26},{3,15},{4,8},{5,29},{6,10},{7,31},{8,4},{9,17... | collective-permute-start | bytes 491528 | tf_op jit(solution)/shard_map/ppermute | solution.py:187
  34.6 4.8 %collective-permute-start.6 = (f32[8,5120]{1,0:T(8,128)S(1)}, f32[8,5120]{1,0:T(8,128)S(1)}, u32[]{:S(2)}, u32[]{:S(2)}) collective-permute-start(f32[8,5120]{1,0:T(8,128)S(1)} %pad_maximum_fusion.2), channel_id=1, source_target_pairs={{0,24},{1,13},{2,26},{3,15},{4,8},{5,29},{6,10},{7,31},{8,4},{9,17... | collective-permute-start | bytes 491528 | tf_op jit(solution)/shard_map/ppermute | solution.py:187
  36.9 2.7 %collective-permute-start.15 = (f32[16,5120]{1,0:T(8,128)S(1)}, f32[16,5120]{1,0:T(8,128)S(1)}, u32[]{:S(2)}, u32[]{:S(2)}) collective-permute-start(f32[16,5120]{1,0:T(8,128)S(1)} %pad_maximum_fusion.1.mine), channel_id=1, source_target_pairs={{0,8},{8,0},{16,24},{24,16},{1,9},{9,1},{17,25},{25,17},{2,10},{10... | collective-permute-start | bytes 983048 | tf_op jit(solution)/shard_map/ppermute | solution.py:190
  39.5 1.7 %collective-permute-start.7 = (f32[16,5120]{1,0:T(8,128)S(1)}, f32[16,5120]{1,0:T(8,128)S(1)}, u32[]{:S(2)}, u32[]{:S(2)}) collective-permute-start(f32[16,5120]{1,0:T(8,128)S(1)} %pad_maximum_fusion.mine), channel_id=1, source_target_pairs={{0,8},{8,0},{16,24},{24,16},{1,9},{9,1},{17,25},{25,17},{2,10},{10... | collective-permute-start | bytes 983048 | tf_op jit(solution)/shard_map/ppermute | solution.py:190

commit v5 on v4

--- a/solution.py
+++ b/solution.py
@@ -24,55 +24,21 @@
     return role_of(*(lax.axis_index(axis) for axis in AXES))
 
 
-def adapter_kernel(
-    parts, flip, lengths_in, rows, query_grad, value_grad, query_down, value_down, query_up, value_up,
-    down_sum, up_sum, held_rows, held_grad, held_down, held_up, lengths, sems,
-):
-    tokens, width = held_rows.shape
-    step = width // parts
-    cuts = [pl.ds(k * step, step) for k in range(parts)]
-    query = (role_here() ^ flip) == 0
-
-    def copies(down, up, grad):
-        small = [
-            pltpu.make_async_copy(down, held_down, sems.at[0, parts]),
-            pltpu.make_async_copy(up, held_up, sems.at[1, parts]),
-            pltpu.make_async_copy(lengths_in, lengths, sems.at[0, parts + 1]),
-        ]
-        large = [
-            (
-                pltpu.make_async_copy(rows.at[:, cut], held_rows.at[:, cut], sems.at[0, k]),
-                pltpu.make_async_copy(grad.at[:, cut], held_grad.at[:, cut], sems.at[1, k]),
-            )
-            for k, cut in enumerate(cuts)
-        ]
-        return small, large
-
-    def start(*which):
-        small, large = copies(*which)
-        for copy in small:
-            copy.start()
-        for pair in large:
-            for copy in pair:
-                copy.start()
-
-    @pl.when(query)
-    def _():
-        start(query_down, query_up, query_grad)
-
-    @pl.when(jnp.logical_not(query))
-    def _():
-        start(value_down, value_up, value_grad)
-
-    small, large = copies(query_down, query_up, query_grad)
-    for copy in small:
-        copy.wait()
+def store_sums(lengths, rows, grad, down, up, down_sum, up_sum, arrive, rows_held):
+    tokens, width = rows.shape
+    step = width // PARTS
+    cuts = [pl.ds(k * step, step) for k in range(PARTS)]
     inner = back = 0.0
-    for cut, pair in zip(cuts, large):
-        for copy in pair:
-            copy.wait()
-        inner = inner + dot(held_down[:, cut], held_rows[:, cut], NT)
-        back = back + dot(held_up[:, cut], held_grad[:, cut], NT)
+    order = [("rows", k) for k in range(PARTS)] + [("grad", k) for k in range(PARTS)]
+    if not rows_held:
+        order.sort(key=lambda item: item[1])
+    for name, k in order:
+        arrive(name, k)
+        if name == "rows":
+            inner = inner + dot(down[:, cuts[k]], rows[:, cuts[k]], NT)
+        else:
+            back = back + dot(up[:, cuts[k]], grad[:, cuts[k]], NT)
+    arrive("lengths", 0)
     seqs = lengths.shape[0]
     seq_len = tokens // seqs
     token = lax.broadcasted_iota(jnp.int32, inner.shape, 1)
@@ -85,32 +51,108 @@
     inner = jnp.where(valid, inner, 0.0).astype(jnp.bfloat16)
     back = jnp.where(valid, back, 0.0).astype(jnp.bfloat16)
     for cut in cuts:
-        down_sum[:, cut] = dot(back, held_rows[:, cut], NN)
-        up_sum[:, cut] = dot(inner, held_grad[:, cut], NN)
+        down_sum[:, cut] = dot(back, rows[:, cut], NN)
+        up_sum[:, cut] = dot(inner, grad[:, cut], NN)
     down_sum[:, width:] = jnp.full((down_sum.shape[0], LANES), count.astype(jnp.float32), jnp.float32)
 
 
-def adapter_sums(flip, lengths, rows, *rest):
+def load_and_sum(flip, lengths_in, rows_in, queries, values, rows, held, lengths, down_sum, up_sum, sems):
+    held_grad, held_down, held_up = held
+    step = rows.shape[1] // PARTS
+
+    def copies(which):
+        grad, down, up = which
+        plan = {
+            ("maps", 0): pltpu.make_async_copy(down, held_down, sems.at[0, PARTS]),
+            ("maps", 1): pltpu.make_async_copy(up, held_up, sems.at[1, PARTS]),
+            ("lengths", 0): pltpu.make_async_copy(lengths_in, lengths, sems.at[0, PARTS + 1]),
+        }
+        for k in range(PARTS):
+            cut = pl.ds(k * step, step)
+            if rows_in is not None:
+                plan["rows", k] = pltpu.make_async_copy(rows_in.at[:, cut], rows.at[:, cut], sems.at[0, k])
+            plan["grad", k] = pltpu.make_async_copy(grad.at[:, cut], held_grad.at[:, cut], sems.at[1, k])
+        return plan
+
+    def start(which):
+        for copy in copies(which).values():
+            copy.start()
+
+    query = (role_here() ^ flip) == 0
+    pl.when(query)(lambda: start(queries))
+    pl.when(jnp.logical_not(query))(lambda: start(values))
+    plan = copies(queries)
+
+    def arrive(*key):
+        if key == ("rows", 0):
+            plan["maps", 0].wait()
+        if key == ("grad", 0):
+            plan["maps", 1].wait()
+        if key in plan:
+            plan[key].wait()
+
+    store_sums(lengths, rows, held_grad, held_down, held_up, down_sum, up_sum, arrive, rows_in is None)
+
+
+def sent_kernel(
+    lengths_in, rows_in, query_grad, value_grad, query_down, value_down, query_up, value_up,
+    down_sum, up_sum, rows, held_grad, held_down, held_up, lengths, sems,
+):
+    queries, values = (query_grad, query_down, query_up), (value_grad, value_down, value_up)
+    held = (held_grad, held_down, held_up)
+    load_and_sum(1, lengths_in, rows_in, queries, values, rows, held, lengths, down_sum, up_sum, sems)
+
+
+def kept_kernel(
+    lengths_in, rows, query_grad, value_grad, query_down, value_down, query_up, value_up,
+    down_sum, up_sum, held_grad, held_down, held_up, lengths, sems,
+):
+    queries, values = (query_grad, query_down, query_up), (value_grad, value_down, value_up)
+    held = (held_grad, held_down, held_up)
+    load_and_sum(0, lengths_in, None, queries, values, rows, held, lengths, down_sum, up_sum, sems)
+
+
+def adapter_sums(lengths, rows, *rest):
     tokens, width = rows.shape
     rank = rest[-1].shape[0]
     wide = pltpu.VMEM((tokens, width), rows.dtype)
     thin = pltpu.VMEM((rank, width), rows.dtype)
-    args = [pltpu.with_memory_space_constraint(x, pltpu.HBM) for x in (lengths, rows, *rest)]
-    return pl.pallas_call(
-        functools.partial(adapter_kernel, PARTS, flip),
-        out_shape=(pltpu.VMEM((rank, width + LANES), jnp.float32), pltpu.VMEM((rank, width), jnp.float32)),
-        in_specs=[pl.BlockSpec(memory_space=pltpu.HBM)] * len(args),
-        out_specs=(pl.BlockSpec(memory_space=pltpu.VMEM),) * 2,
+    sums = (pltpu.VMEM((rank, width + LANES), jnp.float32), pltpu.VMEM((rank, width), jnp.float32))
+    far, near = (pl.BlockSpec(memory_space=space) for space in (pltpu.HBM, pltpu.VMEM))
+    common = dict(
         scratch_shapes=[
-            wide, wide, thin, thin, pltpu.SMEM(lengths.shape, lengths.dtype),
-            pltpu.SemaphoreType.DMA((2, PARTS + 2)),
+            wide, thin, thin, pltpu.SMEM(lengths.shape, lengths.dtype), pltpu.SemaphoreType.DMA((2, PARTS + 2))
         ],
         compiler_params=pltpu.CompilerParams(vmem_limit_bytes=16 << 20),
         cost_estimate=pl.CostEstimate(
             flops=8 * rank * tokens * width, bytes_accessed=4 * tokens * width, transcendentals=0
         ),
-        name="adapter",
-    )(*args)
+    )
+
+    def put(space, *arrays):
+        return [pltpu.with_memory_space_constraint(x, space) for x in arrays]
+
+    first, *others = put(pltpu.HBM, lengths, *rest)
+    *sent, held = pl.pallas_call(
+        sent_kernel,
+        out_shape=(*sums, wide),
+        in_specs=[far] * (2 + len(others)),
+        out_specs=(near,) * 3,
+        name="sent",
+        **common,
+    )(first, *put(pltpu.HBM, rows), *others)
+
+    def kept():
+        return pl.pallas_call(
+            kept_kernel,
+            out_shape=sums,
+            in_specs=[far, near] + [far] * len(others),
+            out_specs=(near,) * 2,
+            name="kept",
+            **common,
+        )(first, *put(pltpu.VMEM, held), *others)
+
+    return sent, kept
 
 
 def finish_kernel(mine, other, total, query, value, out, sems):
@@ -206,10 +248,9 @@
     args = (lengths, hidden_rows, query_grad, value_grad, query_down, value_down, query_up, value_up)
     swaps = Swaps(sizes)
     widths = [hidden_rows.shape[1]] * 2
-    sent = adapter_sums(1, *args)
+    sent, kept = adapter_sums(*args)
     got = [swaps.swap_cores(x) for x in sent]
-    kept = adapter_sums(0, *args)
-    held = [x + y for x, y in zip(kept, got)]
+    held = [x + y for x, y in zip(kept(), got)]
     cut = []
     for stage in range(swaps.count()):
         axis = None

time: 42.3 us -> 43.3 us (1.024)
  Pallas kernels: 7.45 us -> 8.48 us
    pallas_call x2, Pallas kernels: 5.6 us -> 6.63 us  [the longest x1 3.53 us: adapter_sums(): pl.pallas_call(sent_kernel, out_shape=(*sums, wide), in_specs=[far] * (2...]
where the time goes in v5:
time: 43.3 us; the launch traced here: 43.1 us
  starting transfers between devices  19.4 us (45%)
  waiting for transfers between devices  14 us (32%)
  Pallas kernels  8.48 us (20%)
  between operations  0.8 us (2%)
  other arithmetic  0.45 us (1%)
    ppermute x12, starting transfers between devices, swap(): return lax.ppermute(array, AXES, pairs)  18.3 us
    ppermute x12, waiting for transfers between devices, swap(): return lax.ppermute(array, AXES, pairs)  13.4 us
    pallas_call x1, Pallas kernels, adapter_sums(): pl.pallas_call(sent_kernel, out_shape=(*sums, wide), in_specs=[far] * (2...  3.53 us
    pallas_call x1, Pallas kernels, kept(): pl.pallas_call(kept_kernel, out_shape=sums, in_specs=[far, near] + [far]...  3.1 us
    pallas_call x2, Pallas kernels, finish(): pl.pallas_call(finish_kernel, out_shape=(jax.ShapeDtypeStruct(mine.shape,...  1.85 us
    ppermute x4, starting transfers between devices, swap_cores(): lax.ppermute(array, 'gx', [(i, i ^ 1) for i in range(self.sizes['gx'])])  1.07 us
  transfers between devices with their start and end apart: 16, of which 11 were waited for; matrix products, arithmetic and copies ran while one was open for 1% of the time, Pallas kernels for 9%

profile of v5, /device:TPU:0, one launch (start us, length us, event | category | flops | bytes accessed | tf_op | source)
XLA Modules:
  0.0 43.1 jit_solution(11717338635307918804)
XLA Ops:
  0.6 3.5 %sent.1 = (f32[16,5248]{1,0:T(8,128)S(1)}, f32[16,5120]{1,0:T(8,128)S(1)}, bf16[128,5120]{1,0:T(8,128)(2,1)S(1)}) custom-call(s32[2]{0:T(128)} %lengths_in.3, bf16[128,5120]{1,0:T(8,128)(2,1)} %rows_in.1, bf16[128,5120]{1,0:T(8,128)(2,1)} %query_grad.3, bf16[128,5120]{1,0:T(8,128)(2,1)} %value_grad.3, bf16[16,5120]{1,0:T(8,128)(2,1)} %query_down.3, ...), custom_call_target="tpu_custom_call" | custom-call | flops 83886080 | bytes 2621440 | tf_op jit(solution)/shard_map/sent/pallas_call | solution.py:136
  4.2 0.5 %collective-permute-start.8 = (f32[16,5120]{1,0:T(8,128)S(1)}, f32[16,5120]{1,0:T(8,128)S(1)}, u32[]{:S(2)}, u32[]{:S(2)}) collective-permute-start(f32[16,5120]{1,0:T(8,128)S(1)} %get-tuple-element.18), channel_id=1, source_target_pairs={{0,8},{8,0},{16,24},{24,16},{1,9},{9,1},{17,25},{25,17},{2,10},{10... | collective-permute-start | bytes 983048 | tf_op jit(solution)/shard_map/ppermute | solution.py:232
  4.7 0.1 collective-permute-start
  4.8 3.1 %kept.1 = (f32[16,5248]{1,0:T(8,128)S(1)}, f32[16,5120]{1,0:T(8,128)S(1)}) custom-call(s32[2]{0:T(128)} %lengths_in.3, bf16[128,5120]{1,0:T(8,128)(2,1)S(1)} %get-tuple-element.13.rows, bf16[128,5120]{1,0:T(8,128)(2,1)} %query_grad.3, bf16[128,5120]{1,0:T(8,128)(2,1)} %value_grad.3, bf16[16,5120]{1,0:T(8,128)(2,1)} %query_down.3, ...), custom_call_target="tpu_custom_call" | custom-call | flops 83886080 | bytes 2621440 | tf_op jit(solution)/shard_map/kept/pallas_call | solution.py:146
  7.9 0.0 collective-permute-done.8
  8.0 2.7 %collective-permute-start.9 = (f32[8,5120]{1,0:T(8,128)S(1)}, f32[8,5120]{1,0:T(8,128)S(1)}, u32[]{:S(2)}, u32[]{:S(2)}) collective-permute-start(f32[8,5120]{1,0:T(8,128)S(1)} %slice_select_fusion.1), channel_id=1, source_target_pairs={{0,24},{1,13},{2,26},{3,15},{4,8},{5,29},{6,10},{7,31},{8,4},{9,17... | collective-permute-start | bytes 491528 | tf_op jit(solution)/shard_map/ppermute | solution.py:229
  10.6 0.0 collective-permute-done
  10.7 0.1 collective-permute-start.1
  10.8 2.8 %collective-permute-done.9 = f32[8,5120]{1,0:T(8,128)S(1)} collective-permute-done((f32[8,5120]{1,0:T(8,128)S(1)}, f32[8,5120]{1,0:T(8,128)S(1)}, u32[]{:S(2)}, u32[]{:S(2)}) %collective-permute-start.9) | collective-permute-done | bytes 163872 | tf_op jit(solution)/shard_map/ppermute | solution.py:229
  13.7 2.1 %collective-permute-start.10 = (f32[8,2560]{1,0:T(8,128)S(1)}, f32[8,2560]{1,0:T(8,128)S(1)}, u32[]{:S(2)}, u32[]{:S(2)}) collective-permute-start(f32[8,2560]{1,0:T(8,128)S(1)} %slice_select_fusion.3), channel_id=1, source_target_pairs={{0,12},{1,25},{2,14},{3,27},{4,28},{5,9},{6,30},{7,11},{8,16},{9,5... | collective-permute-start | bytes 245768 | tf_op jit(solution)/shard_map/ppermute | solution.py:229
  15.8 0.0 collective-permute-done.1
  15.9 1.5 %collective-permute-start.2 = (f32[8,2688]{1,0:T(8,128)S(1)}, f32[8,2688]{1,0:T(8,128)S(1)}, u32[]{:S(2)}, u32[]{:S(2)}) collective-permute-start(f32[8,2688]{1,0:T(8,128)S(1)} %slice_select_fusion.2), channel_id=1, source_target_pairs={{0,12},{1,25},{2,14},{3,27},{4,28},{5,9},{6,30},{7,11},{8,16},{9,5... | collective-permute-start | bytes 258056 | tf_op jit(solution)/shard_map/ppermute | solution.py:229
  17.4 0.5 %collective-permute-done.10 = f32[8,2560]{1,0:T(8,128)S(1)} collective-permute-done((f32[8,2560]{1,0:T(8,128)S(1)}, f32[8,2560]{1,0:T(8,128)S(1)}, u32[]{:S(2)}, u32[]{:S(2)}) %collective-permute-start.10) | collective-permute-done | bytes 81952 | tf_op jit(solution)/shard_map/ppermute | solution.py:229
  18.0 1.9 %collective-permute-start.11 = (f32[8,2560]{1,0:T(8,128)S(1)}, f32[8,2560]{1,0:T(8,128)S(1)}, u32[]{:S(2)}, u32[]{:S(2)}) collective-permute-start(f32[8,2560]{1,0:T(8,128)S(1)} %select_add_fusion.3), channel_id=1, source_target_pairs={{0,9},{1,3},{2,11},{3,1},{4,6},{5,12},{6,4},{7,14},{8,10},{9,0},{1... | collective-permute-start | bytes 245768 | tf_op jit(solution)/shard_map/ppermute | solution.py:229
  19.8 0.1 collective-permute-done.2
  19.9 1.5 %collective-permute-start.3 = (f32[8,2688]{1,0:T(8,128)S(1)}, f32[8,2688]{1,0:T(8,128)S(1)}, u32[]{:S(2)}, u32[]{:S(2)}) collective-permute-start(f32[8,2688]{1,0:T(8,128)S(1)} %select_add_fusion.2), channel_id=1, source_target_pairs={{0,9},{1,3},{2,11},{3,1},{4,6},{5,12},{6,4},{7,14},{8,10},{9,0},{1... | collective-permute-start | bytes 258056 | tf_op jit(solution)/shard_map/ppermute | solution.py:229
  21.5 0.8 %collective-permute-done.11 = f32[8,2560]{1,0:T(8,128)S(1)} collective-permute-done((f32[8,2560]{1,0:T(8,128)S(1)}, f32[8,2560]{1,0:T(8,128)S(1)}, u32[]{:S(2)}, u32[]{:S(2)}) %collective-permute-start.11) | collective-permute-done | bytes 81952 | tf_op jit(solution)/shard_map/ppermute | solution.py:229
  22.2 3.0 %collective-permute-start.12 = (f32[8,2560]{1,0:T(8,128)S(1)}, f32[8,2560]{1,0:T(8,128)S(1)}, u32[]{:S(2)}, u32[]{:S(2)}) collective-permute-start(f32[8,2560]{1,0:T(8,128)S(1)} %add.38), channel_id=1, source_target_pairs={{0,2},{1,8},{2,0},{3,10},{4,13},{5,7},{6,15},{7,5},{8,1},{9,11},{1... | collective-permute-start | bytes 245768 | tf_op jit(solution)/shard_map/ppermute | solution.py:229
  25.2 0.0 collective-permute-done.3
  25.3 1.7 %collective-permute-start.4 = (f32[8,2688]{1,0:T(8,128)S(1)}, f32[8,2688]{1,0:T(8,128)S(1)}, u32[]{:S(2)}, u32[]{:S(2)}) collective-permute-start(f32[8,2688]{1,0:T(8,128)S(1)} %add.33), channel_id=1, source_target_pairs={{0,2},{1,8},{2,0},{3,10},{4,13},{5,7},{6,15},{7,5},{8,1},{9,11},{1... | collective-permute-start | bytes 258056 | tf_op jit(solution)/shard_map/ppermute | solution.py:229
  27.0 2.1 %collective-permute-done.12 = f32[8,2560]{1,0:T(8,128)S(1)} collective-permute-done((f32[8,2560]{1,0:T(8,128)S(1)}, f32[8,2560]{1,0:T(8,128)S(1)}, u32[]{:S(2)}, u32[]{:S(2)}) %collective-permute-start.12) | collective-permute-done | bytes 81952 | tf_op jit(solution)/shard_map/ppermute | solution.py:229
  29.1 0.9 %collective-permute-start.13 = (f32[8,2560]{1,0:T(8,128)S(1)}, f32[8,2560]{1,0:T(8,128)S(1)}, u32[]{:S(2)}, u32[]{:S(2)}) collective-permute-start(f32[8,2560]{1,0:T(8,128)S(1)} %add.39), channel_id=1, source_target_pairs={{0,12},{1,25},{2,14},{3,27},{4,28},{5,9},{6,30},{7,11},{8,16},{9,5... | collective-permute-start | bytes 245768 | tf_op jit(solution)/shard_map/ppermute | solution.py:229
  30.0 1.6 %collective-permute-done.4 = f32[8,2688]{1,0:T(8,128)S(1)} collective-permute-done((f32[8,2688]{1,0:T(8,128)S(1)}, f32[8,2688]{1,0:T(8,128)S(1)}, u32[]{:S(2)}, u32[]{:S(2)}) %collective-permute-start.4) | collective-permute-done | bytes 86048 | tf_op jit(solution)/shard_map/ppermute | solution.py:229
  31.7 0.1 collective-permute-start.5
  31.7 1.3 %collective-permute-done.13 = f32[8,2560]{1,0:T(8,128)S(1)} collective-permute-done((f32[8,2560]{1,0:T(8,128)S(1)}, f32[8,2560]{1,0:T(8,128)S(1)}, u32[]{:S(2)}, u32[]{:S(2)}) %collective-permute-start.13) | collective-permute-done | bytes 81952 | tf_op jit(solution)/shard_map/ppermute | solution.py:229
  33.1 1.5 %collective-permute-start.14 = (f32[8,5120]{1,0:T(8,128)S(1)}, f32[8,5120]{1,0:T(8,128)S(1)}, u32[]{:S(2)}, u32[]{:S(2)}) collective-permute-start(f32[8,5120]{1,0:T(8,128)S(1)} %pad_maximum_fusion.3), channel_id=1, source_target_pairs={{0,24},{1,13},{2,26},{3,15},{4,8},{5,29},{6,10},{7,31},{8,4},{9,17... | collective-permute-start | bytes 491528 | tf_op jit(solution)/shard_map/ppermute | solution.py:229
  34.6 1.0 %collective-permute-done.5 = f32[8,2560]{1,0:T(8,128)S(1)} collective-permute-done((f32[8,2560]{1,0:T(8,128)S(1)}, f32[8,2560]{1,0:T(8,128)S(1)}, u32[]{:S(2)}, u32[]{:S(2)}) %collective-permute-start.5) | collective-permute-done | bytes 81952 | tf_op jit(solution)/shard_map/ppermute | solution.py:229
  35.6 1.4 %collective-permute-start.6 = (f32[8,5120]{1,0:T(8,128)S(1)}, f32[8,5120]{1,0:T(8,128)S(1)}, u32[]{:S(2)}, u32[]{:S(2)}) collective-permute-start(f32[8,5120]{1,0:T(8,128)S(1)} %pad_maximum_fusion.2), channel_id=1, source_target_pairs={{0,24},{1,13},{2,26},{3,15},{4,8},{5,29},{6,10},{7,31},{8,4},{9,17... | collective-permute-start | bytes 491528 | tf_op jit(solution)/shard_map/ppermute | solution.py:229
  37.0 0.9 %collective-permute-done.14 = f32[8,5120]{1,0:T(8,128)S(1)} collective-permute-done((f32[8,5120]{1,0:T(8,128)S(1)}, f32[8,5120]{1,0:T(8,128)S(1)}, u32[]{:S(2)}, u32[]{:S(2)}) %collective-permute-start.14) | collective-permute-done | bytes 163872 | tf_op jit(solution)/shard_map/ppermute | solution.py:229
  38.0 0.3 collective-permute-start.15
  38.2 2.2 %collective-permute-done.6 = f32[8,5120]{1,0:T(8,128)S(1)} collective-permute-done((f32[8,5120]{1,0:T(8,128)S(1)}, f32[8,5120]{1,0:T(8,128)S(1)}, u32[]{:S(2)}, u32[]{:S(2)}) %collective-permute-start.6) | collective-permute-done | bytes 163872 | tf_op jit(solution)/shard_map/ppermute | solution.py:229
  40.5 0.2 collective-permute-start.7
  40.7 0.0 collective-permute-done.15.other
  40.7 0.9 %finish.3 = (f32[16,5120]{1,0:T(8,128)}, f32[16,5120]{1,0:T(8,128)}) custom-call(f32[16,5120]{1,0:T(8,128)S(1)} %pad_maximum_fusion.1.mine, f32[16,5120]{1,0:T(8,128)S(1)} %collective-permute-done.15.other, f32[8,128]{1,0:T(8,128)S(1)} %slice.47.total), custom_call_target="tpu_custom_call" | custom-call | flops 163840 | bytes 1310720 | tf_op jit(solution)/shard_map/finish/pallas_call | solution.py:177
  41.6 0.6 %collective-permute-done.7.other = f32[16,5120]{1,0:T(8,128)S(1)} collective-permute-done((f32[16,5120]{1,0:T(8,128)S(1)}, f32[16,5120]{1,0:T(8,128)S(1)}, u32[]{:S(2)}, u32[]{:S(2)}) %collective-permute-start.7) | collective-permute-done | bytes 327712 | tf_op jit(solution)/shard_map/ppermute | solution.py:232
  42.2 0.9 %finish.2 = (f32[16,5120]{1,0:T(8,128)}, f32[16,5120]{1,0:T(8,128)}) custom-call(f32[16,5120]{1,0:T(8,128)S(1)} %pad_maximum_fusion.mine, f32[16,5120]{1,0:T(8,128)S(1)} %collective-permute-done.7.other, f32[8,128]{1,0:T(8,128)S(1)} %slice.47.total), custom_call_target="tpu_custom_call" | custom-call | flops 163840 | bytes 1310720 | tf_op jit(solution)/shard_map/finish/pallas_call | solution.py:177
  (26 shorter events, 0.5 us)
Async XLA Ops:
  4.2 3.7 %collective-permute-start.8 = (f32[16,5120]{1,0:T(8,128)S(1)}, f32[16,5120]{1,0:T(8,128)S(1)}, u32[]{:S(2)}, u32[]{:S(2)}) collective-permute-start(f32[16,5120]{1,0:T(8,128)S(1)} %get-tuple-element.18), channel_id=1, source_target_pairs={{0,8},{8,0},{16,24},{24,16},{1,9},{9,1},{17,25},{25,17},{2,10},{10... | collective-permute-start | bytes 983048 | tf_op jit(solution)/shard_map/ppermute | solution.py:232
  4.7 5.9 %collective-permute-start = (f32[16,5248]{1,0:T(8,128)S(1)}, f32[16,5248]{1,0:T(8,128)S(1)}, u32[]{:S(2)}, u32[]{:S(2)}) collective-permute-start(f32[16,5248]{1,0:T(8,128)S(1)} %get-tuple-element.15), channel_id=1, source_target_pairs={{0,8},{8,0},{16,24},{24,16},{1,9},{9,1},{17,25},{25,17},{2,10},{10... | collective-permute-start | bytes 1007624 | tf_op jit(solution)/shard_map/ppermute | solution.py:232
  8.0 5.7 %collective-permute-start.9 = (f32[8,5120]{1,0:T(8,128)S(1)}, f32[8,5120]{1,0:T(8,128)S(1)}, u32[]{:S(2)}, u32[]{:S(2)}) collective-permute-start(f32[8,5120]{1,0:T(8,128)S(1)} %slice_select_fusion.1), channel_id=1, source_target_pairs={{0,24},{1,13},{2,26},{3,15},{4,8},{5,29},{6,10},{7,31},{8,4},{9,17... | collective-permute-start | bytes 491528 | tf_op jit(solution)/shard_map/ppermute | solution.py:229
  10.7 5.1 %collective-permute-start.1 = (f32[8,5248]{1,0:T(8,128)S(1)}, f32[8,5248]{1,0:T(8,128)S(1)}, u32[]{:S(2)}, u32[]{:S(2)}) collective-permute-start(f32[8,5248]{1,0:T(8,128)S(1)} %slice_select_fusion), channel_id=1, source_target_pairs={{0,24},{1,13},{2,26},{3,15},{4,8},{5,29},{6,10},{7,31},{8,4},{9,17... | collective-permute-start | bytes 503816 | tf_op jit(solution)/shard_map/ppermute | solution.py:229
  13.7 4.3 %collective-permute-start.10 = (f32[8,2560]{1,0:T(8,128)S(1)}, f32[8,2560]{1,0:T(8,128)S(1)}, u32[]{:S(2)}, u32[]{:S(2)}) collective-permute-start(f32[8,2560]{1,0:T(8,128)S(1)} %slice_select_fusion.3), channel_id=1, source_target_pairs={{0,12},{1,25},{2,14},{3,27},{4,28},{5,9},{6,30},{7,11},{8,16},{9,5... | collective-permute-start | bytes 245768 | tf_op jit(solution)/shard_map/ppermute | solution.py:229
  15.9 4.0 %collective-permute-start.2 = (f32[8,2688]{1,0:T(8,128)S(1)}, f32[8,2688]{1,0:T(8,128)S(1)}, u32[]{:S(2)}, u32[]{:S(2)}) collective-permute-start(f32[8,2688]{1,0:T(8,128)S(1)} %slice_select_fusion.2), channel_id=1, source_target_pairs={{0,12},{1,25},{2,14},{3,27},{4,28},{5,9},{6,30},{7,11},{8,16},{9,5... | collective-permute-start | bytes 258056 | tf_op jit(solution)/shard_map/ppermute | solution.py:229
  18.0 4.2 %collective-permute-start.11 = (f32[8,2560]{1,0:T(8,128)S(1)}, f32[8,2560]{1,0:T(8,128)S(1)}, u32[]{:S(2)}, u32[]{:S(2)}) collective-permute-start(f32[8,2560]{1,0:T(8,128)S(1)} %select_add_fusion.3), channel_id=1, source_target_pairs={{0,9},{1,3},{2,11},{3,1},{4,6},{5,12},{6,4},{7,14},{8,10},{9,0},{1... | collective-permute-start | bytes 245768 | tf_op jit(solution)/shard_map/ppermute | solution.py:229
  19.9 5.3 %collective-permute-start.3 = (f32[8,2688]{1,0:T(8,128)S(1)}, f32[8,2688]{1,0:T(8,128)S(1)}, u32[]{:S(2)}, u32[]{:S(2)}) collective-permute-start(f32[8,2688]{1,0:T(8,128)S(1)} %select_add_fusion.2), channel_id=1, source_target_pairs={{0,9},{1,3},{2,11},{3,1},{4,6},{5,12},{6,4},{7,14},{8,10},{9,0},{1... | collective-permute-start | bytes 258056 | tf_op jit(solution)/shard_map/ppermute | solution.py:229
  22.2 6.9 %collective-permute-start.12 = (f32[8,2560]{1,0:T(8,128)S(1)}, f32[8,2560]{1,0:T(8,128)S(1)}, u32[]{:S(2)}, u32[]{:S(2)}) collective-permute-start(f32[8,2560]{1,0:T(8,128)S(1)} %add.38), channel_id=1, source_target_pairs={{0,2},{1,8},{2,0},{3,10},{4,13},{5,7},{6,15},{7,5},{8,1},{9,11},{1... | collective-permute-start | bytes 245768 | tf_op jit(solution)/shard_map/ppermute | solution.py:229
  25.3 6.4 %collective-permute-start.4 = (f32[8,2688]{1,0:T(8,128)S(1)}, f32[8,2688]{1,0:T(8,128)S(1)}, u32[]{:S(2)}, u32[]{:S(2)}) collective-permute-start(f32[8,2688]{1,0:T(8,128)S(1)} %add.33), channel_id=1, source_target_pairs={{0,2},{1,8},{2,0},{3,10},{4,13},{5,7},{6,15},{7,5},{8,1},{9,11},{1... | collective-permute-start | bytes 258056 | tf_op jit(solution)/shard_map/ppermute | solution.py:229
  29.1 3.9 %collective-permute-start.13 = (f32[8,2560]{1,0:T(8,128)S(1)}, f32[8,2560]{1,0:T(8,128)S(1)}, u32[]{:S(2)}, u32[]{:S(2)}) collective-permute-start(f32[8,2560]{1,0:T(8,128)S(1)} %add.39), channel_id=1, source_target_pairs={{0,12},{1,25},{2,14},{3,27},{4,28},{5,9},{6,30},{7,11},{8,16},{9,5... | collective-permute-start | bytes 245768 | tf_op jit(solution)/shard_map/ppermute | solution.py:229
  31.7 3.9 %collective-permute-start.5 = (f32[8,2560]{1,0:T(8,128)S(1)}, f32[8,2560]{1,0:T(8,128)S(1)}, u32[]{:S(2)}, u32[]{:S(2)}) collective-permute-start(f32[8,2560]{1,0:T(8,128)S(1)} %slice.46), channel_id=1, source_target_pairs={{0,12},{1,25},{2,14},{3,27},{4,28},{5,9},{6,30},{7,11},{8,16},{9,5... | collective-permute-start | bytes 245768 | tf_op jit(solution)/shard_map/ppermute | solution.py:229
  33.1 4.8 %collective-permute-start.14 = (f32[8,5120]{1,0:T(8,128)S(1)}, f32[8,5120]{1,0:T(8,128)S(1)}, u32[]{:S(2)}, u32[]{:S(2)}) collective-permute-start(f32[8,5120]{1,0:T(8,128)S(1)} %pad_maximum_fusion.3), channel_id=1, source_target_pairs={{0,24},{1,13},{2,26},{3,15},{4,8},{5,29},{6,10},{7,31},{8,4},{9,17... | collective-permute-start | bytes 491528 | tf_op jit(solution)/shard_map/ppermute | solution.py:229
  35.6 4.8 %collective-permute-start.6 = (f32[8,5120]{1,0:T(8,128)S(1)}, f32[8,5120]{1,0:T(8,128)S(1)}, u32[]{:S(2)}, u32[]{:S(2)}) collective-permute-start(f32[8,5120]{1,0:T(8,128)S(1)} %pad_maximum_fusion.2), channel_id=1, source_target_pairs={{0,24},{1,13},{2,26},{3,15},{4,8},{5,29},{6,10},{7,31},{8,4},{9,17... | collective-permute-start | bytes 491528 | tf_op jit(solution)/shard_map/ppermute | solution.py:229
  38.0 2.7 %collective-permute-start.15 = (f32[16,5120]{1,0:T(8,128)S(1)}, f32[16,5120]{1,0:T(8,128)S(1)}, u32[]{:S(2)}, u32[]{:S(2)}) collective-permute-start(f32[16,5120]{1,0:T(8,128)S(1)} %pad_maximum_fusion.1.mine), channel_id=1, source_target_pairs={{0,8},{8,0},{16,24},{24,16},{1,9},{9,1},{17,25},{25,17},{2,10},{10... | collective-permute-start | bytes 983048 | tf_op jit(solution)/shard_map/ppermute | solution.py:232
  40.5 1.7 %collective-permute-start.7 = (f32[16,5120]{1,0:T(8,128)S(1)}, f32[16,5120]{1,0:T(8,128)S(1)}, u32[]{:S(2)}, u32[]{:S(2)}) collective-permute-start(f32[16,5120]{1,0:T(8,128)S(1)} %pad_maximum_fusion.mine), channel_id=1, source_target_pairs={{0,8},{8,0},{16,24},{24,16},{1,9},{9,1},{17,25},{25,17},{2,10},{10... | collective-permute-start | bytes 983048 | tf_op jit(solution)/shard_map/ppermute | solution.py:232

commit v6 on v4

--- a/solution.py
+++ b/solution.py
@@ -11,13 +11,23 @@
 LANES = 128
 SUBLANES = 8
 PARTS = 4
+CHUNKS = 3
 NT = (((1,), (1,)), ((), ()))
 NN = (((1,), (0,)), ((), ()))
 dot = functools.partial(lax.dot_general, preferred_element_type=jnp.float32)
 
 
+def chunks_of(width):
+    tiles = width // LANES
+    ends = [-(-tiles * k // CHUNKS) * LANES for k in range(CHUNKS + 1)]
+    return [(a, b - a) for a, b in zip(ends, ends[1:])]
+
+
 def role_of(gx, gy, gz):
-    return (gx ^ (gx >> 1) ^ gy ^ gz) & 1
+    bits = gx ^ gy ^ gz
+    for shift in (8, 4, 2, 1):
+        bits = bits ^ (bits >> shift)
+    return bits & 1
 
 
 def role_here():
@@ -26,8 +36,9 @@
 
 def adapter_kernel(
     parts, flip, lengths_in, rows, query_grad, value_grad, query_down, value_down, query_up, value_up,
-    down_sum, up_sum, held_rows, held_grad, held_down, held_up, lengths, sems,
+    *refs,
 ):
+    *sums, held_rows, held_grad, held_down, held_up, lengths, sems = refs
     tokens, width = held_rows.shape
     step = width // parts
     cuts = [pl.ds(k * step, step) for k in range(parts)]
@@ -84,10 +95,12 @@
         count = count + lengths[s]
     inner = jnp.where(valid, inner, 0.0).astype(jnp.bfloat16)
     back = jnp.where(valid, back, 0.0).astype(jnp.bfloat16)
-    for cut in cuts:
-        down_sum[:, cut] = dot(back, held_rows[:, cut], NN)
-        up_sum[:, cut] = dot(inner, held_grad[:, cut], NN)
-    down_sum[:, width:] = jnp.full((down_sum.shape[0], LANES), count.astype(jnp.float32), jnp.float32)
+    rank = inner.shape[0]
+    for block, (first, columns) in zip(sums, chunks_of(width)):
+        cut = pl.ds(first, columns)
+        block[:rank, :columns] = dot(back, held_rows[:, cut], NN)
+        block[rank:, :columns] = dot(inner, held_grad[:, cut], NN)
+    sums[-1][:, columns:] = jnp.full((2 * rank, LANES), count.astype(jnp.float32), jnp.float32)
 
 
 def adapter_sums(flip, lengths, rows, *rest):
@@ -95,12 +108,14 @@
     rank = rest[-1].shape[0]
     wide = pltpu.VMEM((tokens, width), rows.dtype)
     thin = pltpu.VMEM((rank, width), rows.dtype)
+    widths = [columns for _, columns in chunks_of(width)]
+    widths[-1] += LANES
     args = [pltpu.with_memory_space_constraint(x, pltpu.HBM) for x in (lengths, rows, *rest)]
     return pl.pallas_call(
         functools.partial(adapter_kernel, PARTS, flip),
-        out_shape=(pltpu.VMEM((rank, width + LANES), jnp.float32), pltpu.VMEM((rank, width), jnp.float32)),
+        out_shape=tuple(pltpu.VMEM((2 * rank, columns), jnp.float32) for columns in widths),
         in_specs=[pl.BlockSpec(memory_space=pltpu.HBM)] * len(args),
-        out_specs=(pl.BlockSpec(memory_space=pltpu.VMEM),) * 2,
+        out_specs=(pl.BlockSpec(memory_space=pltpu.VMEM),) * len(widths),
         scratch_shapes=[
             wide, wide, thin, thin, pltpu.SMEM(lengths.shape, lengths.dtype),
             pltpu.SemaphoreType.DMA((2, PARTS + 2)),
@@ -113,35 +128,40 @@
     )(*args)
 
 
-def finish_kernel(mine, other, total, query, value, out, sems):
+def finish_kernel(first, mine, other, total, *refs):
+    *targets, out, sems = refs[-6:]
     role = role_here()
-    rows = mine.shape[0] // 2
+    rank = mine.shape[0] // 2
+    columns = pl.ds(first, mine.shape[1])
     by = total[0, 0]
     copies = []
     for k in range(2):
-        cut = pl.ds(k * rows, rows)
+        cut = pl.ds(k * rank, rank)
         out[role, cut] = mine[cut] / by
         out[1 - role, cut] = other[cut] / by
-        for c, target in enumerate((query, value)):
-            copies.append(pltpu.make_async_copy(out.at[c, cut], target.at[cut], sems.at[c, k]))
+        for c in range(2):
+            target = targets[2 * c + k].at[:, columns]
+            copies.append(pltpu.make_async_copy(out.at[c, cut], target, sems.at[c, k]))
             copies[-1].start()
     for copy in copies:
         copy.wait()
 
 
-def finish(mine, other, total):
+def finish(first, width, mine, other, total, outs):
     near = pl.BlockSpec(memory_space=pltpu.VMEM)
     far = pl.BlockSpec(memory_space=pltpu.HBM)
+    shape = (mine.shape[0] // 2, width)
     return pl.pallas_call(
-        finish_kernel,
-        out_shape=(jax.ShapeDtypeStruct(mine.shape, mine.dtype),) * 2,
-        in_specs=[near] * 3,
-        out_specs=(far,) * 2,
+        functools.partial(finish_kernel, first),
+        out_shape=(jax.ShapeDtypeStruct(shape, mine.dtype),) * 4,
+        in_specs=[near] * 3 + [far] * len(outs),
+        out_specs=(far,) * 4,
         scratch_shapes=[pltpu.VMEM((2, *mine.shape), mine.dtype), pltpu.SemaphoreType.DMA((2, 2))],
+        input_output_aliases={3 + k: k for k in range(len(outs))},
         compiler_params=pltpu.CompilerParams(vmem_limit_bytes=8 << 20),
         cost_estimate=pl.CostEstimate(flops=2 * mine.size, bytes_accessed=16 * mine.size, transcendentals=0),
         name="finish",
-    )(*(pltpu.with_memory_space_constraint(x, pltpu.VMEM) for x in (mine, other, total)))
+    )(*(pltpu.with_memory_space_constraint(x, pltpu.VMEM) for x in (mine, other, total)), *outs)
 
 
 def axis_bits(axis, size, first=0):
@@ -190,54 +210,37 @@
         return lax.ppermute(array, "gx", [(i, i ^ 1) for i in range(self.sizes["gx"])])
 
 
-def halves(array, width, axis):
-    if axis == 0:
-        rows = array.shape[0] // 2
-        return array[:rows], array[rows:]
-    tail = array[:, width:]
-    half = width // 2
-    low, high = array[:, :half], array[:, half:width]
-    if not tail.shape[1]:
-        return low, high
-    return jnp.concatenate([low, tail], axis=1), jnp.concatenate([high, tail], axis=1)
-
-
 def body(sizes, hidden_rows, query_grad, value_grad, query_down, query_up, value_down, value_up, lengths):
     args = (lengths, hidden_rows, query_grad, value_grad, query_down, value_down, query_up, value_up)
     swaps = Swaps(sizes)
-    widths = [hidden_rows.shape[1]] * 2
     sent = adapter_sums(1, *args)
     got = [swaps.swap_cores(x) for x in sent]
     kept = adapter_sums(0, *args)
     held = [x + y for x, y in zip(kept, got)]
-    cut = []
+    halved = 0
     for stage in range(swaps.count()):
-        axis = None
-        if stage == len(cut):
-            if held[0].shape[0] % (2 * SUBLANES) == 0:
-                axis = 0
-            elif widths[0] % (2 * LANES) == 0 and len(cut) < 2:
-                axis = 1
-        if axis is None:
+        rows = held[0].shape[0] // 2
+        if stage > halved or rows % SUBLANES:
             held = [x + swaps.swap(stage, x) for x in held]
             continue
         high = swaps.high(stage)
         for c, x in enumerate(held):
-            low_half, high_half = halves(x, widths[c], axis)
-            sent = jnp.where(high, low_half, high_half)
-            held[c] = jnp.where(high, high_half, low_half) + swaps.swap(stage, sent)
-            if axis == 1:
-                widths[c] //= 2
-        cut.append(axis)
-    total = held[0][:, widths[0]:]
-    held = [x[:, :width] for x, width in zip(held, widths)]
-    for stage, axis in reversed(list(enumerate(cut))):
+            sent = jnp.where(high, x[:rows], x[rows:])
+            held[c] = jnp.where(high, x[rows:], x[:rows]) + swaps.swap(stage, sent)
+        halved += 1
+    width = hidden_rows.shape[1]
+    blocks = chunks_of(width)
+    total = held[-1][:, blocks[-1][1]:]
+    held[-1] = held[-1][:, :blocks[-1][1]]
+    for stage in reversed(range(halved)):
         high = swaps.high(stage)
         for c, x in enumerate(held):
             other = swaps.swap(stage, x)
-            held[c] = jnp.concatenate([jnp.where(high, other, x), jnp.where(high, x, other)], axis=axis)
-    query, value = zip(*(finish(x, swaps.swap_cores(x), total) for x in held))
-    return (*query, *value)
+            held[c] = jnp.concatenate([jnp.where(high, other, x), jnp.where(high, x, other)], axis=0)
+    outs = ()
+    for (first, _), x in zip(blocks, held):
+        outs = finish(first, width, x, swaps.swap_cores(x), total, outs)
+    return tuple(outs)
 
 
 def solution(mesh):

time: 42.3 us -> 46 us (1.087)
  starting transfers between devices: 19.4 us -> 30.1 us
  waiting for transfers between devices: 14 us -> 6.2 us
  Pallas kernels: 7.45 us -> 8.17 us
    ppermute x12 -> x18, waiting for transfers between devices: 13.4 us -> 5.17 us  [swap(): return lax.ppermute(array, AXES, pairs)]
    ppermute x12 -> x18, starting transfers between devices: 18.3 us -> 24.5 us  [swap(): return lax.ppermute(array, AXES, pairs)]
    ppermute x4 -> x6, starting transfers between devices: 1.07 us -> 5.61 us  [swap_cores(): lax.ppermute(array, 'gx', [(i, i ^ 1) for i in range(self.sizes['gx'])])]
    pallas_call x2 -> x3, Pallas kernels: 1.85 us -> 2.53 us  [finish(): pl.pallas_call(functools.partial(finish_kernel, first), out_shape=(jax.Sh...]
    ppermute x4 -> x6, waiting for transfers between devices: 0.58 us -> 1.02 us  [swap_cores(): lax.ppermute(array, 'gx', [(i, i ^ 1) for i in range(self.sizes['gx'])])]
  transfers between devices with their start and end apart: 16 -> 24, of which waited for: 11 -> 7; matrix products, arithmetic and copies ran while one was open for 1% -> 1% of each run, Pallas kernels for 9% -> 10%
where the time goes in v6:
time: 46 us; the launch traced here: 45.8 us
  starting transfers between devices  30.1 us (65%)
  Pallas kernels  8.17 us (18%)
  waiting for transfers between devices  6.2 us (13%)
  between operations  0.86 us (2%)
  other arithmetic  0.48 us (1%)
    ppermute x18, starting transfers between devices, swap(): return lax.ppermute(array, AXES, pairs)  24.5 us
    pallas_call x2, Pallas kernels, adapter_sums(): pl.pallas_call(functools.partial(adapter_kernel, PARTS, flip), out_shape=...  5.64 us
    ppermute x6, starting transfers between devices, swap_cores(): lax.ppermute(array, 'gx', [(i, i ^ 1) for i in range(self.sizes['gx'])])  5.61 us
    ppermute x18, waiting for transfers between devices, swap(): return lax.ppermute(array, AXES, pairs)  5.17 us
    pallas_call x3, Pallas kernels, finish(): pl.pallas_call(functools.partial(finish_kernel, first), out_shape=(jax.Sh...  2.53 us
    ppermute x6, waiting for transfers between devices, swap_cores(): lax.ppermute(array, 'gx', [(i, i ^ 1) for i in range(self.sizes['gx'])])  1.02 us
  transfers between devices with their start and end apart: 24, of which 7 were waited for; matrix products, arithmetic and copies ran while one was open for 1% of the time, Pallas kernels for 10%

profile of v6, /device:TPU:0, one launch (start us, length us, event | category | flops | bytes accessed | tf_op | source)
XLA Modules:
  0.0 45.8 jit_solution(11714434031494087178)
XLA Ops:
  0.6 2.8 %adapter.3 = (f32[32,1792]{1,0:T(8,128)S(1)}, f32[32,1664]{1,0:T(8,128)S(1)}, f32[32,1792]{1,0:T(8,128)S(1)}) custom-call(s32[2]{0:T(128)} %lengths_in.3, bf16[128,5120]{1,0:T(8,128)(2,1)} %rows.3, bf16[128,5120]{1,0:T(8,128)(2,1)} %query_grad.3, bf16[128,5120]{1,0:T(8,128)(2,1)} %value_grad.3, bf16[16,5120]{1,0:T(8,128)(2,1)} %query_down.3, ...), custom_call_target="tpu_custom_call" | custom-call | flops 83886080 | bytes 2621440 | tf_op jit(solution)/shard_map/adapter/pallas_call | solution.py:114
  3.5 0.5 %collective-permute-start.8 = (f32[32,1664]{1,0:T(8,128)S(1)}, f32[32,1664]{1,0:T(8,128)S(1)}, u32[]{:S(2)}, u32[]{:S(2)}) collective-permute-start(f32[32,1664]{1,0:T(8,128)S(1)} %get-tuple-element.21), channel_id=1, source_target_pairs={{0,8},{8,0},{16,24},{24,16},{1,9},{9,1},{17,25},{25,17},{2,10},{10... | collective-permute-start | bytes 638984 | tf_op jit(solution)/shard_map/ppermute | solution.py:210
  4.0 0.1 collective-permute-start.16
  4.1 0.4 collective-permute-start
  4.5 2.8 %adapter.2 = (f32[32,1792]{1,0:T(8,128)S(1)}, f32[32,1664]{1,0:T(8,128)S(1)}, f32[32,1792]{1,0:T(8,128)S(1)}) custom-call(s32[2]{0:T(128)} %lengths_in.3, bf16[128,5120]{1,0:T(8,128)(2,1)} %rows.3, bf16[128,5120]{1,0:T(8,128)(2,1)} %query_grad.3, bf16[128,5120]{1,0:T(8,128)(2,1)} %value_grad.3, bf16[16,5120]{1,0:T(8,128)(2,1)} %query_down.3, ...), custom_call_target="tpu_custom_call" | custom-call | flops 83886080 | bytes 2621440 | tf_op jit(solution)/shard_map/adapter/pallas_call | solution.py:114
  7.3 0.0 collective-permute-done.8
  7.4 2.7 %collective-permute-start.9 = (f32[16,1664]{1,0:T(8,128)S(1)}, f32[16,1664]{1,0:T(8,128)S(1)}, u32[]{:S(2)}, u32[]{:S(2)}) collective-permute-start(f32[16,1664]{1,0:T(8,128)S(1)} %slice_select_fusion.2), channel_id=1, source_target_pairs={{0,24},{1,13},{2,14},{3,27},{4,8},{5,29},{6,30},{7,11},{8,4},{9,17... | collective-permute-start | bytes 319496 | tf_op jit(solution)/shard_map/ppermute | solution.py:207
  10.1 0.0 collective-permute-done.16
  10.1 0.1 collective-permute-start.17
  10.2 0.0 collective-permute-done
  10.3 1.8 %collective-permute-start.1 = (f32[16,1792]{1,0:T(8,128)S(1)}, f32[16,1792]{1,0:T(8,128)S(1)}, u32[]{:S(2)}, u32[]{:S(2)}) collective-permute-start(f32[16,1792]{1,0:T(8,128)S(1)} %slice_select_fusion.1), channel_id=1, source_target_pairs={{0,24},{1,13},{2,14},{3,27},{4,8},{5,29},{6,30},{7,11},{8,4},{9,17... | collective-permute-start | bytes 344072 | tf_op jit(solution)/shard_map/ppermute | solution.py:207
  12.0 0.4 collective-permute-done.9
  12.5 2.1 %collective-permute-start.10 = (f32[8,1664]{1,0:T(8,128)S(1)}, f32[8,1664]{1,0:T(8,128)S(1)}, u32[]{:S(2)}, u32[]{:S(2)}) collective-permute-start(f32[8,1664]{1,0:T(8,128)S(1)} %slice_select_fusion.5), channel_id=1, source_target_pairs={{0,12},{1,25},{2,26},{3,15},{4,28},{5,9},{6,10},{7,31},{8,16},{9,5... | collective-permute-start | bytes 159752 | tf_op jit(solution)/shard_map/ppermute | solution.py:207
  14.6 0.0 collective-permute-done.17
  14.7 1.3 %collective-permute-start.18 = (f32[8,1792]{1,0:T(8,128)S(1)}, f32[8,1792]{1,0:T(8,128)S(1)}, u32[]{:S(2)}, u32[]{:S(2)}) collective-permute-start(f32[8,1792]{1,0:T(8,128)S(1)} %slice_select_fusion.3), channel_id=1, source_target_pairs={{0,12},{1,25},{2,26},{3,15},{4,28},{5,9},{6,10},{7,31},{8,16},{9,5... | collective-permute-start | bytes 172040 | tf_op jit(solution)/shard_map/ppermute | solution.py:207
  16.0 0.0 collective-permute-done.1
  16.1 1.2 %collective-permute-start.2 = (f32[8,1792]{1,0:T(8,128)S(1)}, f32[8,1792]{1,0:T(8,128)S(1)}, u32[]{:S(2)}, u32[]{:S(2)}) collective-permute-start(f32[8,1792]{1,0:T(8,128)S(1)} %slice_select_fusion.4), channel_id=1, source_target_pairs={{0,12},{1,25},{2,26},{3,15},{4,28},{5,9},{6,10},{7,31},{8,16},{9,5... | collective-permute-start | bytes 172040 | tf_op jit(solution)/shard_map/ppermute | solution.py:207
  17.3 0.0 collective-permute-done.10
  17.3 1.3 %collective-permute-start.11 = (f32[8,1664]{1,0:T(8,128)S(1)}, f32[8,1664]{1,0:T(8,128)S(1)}, u32[]{:S(2)}, u32[]{:S(2)}) collective-permute-start(f32[8,1664]{1,0:T(8,128)S(1)} %select_add_fusion.5), channel_id=1, source_target_pairs={{0,9},{1,11},{2,8},{3,10},{4,14},{5,12},{6,15},{7,13},{8,2},{9,0},... | collective-permute-start | bytes 159752 | tf_op jit(solution)/shard_map/ppermute | solution.py:207
  18.6 0.0 collective-permute-done.18
  18.7 1.1 %collective-permute-start.19 = (f32[8,1792]{1,0:T(8,128)S(1)}, f32[8,1792]{1,0:T(8,128)S(1)}, u32[]{:S(2)}, u32[]{:S(2)}) collective-permute-start(f32[8,1792]{1,0:T(8,128)S(1)} %select_add_fusion.3), channel_id=1, source_target_pairs={{0,9},{1,11},{2,8},{3,10},{4,14},{5,12},{6,15},{7,13},{8,2},{9,0},... | collective-permute-start | bytes 172040 | tf_op jit(solution)/shard_map/ppermute | solution.py:207
  19.8 0.0 collective-permute-done.2
  19.8 1.3 %collective-permute-start.3 = (f32[8,1792]{1,0:T(8,128)S(1)}, f32[8,1792]{1,0:T(8,128)S(1)}, u32[]{:S(2)}, u32[]{:S(2)}) collective-permute-start(f32[8,1792]{1,0:T(8,128)S(1)} %select_add_fusion.4), channel_id=1, source_target_pairs={{0,9},{1,11},{2,8},{3,10},{4,14},{5,12},{6,15},{7,13},{8,2},{9,0},... | collective-permute-start | bytes 172040 | tf_op jit(solution)/shard_map/ppermute | solution.py:207
  21.1 0.0 collective-permute-done.11
  21.1 2.6 %collective-permute-start.12 = (f32[8,1664]{1,0:T(8,128)S(1)}, f32[8,1664]{1,0:T(8,128)S(1)}, u32[]{:S(2)}, u32[]{:S(2)}) collective-permute-start(f32[8,1664]{1,0:T(8,128)S(1)} %add.53), channel_id=1, source_target_pairs={{0,10},{1,8},{2,11},{3,9},{4,13},{5,15},{6,12},{7,14},{8,1},{9,3},... | collective-permute-start | bytes 159752 | tf_op jit(solution)/shard_map/ppermute | solution.py:207
  23.8 0.0 collective-permute-done.19
  23.8 1.7 %collective-permute-start.20 = (f32[8,1792]{1,0:T(8,128)S(1)}, f32[8,1792]{1,0:T(8,128)S(1)}, u32[]{:S(2)}, u32[]{:S(2)}) collective-permute-start(f32[8,1792]{1,0:T(8,128)S(1)} %add.58), channel_id=1, source_target_pairs={{0,10},{1,8},{2,11},{3,9},{4,13},{5,15},{6,12},{7,14},{8,1},{9,3},... | collective-permute-start | bytes 172040 | tf_op jit(solution)/shard_map/ppermute | solution.py:207
  25.5 0.0 collective-permute-done.3
  25.5 1.5 %collective-permute-start.4 = (f32[8,1792]{1,0:T(8,128)S(1)}, f32[8,1792]{1,0:T(8,128)S(1)}, u32[]{:S(2)}, u32[]{:S(2)}) collective-permute-start(f32[8,1792]{1,0:T(8,128)S(1)} %add.48), channel_id=1, source_target_pairs={{0,10},{1,8},{2,11},{3,9},{4,13},{5,15},{6,12},{7,14},{8,1},{9,3},... | collective-permute-start | bytes 172040 | tf_op jit(solution)/shard_map/ppermute | solution.py:207
  27.0 0.8 %collective-permute-done.12 = f32[8,1664]{1,0:T(8,128)S(1)} collective-permute-done((f32[8,1664]{1,0:T(8,128)S(1)}, f32[8,1664]{1,0:T(8,128)S(1)}, u32[]{:S(2)}, u32[]{:S(2)}) %collective-permute-start.12) | collective-permute-done | bytes 53280 | tf_op jit(solution)/shard_map/ppermute | solution.py:207
  27.7 1.0 %collective-permute-start.13 = (f32[8,1664]{1,0:T(8,128)S(1)}, f32[8,1664]{1,0:T(8,128)S(1)}, u32[]{:S(2)}, u32[]{:S(2)}) collective-permute-start(f32[8,1664]{1,0:T(8,128)S(1)} %add.54), channel_id=1, source_target_pairs={{0,12},{1,25},{2,26},{3,15},{4,28},{5,9},{6,10},{7,31},{8,16},{9,5... | collective-permute-start | bytes 159752 | tf_op jit(solution)/shard_map/ppermute | solution.py:207
  28.7 0.0 collective-permute-done.20
  28.7 0.9 %collective-permute-start.21 = (f32[8,1792]{1,0:T(8,128)S(1)}, f32[8,1792]{1,0:T(8,128)S(1)}, u32[]{:S(2)}, u32[]{:S(2)}) collective-permute-start(f32[8,1792]{1,0:T(8,128)S(1)} %add.59), channel_id=1, source_target_pairs={{0,12},{1,25},{2,26},{3,15},{4,28},{5,9},{6,10},{7,31},{8,16},{9,5... | collective-permute-start | bytes 172040 | tf_op jit(solution)/shard_map/ppermute | solution.py:207
  29.6 0.8 %collective-permute-done.4 = f32[8,1792]{1,0:T(8,128)S(1)} collective-permute-done((f32[8,1792]{1,0:T(8,128)S(1)}, f32[8,1792]{1,0:T(8,128)S(1)}, u32[]{:S(2)}, u32[]{:S(2)}) %collective-permute-start.4) | collective-permute-done | bytes 57376 | tf_op jit(solution)/shard_map/ppermute | solution.py:207
  30.4 1.2 %collective-permute-start.5 = (f32[8,1664]{1,0:T(8,128)S(1)}, f32[8,1664]{1,0:T(8,128)S(1)}, u32[]{:S(2)}, u32[]{:S(2)}) collective-permute-start(f32[8,1664]{1,0:T(8,128)S(1)} %slice.72), channel_id=1, source_target_pairs={{0,12},{1,25},{2,26},{3,15},{4,28},{5,9},{6,10},{7,31},{8,16},{9,5... | collective-permute-start | bytes 159752 | tf_op jit(solution)/shard_map/ppermute | solution.py:207
  31.7 0.0 collective-permute-done.13
  31.7 0.7 %collective-permute-start.14 = (f32[16,1664]{1,0:T(8,128)S(1)}, f32[16,1664]{1,0:T(8,128)S(1)}, u32[]{:S(2)}, u32[]{:S(2)}) collective-permute-start(f32[16,1664]{1,0:T(8,128)S(1)} %pad_maximum_fusion.5), channel_id=1, source_target_pairs={{0,24},{1,13},{2,14},{3,27},{4,8},{5,29},{6,30},{7,11},{8,4},{9,17... | collective-permute-start | bytes 319496 | tf_op jit(solution)/shard_map/ppermute | solution.py:207
  32.4 1.7 %collective-permute-done.5 = f32[8,1664]{1,0:T(8,128)S(1)} collective-permute-done((f32[8,1664]{1,0:T(8,128)S(1)}, f32[8,1664]{1,0:T(8,128)S(1)}, u32[]{:S(2)}, u32[]{:S(2)}) %collective-permute-start.5) | collective-permute-done | bytes 53280 | tf_op jit(solution)/shard_map/ppermute | solution.py:207
  34.1 1.3 %collective-permute-start.6 = (f32[16,1664]{1,0:T(8,128)S(1)}, f32[16,1664]{1,0:T(8,128)S(1)}, u32[]{:S(2)}, u32[]{:S(2)}) collective-permute-start(f32[16,1664]{1,0:T(8,128)S(1)} %pad_maximum_fusion.4), channel_id=1, source_target_pairs={{0,24},{1,13},{2,14},{3,27},{4,8},{5,29},{6,30},{7,11},{8,4},{9,17... | collective-permute-start | bytes 319496 | tf_op jit(solution)/shard_map/ppermute | solution.py:207
  35.4 0.0 collective-permute-done.21
  35.4 0.6 %collective-permute-start.22 = (f32[16,1792]{1,0:T(8,128)S(1)}, f32[16,1792]{1,0:T(8,128)S(1)}, u32[]{:S(2)}, u32[]{:S(2)}) collective-permute-start(f32[16,1792]{1,0:T(8,128)S(1)} %pad_maximum_fusion.3), channel_id=1, source_target_pairs={{0,24},{1,13},{2,14},{3,27},{4,8},{5,29},{6,30},{7,11},{8,4},{9,17... | collective-permute-start | bytes 344072 | tf_op jit(solution)/shard_map/ppermute | solution.py:207
  36.0 0.5 %collective-permute-done.14 = f32[16,1664]{1,0:T(8,128)S(1)} collective-permute-done((f32[16,1664]{1,0:T(8,128)S(1)}, f32[16,1664]{1,0:T(8,128)S(1)}, u32[]{:S(2)}, u32[]{:S(2)}) %collective-permute-start.14) | collective-permute-done | bytes 106528 | tf_op jit(solution)/shard_map/ppermute | solution.py:207
  36.5 2.1 %collective-permute-start.15 = (f32[32,1664]{1,0:T(8,128)S(1)}, f32[32,1664]{1,0:T(8,128)S(1)}, u32[]{:S(2)}, u32[]{:S(2)}) collective-permute-start(f32[32,1664]{1,0:T(8,128)S(1)} %pad_maximum_fusion.2.mine), channel_id=1, source_target_pairs={{0,8},{8,0},{16,24},{24,16},{1,9},{9,1},{17,25},{25,17},{2,10},{10... | collective-permute-start | bytes 638984 | tf_op jit(solution)/shard_map/ppermute | solution.py:210
  38.6 0.0 collective-permute-done.6
  38.6 1.1 %collective-permute-done.22 = f32[16,1792]{1,0:T(8,128)S(1)} collective-permute-done((f32[16,1792]{1,0:T(8,128)S(1)}, f32[16,1792]{1,0:T(8,128)S(1)}, u32[]{:S(2)}, u32[]{:S(2)}) %collective-permute-start.22) | collective-permute-done | bytes 114720 | tf_op jit(solution)/shard_map/ppermute | solution.py:207
  39.8 2.4 %collective-permute-start.23 = (f32[32,1792]{1,0:T(8,128)S(1)}, f32[32,1792]{1,0:T(8,128)S(1)}, u32[]{:S(2)}, u32[]{:S(2)}) collective-permute-start(f32[32,1792]{1,0:T(8,128)S(1)} %pad_maximum_fusion.mine), channel_id=1, source_target_pairs={{0,8},{8,0},{16,24},{24,16},{1,9},{9,1},{17,25},{25,17},{2,10},{10... | collective-permute-start | bytes 688136 | tf_op jit(solution)/shard_map/ppermute | solution.py:210
  42.1 0.1 collective-permute-start.7
  42.2 1.0 %collective-permute-done.23.other = f32[32,1792]{1,0:T(8,128)S(1)} collective-permute-done((f32[32,1792]{1,0:T(8,128)S(1)}, f32[32,1792]{1,0:T(8,128)S(1)}, u32[]{:S(2)}, u32[]{:S(2)}) %collective-permute-start.23) | collective-permute-done | bytes 229408 | tf_op jit(solution)/shard_map/ppermute | solution.py:210
  43.2 0.8 %finish.3 = (f32[16,5120]{1,0:T(8,128)}, f32[16,5120]{1,0:T(8,128)}, f32[16,5120]{1,0:T(8,128)}, f32[16,5120]{1,0:T(8,128)}) custom-call(f32[32,1792]{1,0:T(8,128)S(1)} %pad_maximum_fusion.mine, f32[32,1792]{1,0:T(8,128)S(1)} %collective-permute-done.23.other, f32[8,128]{1,0:T(8,128)S(1)} %slice.73.total), custom_call_target="tpu_custom_call" | custom-call | flops 114688 | bytes 917504 | tf_op jit(solution)/shard_map/finish/pallas_call | solution.py:154
  44.1 0.0 collective-permute-done.15.other
  44.1 0.8 %finish.4 = (f32[16,5120]{1,0:T(8,128)}, f32[16,5120]{1,0:T(8,128)}, f32[16,5120]{1,0:T(8,128)}, f32[16,5120]{1,0:T(8,128)}) custom-call(f32[32,1664]{1,0:T(8,128)S(1)} %pad_maximum_fusion.2.mine, f32[32,1664]{1,0:T(8,128)S(1)} %collective-permute-done.15.other, ...), custom_call_target="tpu_custom_call", output_to_operand_aliasing={{0}: (3, {}), {1}: (4, {}), {2}: (5, {}), {3}: (6, {})} | custom-call | flops 106496 | bytes 851968 | tf_op jit(solution)/shard_map/finish/pallas_call | solution.py:154
  45.0 0.0 collective-permute-done.7.other
  45.0 0.8 %finish.5 = (f32[16,5120]{1,0:T(8,128)}, f32[16,5120]{1,0:T(8,128)}, f32[16,5120]{1,0:T(8,128)}, f32[16,5120]{1,0:T(8,128)}) custom-call(f32[32,1664]{1,0:T(8,128)S(1)} %pad_maximum_fusion.1.mine, f32[32,1664]{1,0:T(8,128)S(1)} %collective-permute-done.7.other, ...), custom_call_target="tpu_custom_call", output_to_operand_aliasing={{0}: (3, {}), {1}: (4, {}), {2}: (5, {}), {3}: (6, {})} | custom-call | flops 106496 | bytes 851968 | tf_op jit(solution)/shard_map/finish/pallas_call | solution.py:154
  (35 shorter events, 0.5 us)
Async XLA Ops:
  3.5 3.9 %collective-permute-start.8 = (f32[32,1664]{1,0:T(8,128)S(1)}, f32[32,1664]{1,0:T(8,128)S(1)}, u32[]{:S(2)}, u32[]{:S(2)}) collective-permute-start(f32[32,1664]{1,0:T(8,128)S(1)} %get-tuple-element.21), channel_id=1, source_target_pairs={{0,8},{8,0},{16,24},{24,16},{1,9},{9,1},{17,25},{25,17},{2,10},{10... | collective-permute-start | bytes 638984 | tf_op jit(solution)/shard_map/ppermute | solution.py:210
  4.0 6.0 %collective-permute-start.16 = (f32[32,1792]{1,0:T(8,128)S(1)}, f32[32,1792]{1,0:T(8,128)S(1)}, u32[]{:S(2)}, u32[]{:S(2)}) collective-permute-start(f32[32,1792]{1,0:T(8,128)S(1)} %get-tuple-element.23), channel_id=1, source_target_pairs={{0,8},{8,0},{16,24},{24,16},{1,9},{9,1},{17,25},{25,17},{2,10},{10... | collective-permute-start | bytes 688136 | tf_op jit(solution)/shard_map/ppermute | solution.py:210
  4.1 6.1 %collective-permute-start = (f32[32,1792]{1,0:T(8,128)S(1)}, f32[32,1792]{1,0:T(8,128)S(1)}, u32[]{:S(2)}, u32[]{:S(2)}) collective-permute-start(f32[32,1792]{1,0:T(8,128)S(1)} %get-tuple-element.19), channel_id=1, source_target_pairs={{0,8},{8,0},{16,24},{24,16},{1,9},{9,1},{17,25},{25,17},{2,10},{10... | collective-permute-start | bytes 688136 | tf_op jit(solution)/shard_map/ppermute | solution.py:210
  7.4 5.0 %collective-permute-start.9 = (f32[16,1664]{1,0:T(8,128)S(1)}, f32[16,1664]{1,0:T(8,128)S(1)}, u32[]{:S(2)}, u32[]{:S(2)}) collective-permute-start(f32[16,1664]{1,0:T(8,128)S(1)} %slice_select_fusion.2), channel_id=1, source_target_pairs={{0,24},{1,13},{2,14},{3,27},{4,8},{5,29},{6,30},{7,11},{8,4},{9,17... | collective-permute-start | bytes 319496 | tf_op jit(solution)/shard_map/ppermute | solution.py:207
  10.1 4.5 %collective-permute-start.17 = (f32[16,1792]{1,0:T(8,128)S(1)}, f32[16,1792]{1,0:T(8,128)S(1)}, u32[]{:S(2)}, u32[]{:S(2)}) collective-permute-start(f32[16,1792]{1,0:T(8,128)S(1)} %slice_select_fusion), channel_id=1, source_target_pairs={{0,24},{1,13},{2,14},{3,27},{4,8},{5,29},{6,30},{7,11},{8,4},{9,17... | collective-permute-start | bytes 344072 | tf_op jit(solution)/shard_map/ppermute | solution.py:207
  10.3 5.8 %collective-permute-start.1 = (f32[16,1792]{1,0:T(8,128)S(1)}, f32[16,1792]{1,0:T(8,128)S(1)}, u32[]{:S(2)}, u32[]{:S(2)}) collective-permute-start(f32[16,1792]{1,0:T(8,128)S(1)} %slice_select_fusion.1), channel_id=1, source_target_pairs={{0,24},{1,13},{2,14},{3,27},{4,8},{5,29},{6,30},{7,11},{8,4},{9,17... | collective-permute-start | bytes 344072 | tf_op jit(solution)/shard_map/ppermute | solution.py:207
  12.5 4.8 %collective-permute-start.10 = (f32[8,1664]{1,0:T(8,128)S(1)}, f32[8,1664]{1,0:T(8,128)S(1)}, u32[]{:S(2)}, u32[]{:S(2)}) collective-permute-start(f32[8,1664]{1,0:T(8,128)S(1)} %slice_select_fusion.5), channel_id=1, source_target_pairs={{0,12},{1,25},{2,26},{3,15},{4,28},{5,9},{6,10},{7,31},{8,16},{9,5... | collective-permute-start | bytes 159752 | tf_op jit(solution)/shard_map/ppermute | solution.py:207
  14.7 4.0 %collective-permute-start.18 = (f32[8,1792]{1,0:T(8,128)S(1)}, f32[8,1792]{1,0:T(8,128)S(1)}, u32[]{:S(2)}, u32[]{:S(2)}) collective-permute-start(f32[8,1792]{1,0:T(8,128)S(1)} %slice_select_fusion.3), channel_id=1, source_target_pairs={{0,12},{1,25},{2,26},{3,15},{4,28},{5,9},{6,10},{7,31},{8,16},{9,5... | collective-permute-start | bytes 172040 | tf_op jit(solution)/shard_map/ppermute | solution.py:207
  16.1 3.7 %collective-permute-start.2 = (f32[8,1792]{1,0:T(8,128)S(1)}, f32[8,1792]{1,0:T(8,128)S(1)}, u32[]{:S(2)}, u32[]{:S(2)}) collective-permute-start(f32[8,1792]{1,0:T(8,128)S(1)} %slice_select_fusion.4), channel_id=1, source_target_pairs={{0,12},{1,25},{2,26},{3,15},{4,28},{5,9},{6,10},{7,31},{8,16},{9,5... | collective-permute-start | bytes 172040 | tf_op jit(solution)/shard_map/ppermute | solution.py:207
  17.3 3.8 %collective-permute-start.11 = (f32[8,1664]{1,0:T(8,128)S(1)}, f32[8,1664]{1,0:T(8,128)S(1)}, u32[]{:S(2)}, u32[]{:S(2)}) collective-permute-start(f32[8,1664]{1,0:T(8,128)S(1)} %select_add_fusion.5), channel_id=1, source_target_pairs={{0,9},{1,11},{2,8},{3,10},{4,14},{5,12},{6,15},{7,13},{8,2},{9,0},... | collective-permute-start | bytes 159752 | tf_op jit(solution)/shard_map/ppermute | solution.py:207
  18.7 5.1 %collective-permute-start.19 = (f32[8,1792]{1,0:T(8,128)S(1)}, f32[8,1792]{1,0:T(8,128)S(1)}, u32[]{:S(2)}, u32[]{:S(2)}) collective-permute-start(f32[8,1792]{1,0:T(8,128)S(1)} %select_add_fusion.3), channel_id=1, source_target_pairs={{0,9},{1,11},{2,8},{3,10},{4,14},{5,12},{6,15},{7,13},{8,2},{9,0},... | collective-permute-start | bytes 172040 | tf_op jit(solution)/shard_map/ppermute | solution.py:207
  19.8 5.7 %collective-permute-start.3 = (f32[8,1792]{1,0:T(8,128)S(1)}, f32[8,1792]{1,0:T(8,128)S(1)}, u32[]{:S(2)}, u32[]{:S(2)}) collective-permute-start(f32[8,1792]{1,0:T(8,128)S(1)} %select_add_fusion.4), channel_id=1, source_target_pairs={{0,9},{1,11},{2,8},{3,10},{4,14},{5,12},{6,15},{7,13},{8,2},{9,0},... | collective-permute-start | bytes 172040 | tf_op jit(solution)/shard_map/ppermute | solution.py:207
  21.1 6.6 %collective-permute-start.12 = (f32[8,1664]{1,0:T(8,128)S(1)}, f32[8,1664]{1,0:T(8,128)S(1)}, u32[]{:S(2)}, u32[]{:S(2)}) collective-permute-start(f32[8,1664]{1,0:T(8,128)S(1)} %add.53), channel_id=1, source_target_pairs={{0,10},{1,8},{2,11},{3,9},{4,13},{5,15},{6,12},{7,14},{8,1},{9,3},... | collective-permute-start | bytes 159752 | tf_op jit(solution)/shard_map/ppermute | solution.py:207
  23.8 4.9 %collective-permute-start.20 = (f32[8,1792]{1,0:T(8,128)S(1)}, f32[8,1792]{1,0:T(8,128)S(1)}, u32[]{:S(2)}, u32[]{:S(2)}) collective-permute-start(f32[8,1792]{1,0:T(8,128)S(1)} %add.58), channel_id=1, source_target_pairs={{0,10},{1,8},{2,11},{3,9},{4,13},{5,15},{6,12},{7,14},{8,1},{9,3},... | collective-permute-start | bytes 172040 | tf_op jit(solution)/shard_map/ppermute | solution.py:207
  25.5 4.9 %collective-permute-start.4 = (f32[8,1792]{1,0:T(8,128)S(1)}, f32[8,1792]{1,0:T(8,128)S(1)}, u32[]{:S(2)}, u32[]{:S(2)}) collective-permute-start(f32[8,1792]{1,0:T(8,128)S(1)} %add.48), channel_id=1, source_target_pairs={{0,10},{1,8},{2,11},{3,9},{4,13},{5,15},{6,12},{7,14},{8,1},{9,3},... | collective-permute-start | bytes 172040 | tf_op jit(solution)/shard_map/ppermute | solution.py:207
  27.7 3.9 %collective-permute-start.13 = (f32[8,1664]{1,0:T(8,128)S(1)}, f32[8,1664]{1,0:T(8,128)S(1)}, u32[]{:S(2)}, u32[]{:S(2)}) collective-permute-start(f32[8,1664]{1,0:T(8,128)S(1)} %add.54), channel_id=1, source_target_pairs={{0,12},{1,25},{2,26},{3,15},{4,28},{5,9},{6,10},{7,31},{8,16},{9,5... | collective-permute-start | bytes 159752 | tf_op jit(solution)/shard_map/ppermute | solution.py:207
  28.7 6.7 %collective-permute-start.21 = (f32[8,1792]{1,0:T(8,128)S(1)}, f32[8,1792]{1,0:T(8,128)S(1)}, u32[]{:S(2)}, u32[]{:S(2)}) collective-permute-start(f32[8,1792]{1,0:T(8,128)S(1)} %add.59), channel_id=1, source_target_pairs={{0,12},{1,25},{2,26},{3,15},{4,28},{5,9},{6,10},{7,31},{8,16},{9,5... | collective-permute-start | bytes 172040 | tf_op jit(solution)/shard_map/ppermute | solution.py:207
  30.4 3.6 %collective-permute-start.5 = (f32[8,1664]{1,0:T(8,128)S(1)}, f32[8,1664]{1,0:T(8,128)S(1)}, u32[]{:S(2)}, u32[]{:S(2)}) collective-permute-start(f32[8,1664]{1,0:T(8,128)S(1)} %slice.72), channel_id=1, source_target_pairs={{0,12},{1,25},{2,26},{3,15},{4,28},{5,9},{6,10},{7,31},{8,16},{9,5... | collective-permute-start | bytes 159752 | tf_op jit(solution)/shard_map/ppermute | solution.py:207
  31.7 4.8 %collective-permute-start.14 = (f32[16,1664]{1,0:T(8,128)S(1)}, f32[16,1664]{1,0:T(8,128)S(1)}, u32[]{:S(2)}, u32[]{:S(2)}) collective-permute-start(f32[16,1664]{1,0:T(8,128)S(1)} %pad_maximum_fusion.5), channel_id=1, source_target_pairs={{0,24},{1,13},{2,14},{3,27},{4,8},{5,29},{6,30},{7,11},{8,4},{9,17... | collective-permute-start | bytes 319496 | tf_op jit(solution)/shard_map/ppermute | solution.py:207
  34.1 4.5 %collective-permute-start.6 = (f32[16,1664]{1,0:T(8,128)S(1)}, f32[16,1664]{1,0:T(8,128)S(1)}, u32[]{:S(2)}, u32[]{:S(2)}) collective-permute-start(f32[16,1664]{1,0:T(8,128)S(1)} %pad_maximum_fusion.4), channel_id=1, source_target_pairs={{0,24},{1,13},{2,14},{3,27},{4,8},{5,29},{6,30},{7,11},{8,4},{9,17... | collective-permute-start | bytes 319496 | tf_op jit(solution)/shard_map/ppermute | solution.py:207
  35.4 4.3 %collective-permute-start.22 = (f32[16,1792]{1,0:T(8,128)S(1)}, f32[16,1792]{1,0:T(8,128)S(1)}, u32[]{:S(2)}, u32[]{:S(2)}) collective-permute-start(f32[16,1792]{1,0:T(8,128)S(1)} %pad_maximum_fusion.3), channel_id=1, source_target_pairs={{0,24},{1,13},{2,14},{3,27},{4,8},{5,29},{6,30},{7,11},{8,4},{9,17... | collective-permute-start | bytes 344072 | tf_op jit(solution)/shard_map/ppermute | solution.py:207
  36.5 7.6 %collective-permute-start.15 = (f32[32,1664]{1,0:T(8,128)S(1)}, f32[32,1664]{1,0:T(8,128)S(1)}, u32[]{:S(2)}, u32[]{:S(2)}) collective-permute-start(f32[32,1664]{1,0:T(8,128)S(1)} %pad_maximum_fusion.2.mine), channel_id=1, source_target_pairs={{0,8},{8,0},{16,24},{24,16},{1,9},{9,1},{17,25},{25,17},{2,10},{10... | collective-permute-start | bytes 638984 | tf_op jit(solution)/shard_map/ppermute | solution.py:210
  39.8 3.5 %collective-permute-start.23 = (f32[32,1792]{1,0:T(8,128)S(1)}, f32[32,1792]{1,0:T(8,128)S(1)}, u32[]{:S(2)}, u32[]{:S(2)}) collective-permute-start(f32[32,1792]{1,0:T(8,128)S(1)} %pad_maximum_fusion.mine), channel_id=1, source_target_pairs={{0,8},{8,0},{16,24},{24,16},{1,9},{9,1},{17,25},{25,17},{2,10},{10... | collective-permute-start | bytes 688136 | tf_op jit(solution)/shard_map/ppermute | solution.py:210
  42.1 2.8 %collective-permute-start.7 = (f32[32,1664]{1,0:T(8,128)S(1)}, f32[32,1664]{1,0:T(8,128)S(1)}, u32[]{:S(2)}, u32[]{:S(2)}) collective-permute-start(f32[32,1664]{1,0:T(8,128)S(1)} %pad_maximum_fusion.1.mine), channel_id=1, source_target_pairs={{0,8},{8,0},{16,24},{24,16},{1,9},{9,1},{17,25},{25,17},{2,10},{10... | collective-permute-start | bytes 638984 | tf_op jit(solution)/shard_map/ppermute | solution.py:210
